TPU v7x, 32 devices: a whole 2x2x4 slice. The times are simulated.
32 devices in a mesh: region: 2 (over core), mx: 4 (over y, x), my: 4 (over z).
Axes of the slice: x: 2, y: 2, z: 4, core: 2. Of those that a mesh axis runs over, the one named last changes fastest.
Arguments:
- features_in: bfloat16 [2, 4, 4, 2, 16, 16, 16, 128], P('region', 'mx', 'my'), may hold values from -6 to 6
- conv_weight: bfloat16 [7, 128, 128], replicated, may hold values from -0.1875 to 0.1875
- conv_bias: float32 [128], replicated, may hold values from -3 to 3
- head_weight: bfloat16 [128, 128], replicated, may hold values from -0.5 to 0.5
- grad_out: bfloat16 [2, 4, 4, 2, 16, 16, 16, 128], P('region', 'mx', 'my'), may hold values from -6 to 6
- grad_head: bfloat16 [2, 4, 4, 256, 128], P('region', 'mx', 'my'), may hold values from -6 to 6
- block_count: int32 [2, 4, 4], P('region', 'mx', 'my'), may hold values from 1 to 2, as said below
- neighbours: int32 [2, 4, 4, 2, 6], P('region', 'mx', 'my'), may hold values from 0 to 2, as said below
Outputs:
- features_out: bfloat16 [2, 4, 4, 2, 16, 16, 16, 128], P('region', 'mx', 'my')
- head_out: bfloat16 [2, 4, 4, 256, 128], P('region', 'mx', 'my')
- grad_features: bfloat16 [2, 4, 4, 2, 16, 16, 16, 128], P('region', 'mx', 'my')
- grad_conv: float32 [7, 128, 128], replicated
- grad_bias: float32 [128], replicated
- grad_head_weight: float32 [128, 128], replicated
Inputs may be any that keep to these rules, and one draw needn't show every extreme that they name: A tile's occupied blocks stand in slots 0 to block_count - 1; at least one tile holds exactly 2. `neighbours`: each occupied block has a height; slots of a tile hold rising heights. The -x and +x entries name the slot of the occupied block at the same height in the tile at mx index -1 and +1, the -y and +y entries likewise along my, the -z and +z entries the slot of the occupied block at height - 1 and + 1 in the same tile; 2 where there is no such block, beyond the map's edge and for every entry of an empty slot. Neighbours are mutual: the opposite face of a named block names the block back.
All inputs are finite; a program needn't handle non-finite values.
Results may differ from a plain program's by a relative error of at most 0.0085.
Values may be sent and summed in bfloat16 or wider, within the bound.
No kernel may reach another device: no remote copies, remote signals or barrier semaphores. Data moves between devices by JAX's collectives and lax.ppermute only.
A program may use at most 192 MiB of HBM per device.

v0:
```python
import jax
import jax.numpy as jnp
from jax import lax
from jax.sharding import PartitionSpec as P

SHIFTS = ((0, 0, 0), (-1, 0, 0), (1, 0, 0), (0, -1, 0), (0, 1, 0), (0, 0, -1), (0, 0, 1))


def from_behind(x, axis, by):
    devices = lax.axis_size(axis)
    pairs = [(i, i + by) for i in range(devices) if 0 <= i + by < devices]
    return lax.ppermute(x, axis, pairs)


def extended_2(cells, sides, width):
    for axis, dim in sides:
        count = lax.axis_size(axis)
        ends = count - 1
        head = lax.slice_in_dim(cells, 0, width, axis=dim)
        tail = lax.slice_in_dim(cells, cells.shape[dim] - width, cells.shape[dim], axis=dim)
        cells = jnp.concatenate(
            [
                lax.ppermute(tail, axis, [(i, (i + 1) % count) for i in range(ends)]),
                cells,
                lax.ppermute(head, axis, [((i + 1) % count, i) for i in range(ends)]),
            ],
            axis=dim,
        )
    return cells


def select_rows(layers, slot_index):
    zero_row = jnp.zeros((1,) + layers.shape[1:], layers.dtype)
    return jnp.take(jnp.concatenate([layers, zero_row], axis=0), slot_index, axis=0)


def pad_block(blocks, side_faces, links):
    padded = jnp.pad(blocks, ((0, 0), (1, 1), (1, 1), (1, 1), (0, 0)))
    padded = padded.at[:, 0, 1:-1, 1:-1].set(select_rows(side_faces[0], links[:, 0]))
    padded = padded.at[:, -1, 1:-1, 1:-1].set(select_rows(side_faces[1], links[:, 1]))
    padded = padded.at[:, 1:-1, 0, 1:-1].set(select_rows(side_faces[2], links[:, 2]))
    padded = padded.at[:, 1:-1, -1, 1:-1].set(select_rows(side_faces[3], links[:, 3]))
    padded = padded.at[:, 1:-1, 1:-1, 0].set(select_rows(blocks[:, :, :, -1], links[:, 4]))
    padded = padded.at[:, 1:-1, 1:-1, -1].set(select_rows(blocks[:, :, :, 0], links[:, 5]))
    return padded


def outer_layers(extended):
    return (
        extended[:, 0, 1:-1],
        extended[:, -1, 1:-1],
        extended[:, 1:-1, 0],
        extended[:, 1:-1, -1],
    )


def window(padded, shift):
    edge = padded.shape[1] - 2
    return padded[
        :,
        1 + shift[0] : 1 + shift[0] + edge,
        1 + shift[1] : 1 + shift[1] + edge,
        1 + shift[2] : 1 + shift[2] + edge,
    ]


def stencil(padded, conv_weight, direction):
    edge = padded.shape[1] - 2
    channels = padded.shape[-1]
    pieces = []
    for offset_id in range(7):
        shift = tuple((direction * step for step in SHIFTS[offset_id]))
        pieces.append(window(padded, shift).reshape(-1, channels))
    stacked = jnp.concatenate(pieces, axis=1)
    if direction > 0:
        matrix = conv_weight.reshape(7 * channels, channels)
    else:
        matrix = jnp.transpose(conv_weight, (0, 2, 1)).reshape(7 * channels, channels)
    total = jnp.dot(stacked, matrix, preferred_element_type=jnp.float32)
    return (total.reshape(padded.shape[0], edge, edge, edge, channels), stacked)


def weight_terms(stacked, grad_pre):
    channels = grad_pre.shape[-1]
    rows = grad_pre.reshape(-1, channels)
    terms = lax.dot_general(
        stacked, rows, (((0,), (0,)), ((), ())), preferred_element_type=jnp.float32
    )
    return terms.reshape(7, channels, channels)


def layer_product(layer, matrix):
    channels = layer.shape[-1]
    product = jnp.dot(layer.reshape(-1, channels), matrix.T, preferred_element_type=jnp.float32)
    return product.reshape(layer.shape)


def send_along_x(terms, offset):
    return from_behind(terms.astype(jnp.bfloat16), "mx", offset).astype(terms.dtype)


def send_along_y(terms, offset):
    return from_behind(terms.astype(jnp.bfloat16), "my", offset).astype(terms.dtype)


def body(
    features_in, conv_weight, conv_bias, head_weight, grad_out, grad_head, block_count, neighbours
):
    blocks = features_in.reshape(features_in.shape[3:])
    links = neighbours.reshape(neighbours.shape[3:])
    total_blocks = block_count.reshape(())
    upstream_tile = grad_out.reshape(grad_out.shape[3:])
    head_grad = grad_head.reshape(grad_head.shape[3:])
    slots = blocks.shape[0]
    edge = blocks.shape[1]
    channels = blocks.shape[-1]
    occupied = (jnp.arange(slots) < total_blocks)[:, None, None, None, None]
    extended = extended_2(blocks, (("mx", 1), ("my", 2)), 1)
    padded = pad_block(blocks, outer_layers(extended), links)
    conv_sum, stacked = stencil(padded, conv_weight, 1)
    preact = conv_sum + conv_bias
    result = jnp.where(occupied, blocks.astype(jnp.float32) + jax.nn.silu(preact), 0.0).astype(
        jnp.bfloat16
    )
    scale = 1.0 / (edge * total_blocks).astype(jnp.float32)
    column_mean = jnp.sum(result.astype(jnp.float32), axis=(0, 3)) * scale
    column_bf = column_mean.reshape(-1, channels).astype(jnp.bfloat16)
    head_tile = jnp.dot(column_bf, head_weight, preferred_element_type=jnp.float32).astype(
        jnp.bfloat16
    )
    column_grad = jnp.dot(head_grad, head_weight.T, preferred_element_type=jnp.float32) * scale
    spread = column_grad.reshape(edge, edge, 1, channels)[None]
    grad_result = jnp.where(occupied, upstream_tile.astype(jnp.float32) + spread, 0.0)
    sigma = jax.nn.sigmoid(preact)
    grad_pre = jnp.where(
        occupied, grad_result * sigma * (1.0 + preact * (1.0 - sigma)), 0.0
    ).astype(jnp.bfloat16)
    conv_part = weight_terms(stacked, grad_pre)
    bias_part = jnp.sum(grad_pre.astype(jnp.float32), axis=(0, 1, 2, 3))
    head_part = lax.dot_general(
        column_bf, head_grad, (((0,), (0,)), ((), ())), preferred_element_type=jnp.float32
    )
    zero_layer = jnp.zeros((slots, edge, edge, channels), jnp.bfloat16)
    padded_grad = pad_block(grad_pre, (zero_layer, zero_layer, zero_layer, zero_layer), links)
    transposed = stencil(padded_grad, conv_weight, -1)[0]
    from_upper_x = send_along_x(layer_product(grad_pre[:, 0], conv_weight[1]), -1)
    from_lower_x = send_along_x(layer_product(grad_pre[:, -1], conv_weight[2]), 1)
    transposed = transposed.at[:, -1].add(select_rows(from_upper_x, links[:, 1]))
    transposed = transposed.at[:, 0].add(select_rows(from_lower_x, links[:, 0]))
    from_upper_y = send_along_y(layer_product(grad_pre[:, :, 0], conv_weight[3]), -1)
    from_lower_y = send_along_y(layer_product(grad_pre[:, :, -1], conv_weight[4]), 1)
    transposed = transposed.at[:, :, -1].add(select_rows(from_upper_y, links[:, 3]))
    transposed = transposed.at[:, :, 0].add(select_rows(from_lower_y, links[:, 2]))
    grad_local = jnp.where(occupied, grad_result + transposed, 0.0).astype(jnp.bfloat16)
    grad_conv, grad_bias, grad_head_weight = lax.psum(
        (conv_part, bias_part, head_part), ("region", "mx", "my")
    )
    return (
        result.reshape(features_in.shape),
        head_tile.reshape(grad_head.shape),
        grad_local.reshape(features_in.shape),
        grad_conv,
        grad_bias,
        grad_head_weight,
    )


def solution(mesh):
    return jax.shard_map(
        body,
        mesh=mesh,
        in_specs=(
            P("region", "mx", "my", None, None, None, None, None),
            P(),
            P(),
            P(),
            P("region", "mx", "my", None, None, None, None, None),
            P("region", "mx", "my", None, None),
            P("region", "mx", "my"),
            P("region", "mx", "my", None, None),
        ),
        out_specs=(
            P("region", "mx", "my", None, None, None, None, None),
            P("region", "mx", "my", None, None),
            P("region", "mx", "my", None, None, None, None, None),
            P(),
            P(),
            P(),
        ),
        check_vma=False,
    )
```

profile of v0, /device:TPU:0, one launch (start us, length us, event | category | flops | bytes accessed | tf_op | source)
XLA Modules:
  0.0 359.6 jit_solution(12039950453167308843)
XLA Ops:
  7.2 1.8 fusion.29
  9.1 5.5 %collective-permute-start = (bf16[2,1,16,16,128]{4,3,2,1,0:T(8,128)(2,1)}, bf16[2,1,16,16,128]{4,3,2,1,0:T(8,128)(2,1)}, u32[]{:S(2)}, u32[]{:S(2)}) collective-permute-start(bf16[2,1,16,16,128]{4,3,2,1,0:T(8,128)(2,1)} %get-tuple-element.229), channel_id=1, source_target_pairs={{0,4},{4,8},{8,12},{1,5},{5,9},{9,13},{2,6},{6,10},{10,14},{3,7},{... | collective-permute-start | bytes 393224 | tf_op jit(solution)/shard_map/ppermute | solution.py:23
  14.6 1.3 collective-permute-start.1
  17.1 2.0 fusion.28
  22.4 3.2 pad.80
  25.8 1.2 gather_fusion.6
  35.6 1.5 pad_maximum_fusion
  37.1 4.1 %collective-permute-start.2 = (bf16[2,18,1,16,128]{4,3,2,1,0:T(8,128)(2,1)}, bf16[2,18,1,16,128]{4,3,2,1,0:T(8,128)(2,1)}, u32[]{:S(2)}, u32[]{:S(2)}) collective-permute-start(bf16[2,18,1,16,128]{4,3,2,1,0:T(8,128)(2,1)} %get-tuple-element.223), channel_id=1, source_target_pairs={{0,1},{1,2},{2,3},{4,5},{5,6},{6,7},{8,9},{9,10},{10,11},{12,13},{... | collective-permute-start | bytes 442376 | tf_op jit(solution)/shard_map/ppermute | solution.py:23
  41.2 1.8 collective-permute-start.3
  43.0 1.7 select_bitcast_fusion.5
  44.7 1.8 scatter.40
  46.5 1.7 select_bitcast_fusion.4
  48.2 1.8 scatter.41
  54.3 1.7 select_bitcast_fusion.3
  56.0 1.9 scatter.44
  57.9 1.8 select_bitcast_fusion.2
  59.6 1.8 scatter.45
  61.5 7.5 %scatter.46 = bf16[2,18,18,18,128]{4,3,2,1,0:T(8,128)(2,1)} dynamic-update-slice(bf16[2,18,18,18,128]{4,3,2,1,0:T(8,128)(2,1)} %scatter.45, bf16[2,16,16,1,128]{4,3,2,1,0:T(2,128)(2,1)S(1)} %copy.21, s32[]{:T(128)} %constant.461.clone.1, s32[]{:T(128)} %constant.462.clone.1, s32[]{:T(128)} %constant.462.clone.1, s32[]{:T(128)} %constant.461.clone.1, s32[]{:T(128)} %constant.461.clone.1) | dynamic-update-slice | bytes 262148 | tf_op jit(solution)/shard_map/scatter | solution.py:43
  69.0 7.5 %scatter.49 = bf16[2,18,18,18,128]{4,3,2,1,0:T(8,128)(2,1)} dynamic-update-slice(bf16[2,18,18,18,128]{4,3,2,1,0:T(8,128)(2,1)} %scatter.46, bf16[2,16,16,1,128]{4,3,2,1,0:T(2,128)(2,1)S(1)} %copy.22, s32[]{:T(128)} %constant.461.clone.1, s32[]{:T(128)} %constant.462.clone.1, s32[]{:T(128)} %constant.462.clone.1, s32[]{:T(128)} %constant.463.clone.1, s32[]{:T(128)} %constant.461.clone.1) | dynamic-update-slice | bytes 262148 | tf_op jit(solution)/shard_map/scatter | solution.py:44
  76.5 13.6 %fusion.26 = (bf16[2,16,16,16,128]{4,3,2,1,0:T(8,128)(2,1)}, bf16[2,16,16,16,896]{4,3,2,1,0:T(8,128)(2,1)}, bf16[2,16,16,16,128]{4,3,2,1,0:T(8,128)(2,1)}, bf16[...) fusion(bf16[2,18,18,18,128]{4,3,2,1,0:T(8,128)(2,1)} %scatter.49), kind=kLoop, calls=%fused_computation.132 | loop fusion | bytes 31457280 | tf_op jit(solution)/shard_map/slice | solution.py:59
  90.1 2.5 constant_dynamic-update-slice_fusion.5
  92.6 2.5 constant_dynamic-update-slice_fusion.4
  95.2 2.4 constant_dynamic-update-slice_fusion.3
  97.6 2.6 constant_dynamic-update-slice_fusion.2
  100.2 2.0 constant_dynamic-update-slice_fusion.1
  102.2 2.5 constant_dynamic-update-slice_fusion
  104.8 11.5 %convert_reduce_fusion = (f32[128]{0:T(128)}, bf16[2,16,16,16,128]{4,3,2,1,0:T(8,128)(2,1)S(1)}, f32[16,16,128]{2,1,0:T(8,128)S(1)}, bf16[2,16,16,16,128]{4,3,2,1,0:T(8,128)(2,1)}) fusion(f32[128]{0:T(128)S(1)} %copy-done.34, f32[16,16,128]{2,1,0:T(8,128)S(1)} %bitcast.163, bf16[1,1,1,2,16,16,16,128]{7,6,5,4,3,2,1,0:T(8,128)(2,1)S(1)} %copy-done.15, ...), kind=kOutput, calls=%fused_computation.25 | convolution fusion | flops 1903132544 | bytes 23561218 | tf_op jit(solution)/shard_map/dot_general | solution.py:79
  116.3 3.2 pad.81
  124.9 1.8 scatter.50
  126.7 1.8 scatter.51
  128.5 1.8 scatter.54
  130.2 1.8 scatter.55
  132.0 7.5 %scatter.56 = bf16[2,18,18,18,128]{4,3,2,1,0:T(8,128)(2,1)} dynamic-update-slice(bf16[2,18,18,18,128]{4,3,2,1,0:T(8,128)(2,1)} %scatter.55, bf16[2,16,16,1,128]{4,3,2,1,0:T(2,128)(2,1)S(1)} %copy.23, s32[]{:T(128)} %constant.461.clone.1, s32[]{:T(128)} %constant.462.clone.1, s32[]{:T(128)} %constant.462.clone.1, s32[]{:T(128)} %constant.461.clone.1, s32[]{:T(128)} %constant.461.clone.1) | dynamic-update-slice | bytes 262148 | tf_op jit(solution)/shard_map/scatter | solution.py:43
  139.5 7.5 %scatter.59 = bf16[2,18,18,18,128]{4,3,2,1,0:T(8,128)(2,1)} dynamic-update-slice(bf16[2,18,18,18,128]{4,3,2,1,0:T(8,128)(2,1)} %scatter.56, bf16[2,16,16,1,128]{4,3,2,1,0:T(2,128)(2,1)S(1)} %copy.24, s32[]{:T(128)} %constant.461.clone.1, s32[]{:T(128)} %constant.462.clone.1, s32[]{:T(128)} %constant.462.clone.1, s32[]{:T(128)} %constant.463.clone.1, s32[]{:T(128)} %constant.461.clone.1) | dynamic-update-slice | bytes 262148 | tf_op jit(solution)/shard_map/scatter | solution.py:44
  147.0 2.8 slice_dynamic-update-slice_fusion.6
  150.1 1.4 slice_dynamic-update-slice_fusion.5
  151.5 1.4 slice_dynamic-update-slice_fusion.4
  152.9 1.4 slice_dynamic-update-slice_fusion.3
  154.3 1.4 slice_dynamic-update-slice_fusion.2
  155.7 1.4 slice_dynamic-update-slice_fusion.1
  158.1 1.3 collective-permute-start.4
  159.4 5.2 %collective-permute-start.5 = (bf16[2,16,16,128]{3,2,1,0:T(8,128)(2,1)S(1)}, bf16[2,16,16,128]{3,2,1,0:T(8,128)(2,1)S(1)}, u32[]{:S(2)}, u32[]{:S(2)}) collective-permute-start(bf16[2,16,16,128]{3,2,1,0:T(8,128)(2,1)S(1)} %convolution_convert_fusion.2), channel_id=1, source_target_pairs={{0,4},{4,8},{8,12},{1,5},{5,9},{9,13},{2,6},{6,10},{10,14},{3,7},{... | collective-permute-start | bytes 393224 | tf_op jit(solution)/shard_map/ppermute | solution.py:12
  164.6 1.3 collective-permute-start.6
  165.9 5.8 %collective-permute-start.7 = (bf16[2,16,16,128]{3,2,1,0:T(8,128)(2,1)}, bf16[2,16,16,128]{3,2,1,0:T(8,128)(2,1)}, u32[]{:S(2)}, u32[]{:S(2)}) collective-permute-start(bf16[2,16,16,128]{3,2,1,0:T(8,128)(2,1)} %convolution_convert_fusion), channel_id=1, source_target_pairs={{0,1},{1,2},{2,3},{4,5},{5,6},{6,7},{8,9},{9,10},{10,11},{12,13},{... | collective-permute-start | bytes 393224 | tf_op jit(solution)/shard_map/ppermute | solution.py:12
  171.7 1.6 constant_dynamic-update-slice_fusion.13
  173.3 1.6 constant_dynamic-update-slice_fusion.12
  174.9 1.5 constant_dynamic-update-slice_fusion.11
  176.4 1.5 constant_dynamic-update-slice_fusion.10
  177.9 1.5 constant_dynamic-update-slice_fusion.9
  179.5 1.5 constant_dynamic-update-slice_fusion.8
  181.0 1.6 constant_dynamic-update-slice_fusion.7
  182.6 19.7 %copy.26 = bf16[896,8192]{1,0:T(8,128)(2,1)} copy(bf16[896,8192]{0,1:T(8,128)(2,1)} %bitcast.60) | data formatting | bytes 29360128 | tf_op jit(solution)/shard_map/dot_general | solution.py:86
  202.3 11.3 %fusion.30 = f32[2,16,16,16,128]{4,3,2,1,0:T(8,128)} fusion(bf16[2,16,16,16,896]{4,3,2,1,0:T(8,128)(2,1)} %copy-done.3, bf16[896,128,1,1,1]{1,0,4,3,2:T(8,128)(2,1)S(1)} %bitcast.159), kind=kOutput, calls=%fused_computation.136 | convolution fusion | flops 1879048192 | bytes 19103744 | tf_op jit(solution)/shard_map/dot_general | solution.py:79
  213.6 4.7 %fusion.31 = f32[7,128,128]{2,1,0:T(8,128)} fusion(bf16[7,128,8192]{2,1,0:T(8,128)(2,1)S(1)} %bitcast.146, bf16[8192,128,1]{1,0,2:T(8,128)(2,1)S(1)} %bitcast.158), kind=kOutput, calls=%fused_computation.137 | convolution fusion | flops 1879048192 | bytes 17235968 | tf_op jit(solution)/shard_map/dot_general | solution.py:86
  219.2 40.3 %psum.22 = f32[128]{0:T(128)} all-reduce(f32[128]{0:T(128)S(1)} %copy-done.35), channel_id=1, replica_groups=mesh['region'=2,'mx'=4,'my'=4] {'region','mx','my'}, use_global_device_ids=true, to_apply=%region_3.6 | all-reduce | flops 128 | bytes 1024 | tf_op jit(solution)/shard_map/psum | solution.py:155
  263.1 1.3 gather_fusion.15
  264.4 1.8 fusion.13
  266.1 1.8 fusion.12
  267.9 1.8 fusion.11
  269.7 1.9 fusion.10
  271.6 4.5 %fusion.8 = bf16[1,1,1,2,16,16,16,128]{7,6,5,4,3,2,1,0:T(8,128)(2,1)} fusion(f32[2,16,16,16,128]{4,3,2,1,0:T(8,128)} %fusion.10, bf16[1,1,1,2,16,16,16,128]{7,6,5,4,3,2,1,0:T(8,128)(2,1)S(1)} %copy-done.16, f32[16,16,128]{2,1,0:T(8,128)} %bitcast.164, pred[2]{0:T(512)(128)(4,1)} %copy-done.33), kind=kLoop, calls=%fused_computation.29 | loop fusion | flops 6291456 | bytes 8519682 | tf_op jit(solution)/shard_map/reshape | solution.py:161
  276.1 73.2 %all-reduce.18.cloned.1.call-done = (f32[7,128,128]{2,1,0:T(8,128)}, f32[128,128]{1,0:T(8,128)}) async-done(((f32[7,128,128]{2,1,0:T(8,128)}, f32[128,128]{1,0:T(8,128)}), (f32[7,128,128]{2,1,0:T(8,128)}, f32[128,128]{1,0:T(8,128)})) %all-reduce.18.cloned.1.call-update) | async-done | bytes 524304 | tf_op jit(solution)/shard_map/psum | solution.py:155
  349.2 1.8 copy.80
  351.1 1.5 copy.81
  (151 shorter events, 27.7 us)
Async XLA Ops:
  7.2 14.2 %copy-start = (bf16[1,1,1,256,128]{4,3,2,1,0:T(8,128)(2,1)S(1)}, bf16[1,1,1,256,128]{4,3,2,1,0:T(8,128)(2,1)}, u32[]{:S(2)}) copy-start(bf16[1,1,1,256,128]{4,3,2,1,0:T(8,128)(2,1)} %param.49) | copy-start | bytes 196612
  7.2 15.2 %copy-start.5 = (bf16[1,1,1,2,16,16,16,128]{7,6,5,4,3,2,1,0:T(8,128)(2,1)S(1)}, bf16[1,1,1,2,16,16,16,128]{7,6,5,4,3,2,1,0:T(8,128)(2,1)}, u32[]{:S(2)}) copy-start(bf16[1,1,1,2,16,16,16,128]{7,6,5,4,3,2,1,0:T(8,128)(2,1)} %param.44) | copy-start | bytes 6291460
  7.2 342.1 %all-reduce.18.cloned.1.call-start = ((), (), s32[]{:S(2)}) async-start(), calls=%async_computation | async-start | bytes 1048576 | tf_op jit(solution)/shard_map/psum | solution.py:155
  9.1 22.2 %collective-permute-start = (bf16[2,1,16,16,128]{4,3,2,1,0:T(8,128)(2,1)}, bf16[2,1,16,16,128]{4,3,2,1,0:T(8,128)(2,1)}, u32[]{:S(2)}, u32[]{:S(2)}) collective-permute-start(bf16[2,1,16,16,128]{4,3,2,1,0:T(8,128)(2,1)} %get-tuple-element.229), channel_id=1, source_target_pairs={{0,4},{4,8},{8,12},{1,5},{5,9},{9,13},{2,6},{6,10},{10,14},{3,7},{... | collective-permute-start | bytes 393224 | tf_op jit(solution)/shard_map/ppermute | solution.py:23
  14.6 18.8 %collective-permute-start.1 = (bf16[2,1,16,16,128]{4,3,2,1,0:T(8,128)(2,1)}, bf16[2,1,16,16,128]{4,3,2,1,0:T(8,128)(2,1)}, u32[]{:S(2)}, u32[]{:S(2)}) collective-permute-start(bf16[2,1,16,16,128]{4,3,2,1,0:T(8,128)(2,1)} %get-tuple-element.228), channel_id=1, source_target_pairs={{4,0},{8,4},{12,8},{5,1},{9,5},{13,9},{6,2},{10,6},{14,10},{7,3},{... | collective-permute-start | bytes 393224 | tf_op jit(solution)/shard_map/ppermute | solution.py:25
  17.0 26.0 %copy-start.30 = (pred[2]{0:T(512)(128)(4,1)}, pred[2]{0:T(512)(128)(4,1)S(1)}, u32[]{:S(2)}) copy-start(pred[2]{0:T(512)(128)(4,1)S(1)} %get-tuple-element.245) | copy-start | bytes 10
  17.1 29.4 %copy-start.32 = (pred[2]{0:T(512)(128)(4,1)}, pred[2]{0:T(512)(128)(4,1)S(1)}, u32[]{:S(2)}) copy-start(pred[2]{0:T(512)(128)(4,1)S(1)} %get-tuple-element.244) | copy-start | bytes 10
  17.1 37.2 %copy-start.29 = (pred[2]{0:T(512)(128)(4,1)}, pred[2]{0:T(512)(128)(4,1)S(1)}, u32[]{:S(2)}) copy-start(pred[2]{0:T(512)(128)(4,1)S(1)} %get-tuple-element.243) | copy-start | bytes 10
  17.1 40.8 %copy-start.31 = (pred[2]{0:T(512)(128)(4,1)}, pred[2]{0:T(512)(128)(4,1)S(1)}, u32[]{:S(2)}) copy-start(pred[2]{0:T(512)(128)(4,1)S(1)} %get-tuple-element.242) | copy-start | bytes 10
  19.2 6.5 %copy-start.25 = (pred[2]{0:T(512)(128)(4,1)}, pred[2]{0:T(512)(128)(4,1)S(1)}, u32[]{:S(2)}) copy-start(pred[2]{0:T(512)(128)(4,1)S(1)} %get-tuple-element.240) | copy-start | bytes 10
  19.2 6.5 %copy-start.27 = (pred[2]{0:T(512)(128)(4,1)}, pred[2]{0:T(512)(128)(4,1)S(1)}, u32[]{:S(2)}) copy-start(pred[2]{0:T(512)(128)(4,1)S(1)} %get-tuple-element.241) | copy-start | bytes 10
  19.9 1.4 copy-start.23
  20.0 10.6 %copy-start.24 = (s32[1024]{0:T(1024)}, s32[1024]{0:T(1024)S(1)}, u32[]{:S(2)}) copy-start(s32[1024]{0:T(1024)S(1)} %pad_clamp_fusion) | copy-start | bytes 12292
  21.4 9.6 %copy-start.17 = (bf16[7,128,128]{2,1,0:T(8,128)(2,1)S(1)}, bf16[7,128,128]{2,1,0:T(8,128)(2,1)}, u32[]{:S(2)}) copy-start(bf16[7,128,128]{2,1,0:T(8,128)(2,1)} %param.45) | copy-start | bytes 688132
  22.4 82.3 %copy-start.18 = (f32[256,128]{1,0:T(8,128)}, f32[256,128]{1,0:T(8,128)S(1)}, u32[]{:S(2)}) copy-start(f32[256,128]{1,0:T(8,128)S(1)} %convolution_multiply_fusion) | copy-start | bytes 393220
  31.3 73.5 %copy-start.33 = (pred[2]{0:T(512)(128)(4,1)}, pred[2]{0:T(512)(128)(4,1)S(1)}, u32[]{:S(2)}) copy-start(pred[2]{0:T(512)(128)(4,1)S(1)} %iota_compare_fusion) | copy-start | bytes 10
  37.1 12.9 %collective-permute-start.2 = (bf16[2,18,1,16,128]{4,3,2,1,0:T(8,128)(2,1)}, bf16[2,18,1,16,128]{4,3,2,1,0:T(8,128)(2,1)}, u32[]{:S(2)}, u32[]{:S(2)}) collective-permute-start(bf16[2,18,1,16,128]{4,3,2,1,0:T(8,128)(2,1)} %get-tuple-element.223), channel_id=1, source_target_pairs={{0,1},{1,2},{2,3},{4,5},{5,6},{6,7},{8,9},{9,10},{10,11},{12,13},{... | collective-permute-start | bytes 442376 | tf_op jit(solution)/shard_map/ppermute | solution.py:23
  41.2 10.9 %collective-permute-start.3 = (bf16[2,18,1,16,128]{4,3,2,1,0:T(8,128)(2,1)}, bf16[2,18,1,16,128]{4,3,2,1,0:T(8,128)(2,1)}, u32[]{:S(2)}, u32[]{:S(2)}) collective-permute-start(bf16[2,18,1,16,128]{4,3,2,1,0:T(8,128)(2,1)} %get-tuple-element.222), channel_id=1, source_target_pairs={{1,0},{2,1},{3,2},{5,4},{6,5},{7,6},{9,8},{10,9},{11,10},{13,12},{... | collective-permute-start | bytes 442376 | tf_op jit(solution)/shard_map/ppermute | solution.py:25
  76.5 13.7 %copy-start.1 = (bf16[2,18,18,18,128]{4,3,2,1,0:T(8,128)(2,1)S(1)}, bf16[2,18,18,18,128]{4,3,2,1,0:T(8,128)(2,1)}, u32[]{:S(2)}) copy-start(bf16[2,18,18,18,128]{4,3,2,1,0:T(8,128)(2,1)} %scatter.49) | copy-start | bytes 8957956
  100.2 4.6 %copy-start.15 = (bf16[1,1,1,2,16,16,16,128]{7,6,5,4,3,2,1,0:T(8,128)(2,1)S(1)}, bf16[1,1,1,2,16,16,16,128]{7,6,5,4,3,2,1,0:T(8,128)(2,1)}, u32[]{:S(2)}) copy-start(bf16[1,1,1,2,16,16,16,128]{7,6,5,4,3,2,1,0:T(8,128)(2,1)} %param.48) | copy-start | bytes 6291460
  100.2 4.6 %copy-start.34 = (f32[128]{0:T(128)S(1)}, f32[128]{0:T(128)}, u32[]{:S(2)}) copy-start(f32[128]{0:T(128)} %param.46) | copy-start | bytes 1540
  116.3 5.7 %copy-start.13 = (bf16[2,16,16,16,128]{4,3,2,1,0:T(8,128)(2,1)}, bf16[2,16,16,16,128]{4,3,2,1,0:T(8,128)(2,1)S(1)}, u32[]{:S(2)}) copy-start(bf16[2,16,16,16,128]{4,3,2,1,0:T(8,128)(2,1)S(1)} %get-tuple-element.209) | copy-start | bytes 6291460
  116.3 5.7 %copy-start.22 = (bf16[128,128]{1,0:T(8,128)(2,1)S(1)}, bf16[128,128]{1,0:T(8,128)(2,1)}, u32[]{:S(2)}) copy-start(bf16[128,128]{1,0:T(8,128)(2,1)} %param.47) | copy-start | bytes 98308
  116.3 7.2 %copy-start.28 = (pred[2]{0:T(512)(128)(4,1)S(1)}, pred[2]{0:T(512)(128)(4,1)}, u32[]{:S(2)}) copy-start(pred[2]{0:T(512)(128)(4,1)} %copy-done.27) | copy-start | bytes 10
  116.3 8.3 %copy-start.26 = (pred[2]{0:T(512)(128)(4,1)S(1)}, pred[2]{0:T(512)(128)(4,1)}, u32[]{:S(2)}) copy-start(pred[2]{0:T(512)(128)(4,1)} %copy-done.25) | copy-start | bytes 10
  119.4 5.4 %copy-start.19 = (bf16[2,1,16,16,128]{4,3,2,1,0:T(8,128)(2,1)S(1)}, bf16[2,1,16,16,128]{4,3,2,1,0:T(8,128)(2,1)}, u32[]{:S(2)}) copy-start(bf16[2,1,16,16,128]{4,3,2,1,0:T(8,128)(2,1)} %get-tuple-element.236) | copy-start | bytes 393220
  119.5 7.2 %copy-start.20 = (bf16[2,1,16,16,128]{4,3,2,1,0:T(8,128)(2,1)S(1)}, bf16[2,1,16,16,128]{4,3,2,1,0:T(8,128)(2,1)}, u32[]{:S(2)}) copy-start(bf16[2,1,16,16,128]{4,3,2,1,0:T(8,128)(2,1)} %get-tuple-element.234) | copy-start | bytes 393220
  119.5 10.8 %copy-start.21 = (bf16[2,16,1,16,128]{4,3,2,1,0:T(8,128)(2,1)S(1)}, bf16[2,16,1,16,128]{4,3,2,1,0:T(8,128)(2,1)}, u32[]{:S(2)}) copy-start(bf16[2,16,1,16,128]{4,3,2,1,0:T(8,128)(2,1)} %get-tuple-element.230) | copy-start | bytes 393220
  147.0 3.1 copy-start.2
  155.7 16.0 %copy-start.12 = (bf16[2,16,16,16,128]{4,3,2,1,0:T(8,128)(2,1)S(1)}, bf16[2,16,16,16,128]{4,3,2,1,0:T(8,128)(2,1)}, u32[]{:S(2)}) copy-start(bf16[2,16,16,16,128]{4,3,2,1,0:T(8,128)(2,1)} %get-tuple-element.221) | copy-start | bytes 6291460
  157.2 16.2 %copy-start.11 = (bf16[2,16,16,16,128]{4,3,2,1,0:T(8,128)(2,1)S(1)}, bf16[2,16,16,16,128]{4,3,2,1,0:T(8,128)(2,1)}, u32[]{:S(2)}) copy-start(bf16[2,16,16,16,128]{4,3,2,1,0:T(8,128)(2,1)} %get-tuple-element.220) | copy-start | bytes 6291460
  158.1 22.9 %copy-start.3 = (bf16[2,16,16,16,896]{4,3,2,1,0:T(8,128)(2,1)}, bf16[2,16,16,16,896]{4,3,2,1,0:T(8,128)(2,1)S(1)}, u32[]{:S(2)}) copy-start(bf16[2,16,16,16,896]{4,3,2,1,0:T(8,128)(2,1)S(1)} %slice_dynamic-update-slice_fusion) | copy-start | bytes 44040196
  158.1 101.3 %collective-permute-start.4 = (bf16[2,16,16,128]{3,2,1,0:T(8,128)(2,1)S(1)}, bf16[2,16,16,128]{3,2,1,0:T(8,128)(2,1)S(1)}, u32[]{:S(2)}, u32[]{:S(2)}) collective-permute-start(bf16[2,16,16,128]{3,2,1,0:T(8,128)(2,1)S(1)} %convolution_convert_fusion.3), channel_id=1, source_target_pairs={{4,0},{8,4},{12,8},{5,1},{9,5},{13,9},{6,2},{10,6},{14,10},{7,3},{... | collective-permute-start | bytes 393224 | tf_op jit(solution)/shard_map/ppermute | solution.py:12
  159.4 100.1 %collective-permute-start.5 = (bf16[2,16,16,128]{3,2,1,0:T(8,128)(2,1)S(1)}, bf16[2,16,16,128]{3,2,1,0:T(8,128)(2,1)S(1)}, u32[]{:S(2)}, u32[]{:S(2)}) collective-permute-start(bf16[2,16,16,128]{3,2,1,0:T(8,128)(2,1)S(1)} %convolution_convert_fusion.2), channel_id=1, source_target_pairs={{0,4},{4,8},{8,12},{1,5},{5,9},{9,13},{2,6},{6,10},{10,14},{3,7},{... | collective-permute-start | bytes 393224 | tf_op jit(solution)/shard_map/ppermute | solution.py:12
  164.6 96.1 %collective-permute-start.6 = (bf16[2,16,16,128]{3,2,1,0:T(8,128)(2,1)}, bf16[2,16,16,128]{3,2,1,0:T(8,128)(2,1)}, u32[]{:S(2)}, u32[]{:S(2)}) collective-permute-start(bf16[2,16,16,128]{3,2,1,0:T(8,128)(2,1)} %convolution_convert_fusion.1), channel_id=1, source_target_pairs={{1,0},{2,1},{3,2},{5,4},{6,5},{7,6},{9,8},{10,9},{11,10},{13,12},{... | collective-permute-start | bytes 393224 | tf_op jit(solution)/shard_map/ppermute | solution.py:12
  165.9 96.3 %collective-permute-start.7 = (bf16[2,16,16,128]{3,2,1,0:T(8,128)(2,1)}, bf16[2,16,16,128]{3,2,1,0:T(8,128)(2,1)}, u32[]{:S(2)}, u32[]{:S(2)}) collective-permute-start(bf16[2,16,16,128]{3,2,1,0:T(8,128)(2,1)} %convolution_convert_fusion), channel_id=1, source_target_pairs={{0,1},{1,2},{2,3},{4,5},{5,6},{6,7},{8,9},{9,10},{10,11},{12,13},{... | collective-permute-start | bytes 393224 | tf_op jit(solution)/shard_map/ppermute | solution.py:12
  171.7 3.2 copy-start.10
  173.3 3.1 copy-start.9
  174.9 3.0 copy-start.8
  176.4 3.0 copy-start.7
  177.9 3.1 copy-start.6
  202.3 11.3 %copy-start.4 = (bf16[896,8192]{1,0:T(8,128)(2,1)S(1)}, bf16[896,8192]{1,0:T(8,128)(2,1)}, u32[]{:S(2)}) copy-start(bf16[896,8192]{1,0:T(8,128)(2,1)} %copy.26) | copy-start | bytes 44040196
  202.3 11.3 %copy-start.14 = (bf16[2,16,16,16,128]{4,3,2,1,0:T(8,128)(2,1)S(1)}, bf16[2,16,16,16,128]{4,3,2,1,0:T(8,128)(2,1)}, u32[]{:S(2)}) copy-start(bf16[2,16,16,16,128]{4,3,2,1,0:T(8,128)(2,1)} %copy-done.13) | copy-start | bytes 6291460
  213.6 5.6 %copy-start.35 = (f32[128]{0:T(128)S(1)}, f32[128]{0:T(128)}, u32[]{:S(2)}) copy-start(f32[128]{0:T(128)} %get-tuple-element.208) | copy-start | bytes 1540
  218.3 53.3 %copy-start.16 = (bf16[1,1,1,2,16,16,16,128]{7,6,5,4,3,2,1,0:T(8,128)(2,1)S(1)}, bf16[1,1,1,2,16,16,16,128]{7,6,5,4,3,2,1,0:T(8,128)(2,1)}, u32[]{:S(2)}) copy-start(bf16[1,1,1,2,16,16,16,128]{7,6,5,4,3,2,1,0:T(8,128)(2,1)} %param.48) | copy-start | bytes 6291460
Sparse Core Ops, SparseCore 0:
  219.3 129.9 all-reduce.17
where the time goes:
time: 365 us; the launch traced here: 360 us
  local copies, waits for them, and re-layouts  150 us (41%)
  waiting for transfers between devices  73.2 us (20%)
  blocking collectives  40.3 us (11%)
  matrix products  32.1 us (9%)
  starting transfers between devices  26.4 us (7%)
  other arithmetic  22.4 us (6%)
  between operations  15.8 us (4%)
    psum x1, waiting for transfers between devices, body(): lax.psum((conv_part, bias_part, head_part), ('region', 'mx', 'my'))  73.2 us
    psum x1, blocking collectives, body(): lax.psum((conv_part, bias_part, head_part), ('region', 'mx', 'my'))  40.3 us
    unnamed x95, local copies, waits for them, and re-layouts  35.1 us
    dot_general x2, matrix products, stencil(): total = jnp.dot(stacked, matrix, preferred_element_type=jnp.float32)  22.8 us
    dot_general x1, local copies, waits for them, and re-layouts, weight_terms(): lax.dot_general(stacked, rows, (((0,), (0,)), ((), ())), preferred_elemen...  19.7 us
    gather x16, local copies, waits for them, and re-layouts, select_rows(): jnp.take(jnp.concatenate([layers, zero_row], axis=0), slot_index, axis=0)  15.2 us
    scatter x2, local copies, waits for them, and re-layouts, pad_block(): padded.at[:, 1:-1, 1:-1, 0]  15 us
    scatter x2, local copies, waits for them, and re-layouts, pad_block(): padded.at[:, 1:-1, 1:-1, -1]  15 us
  transfers between devices with their start and end apart: 9, of which 1 were waited for; matrix products, arithmetic and copies ran while one was open for 25% of the time, Pallas kernels for 0%

commit v1 on v0

v1 whole, which is shorter than its diff:
```python
import functools

import jax
import jax.numpy as jnp
from jax import lax
from jax.experimental import pallas as pl
from jax.experimental.pallas import tpu as pltpu
from jax.sharding import PartitionSpec as P

BF = jnp.bfloat16
F32 = jnp.float32
PLANES = 4


def halo_copies(meta, parity, slots, faces, vol, sems):
    edge = vol.shape[1] - 2
    found = []
    for s in range(slots):
        for f in range(4):
            link = meta[4 + s * 6 + f]
            axis, upper = f // 2, f % 2
            at = edge + 1 if upper else 0
            if axis == 0:
                target = vol.at[s, at, 1 : edge + 1]
            else:
                target = vol.at[s, 1 : edge + 1, at]
            source = jnp.minimum(link, slots - 1)
            copies = [
                pltpu.make_async_copy(faces[2 * axis + ph].at[source], target, sems.at[s * 4 + f])
                for ph in range(2)
            ]
            phase = (parity[axis] + upper + 1) % 2
            found.append((link < slots, phase, copies, (s, f, at)))
    return found


def start_halos(found, vol):
    edge = vol.shape[1] - 2
    for valid, phase, copies, (s, f, at) in found:
        for ph in range(2):
            @pl.when(valid & (phase == ph))
            def _(copy=copies[ph]):
                copy.start()

        @pl.when(jnp.logical_not(valid))
        def _():
            if f < 2:
                vol[s, at, 1 : edge + 1] = jnp.zeros((edge, edge, vol.shape[4]), vol.dtype)
            else:
                vol[s, 1 : edge + 1, at] = jnp.zeros((edge, edge, vol.shape[4]), vol.dtype)


def wait_halos(found):
    for valid, _, copies, _ in found:
        @pl.when(valid)
        def _(copy=copies[0]):
            copy.wait()


def windows(meta, vol, zbuf, s, x0, slots, direction):
    edge = vol.shape[1] - 2
    channels = vol.shape[4]
    rows = PLANES * edge * edge

    def at(dx, dy):
        return vol[s, pl.ds(x0 + 1 + dx, PLANES), 1 + dy : 1 + dy + edge]

    centre = at(0, 0)

    def beyond(face, part):
        link = meta[4 + s * 6 + face]
        other = vol[jnp.minimum(link, slots - 1), pl.ds(x0 + 1, PLANES), 1 : 1 + edge]
        other = other.astype(F32).reshape(PLANES * edge, edge, channels)[:, part]
        return jnp.where(link < slots, other, 0.0)

    zbuf[:, 0:8] = beyond(4, slice(edge - 8, edge))
    zbuf[:, 8 : 8 + edge] = centre.astype(F32).reshape(PLANES * edge, edge, channels)
    zbuf[:, 8 + edge : 16 + edge] = beyond(5, slice(0, 8))
    below = zbuf[:, 7 : 7 + edge].astype(BF)
    above = zbuf[:, 9 : 9 + edge].astype(BF)
    d = direction
    pieces = [centre, at(-d, 0), at(d, 0), at(0, -d), at(0, d)]
    pieces += [below, above] if d > 0 else [above, below]
    return jnp.concatenate([piece.reshape(rows, channels) for piece in pieces], axis=1)


def forward_kernel(
    meta, feat, x0f, x1f, y0f, y1f, w, bias, hw, gout, ghead,
    res_o, head_o, gpre_o, gx_o, gy_o, colg_o, pay_o,
    vol, zbuf, colsum, sems,
):
    slots, edge, channels = feat.shape[0], feat.shape[1], feat.shape[4]
    s, xi = pl.program_id(0), pl.program_id(1)
    steps = edge // PLANES
    count = meta[0]
    scale = 1.0 / (edge * count).astype(F32)
    taps = w.shape[0] // channels

    @pl.when((s == 0) & (xi == 0))
    def _():
        body = [
            pltpu.make_async_copy(
                feat.at[i], vol.at[i, 1 : edge + 1, 1 : edge + 1], sems.at[slots * 4 + i]
            )
            for i in range(slots)
        ]
        found = halo_copies(meta, (meta[1], meta[2]), slots, (x0f, x1f, y0f, y1f), vol, sems)
        for copy in body:
            copy.start()
        start_halos(found, vol)
        colg_o[...] = (
            lax.dot_general(
                ghead[...], hw[...], (((1,), (1,)), ((), ())), preferred_element_type=F32
            )
            * scale
        )
        pay_o[...] = jnp.zeros_like(pay_o)
        colsum[...] = jnp.zeros_like(colsum)
        for copy in body:
            copy.wait()
        wait_halos(found)

    x0 = xi * PLANES
    rows = PLANES * edge * edge
    cols = PLANES * edge
    stacked = windows(meta, vol, zbuf, s, x0, slots, 1)
    preact = jnp.dot(stacked, w[...], preferred_element_type=F32) + bias[...]
    occupied = s < count
    sigma = 0.5 * jnp.tanh(0.5 * preact) + 0.5
    silu = preact * sigma
    result = jnp.where(occupied, stacked[:, :channels].astype(F32) + silu, 0.0).astype(BF)
    res_o[0] = result.reshape(PLANES, edge, edge, channels)
    column = pl.ds(pl.multiple_of(x0 * edge, cols), cols)
    spread = colg_o[column].reshape(cols, 1, channels)
    grad_result = gout[0].astype(F32).reshape(cols, edge, channels) + spread
    slope = sigma * (1.0 + (preact - silu))
    gpre = jnp.where(occupied, grad_result.reshape(rows, channels) * slope, 0.0).astype(BF)
    gtile = gpre.reshape(PLANES, edge, edge, channels)
    gpre_o[0] = gtile

    @pl.when(xi == 0)
    def _():
        gx_o[0, s] = gtile[0]

    @pl.when(xi == steps - 1)
    def _():
        gx_o[1, s] = gtile[PLANES - 1]

    gy_o[0, s, pl.ds(x0, PLANES)] = gtile[:, 0]
    gy_o[1, s, pl.ds(x0, PLANES)] = gtile[:, edge - 1]

    of_row = lax.broadcasted_iota(jnp.int32, (cols, rows), 1) // edge
    pool = (of_row == lax.broadcasted_iota(jnp.int32, (cols, rows), 0)).astype(BF)
    colsum[column] += jnp.dot(pool, result, preferred_element_type=F32)
    pay_o[0 : taps * channels] += lax.dot_general(
        stacked, gpre, (((0,), (0,)), ((), ())), preferred_element_type=F32
    )
    ones = jnp.ones((16, rows), BF)
    tail = (taps + 1) * channels
    pay_o[tail : tail + 16] += jnp.dot(ones, gpre, preferred_element_type=F32)

    @pl.when((s == slots - 1) & (xi == steps - 1))
    def _():
        column_bf = (colsum[...] * scale).astype(BF)
        head_o[...] = jnp.dot(column_bf, hw[...], preferred_element_type=F32).astype(BF)
        pay_o[taps * channels : tail] = lax.dot_general(
            column_bf, ghead[...], (((0,), (0,)), ((), ())), preferred_element_type=F32
        )


def backward_kernel(meta, grad, x0f, x1f, y0f, y1f, wt, gout, colg, out_o, vol, zbuf, sems):
    slots, edge, channels = grad.shape[0], grad.shape[1], grad.shape[4]
    s, xi = pl.program_id(0), pl.program_id(1)

    @pl.when((s == 0) & (xi == 0))
    def _():
        body = [
            pltpu.make_async_copy(
                grad.at[i], vol.at[i, 1 : edge + 1, 1 : edge + 1], sems.at[slots * 4 + i]
            )
            for i in range(slots)
        ]
        found = halo_copies(meta, (meta[1], meta[2]), slots, (x0f, x1f, y0f, y1f), vol, sems)
        for copy in body:
            copy.start()
        start_halos(found, vol)
        for copy in body:
            copy.wait()
        wait_halos(found)

    x0 = xi * PLANES
    rows = PLANES * edge * edge
    cols = PLANES * edge
    stacked = windows(meta, vol, zbuf, s, x0, slots, -1)
    conv = jnp.dot(stacked, wt[...], preferred_element_type=F32)
    column = pl.ds(pl.multiple_of(x0 * edge, cols), cols)
    spread = colg[column].reshape(cols, 1, channels)
    grad_result = gout[0].astype(F32).reshape(cols, edge, channels) + spread
    total = jnp.where(s < meta[0], grad_result.reshape(rows, channels) + conv, 0.0).astype(BF)
    out_o[0] = total.reshape(PLANES, edge, edge, channels)


def swap(x, axis, odd):
    pairs = []
    for i in range(odd, lax.axis_size(axis) - 1, 2):
        pairs += [(i, i + 1), (i + 1, i)]
    return lax.ppermute(x, axis, pairs)


def swap_faces(low_high, axis):
    parity = lax.axis_index(axis) % 2
    arrived = []
    for odd in range(2):
        upward = parity == odd
        arrived.append(swap(jnp.where(upward, low_high[1], low_high[0]), axis, odd))
    return arrived


def partner(x, axis, bit):
    return lax.ppermute(x, axis, [(i, i ^ (1 << bit)) for i in range(lax.axis_size(axis))])


def own_bit(axis, bit):
    return (lax.axis_index(axis) >> bit) & 1


def halved(x, axis, bit):
    me = own_bit(axis, bit)
    parts = x.reshape((2, x.shape[0] // 2) + x.shape[1:])
    own = lax.dynamic_index_in_dim(parts, me, 0, False)
    sent = lax.dynamic_index_in_dim(parts, 1 - me, 0, False)
    return own + partner(sent.astype(BF), axis, bit).astype(F32)


def summed(x, axis, bit):
    return x + partner(x.astype(BF), axis, bit).astype(F32)


def doubled(x, axis, bit):
    other = partner(x, axis, bit)
    return jnp.where(
        own_bit(axis, bit) == 0, jnp.concatenate([x, other]), jnp.concatenate([other, x])
    )


def bits(axis):
    return range((lax.axis_size(axis) - 1).bit_length())


def all_summed(x):
    split = [("region", b) for b in bits("region")] + [("my", 0)]
    rest = [("my", b) for b in bits("my")][1:] + [("mx", b) for b in bits("mx")]
    for axis, bit in split:
        x = halved(x, axis, bit)
    for axis, bit in rest:
        x = summed(x, axis, bit)
    x = x.astype(BF)
    for axis, bit in reversed(split):
        x = doubled(x, axis, bit)
    return x.astype(F32)


def body(
    features_in, conv_weight, conv_bias, head_weight, grad_out, grad_head, block_count, neighbours
):
    blocks = features_in.reshape(features_in.shape[3:])
    upstream = grad_out.reshape(grad_out.shape[3:])
    head_grad = grad_head.reshape(grad_head.shape[3:])
    slots, edge, channels = blocks.shape[0], blocks.shape[1], blocks.shape[4]
    taps = conv_weight.shape[0]
    steps = edge // PLANES
    meta = jnp.concatenate(
        [
            block_count.reshape(1),
            (lax.axis_index("mx") % 2).astype(jnp.int32).reshape(1),
            (lax.axis_index("my") % 2).astype(jnp.int32).reshape(1),
            jnp.zeros((1,), jnp.int32),
            neighbours.reshape(-1),
        ]
    )
    faces = swap_faces((blocks[:, 0], blocks[:, -1]), "mx")
    faces += swap_faces((blocks[:, :, 0], blocks[:, :, -1]), "my")

    whole = lambda *shape: pl.BlockSpec(shape, lambda i, j, m: (0,) * len(shape))
    tile = pl.BlockSpec(
        (1, PLANES, edge, edge, channels), lambda i, j, m: (i, j, 0, 0, 0)
    )
    anywhere = pl.BlockSpec(memory_space=pl.ANY)
    volume = (slots, edge, edge, edge, channels)
    padded = pltpu.VMEM((slots, edge + 2, edge + 2, edge, channels), BF)
    zscratch = pltpu.VMEM((PLANES * edge, edge + 16, channels), F32)
    columns = edge * edge
    pay_rows = ((taps + 1) * channels // 64 + 1) * 64
    flops = 2 * slots * edge**3 * taps * channels * channels
    moved = slots * edge**3 * channels * 2
    params = pltpu.CompilerParams(
        dimension_semantics=("arbitrary", "arbitrary"), vmem_limit_bytes=48 << 20
    )
    result, head_tile, gpre, gx, gy, colg, pay = pl.pallas_call(
        forward_kernel,
        grid_spec=pltpu.PrefetchScalarGridSpec(
            num_scalar_prefetch=1,
            grid=(slots, steps),
            in_specs=[
                anywhere, anywhere, anywhere, anywhere, anywhere,
                whole(taps * channels, channels), whole(1, channels), whole(channels, channels),
                tile, whole(columns, channels),
            ],
            out_specs=[
                tile, whole(columns, channels), tile,
                whole(2, slots, edge, edge, channels), whole(2, slots, edge, edge, channels),
                whole(columns, channels), whole(pay_rows, channels),
            ],
            scratch_shapes=[
                padded, zscratch, pltpu.VMEM((columns, channels), F32),
                pltpu.SemaphoreType.DMA((slots * 5,)),
            ],
        ),
        out_shape=[
            jax.ShapeDtypeStruct(volume, BF),
            jax.ShapeDtypeStruct((columns, channels), BF),
            jax.ShapeDtypeStruct(volume, BF),
            jax.ShapeDtypeStruct((2, slots, edge, edge, channels), BF),
            jax.ShapeDtypeStruct((2, slots, edge, edge, channels), BF),
            jax.ShapeDtypeStruct((columns, channels), F32),
            jax.ShapeDtypeStruct((pay_rows, channels), F32),
        ],
        compiler_params=params,
        cost_estimate=pl.CostEstimate(
            flops=2 * flops, bytes_accessed=5 * moved, transcendentals=moved // 2
        ),
        name="forward",
    )(
        meta, blocks, *faces, conv_weight.reshape(taps * channels, channels),
        conv_bias.reshape(1, channels), head_weight, upstream, head_grad,
    )

    grad_faces = swap_faces(gx, "mx") + swap_faces(gy, "my")
    turned = jnp.transpose(conv_weight, (0, 2, 1)).reshape(taps * channels, channels)
    grad_local = pl.pallas_call(
        backward_kernel,
        grid_spec=pltpu.PrefetchScalarGridSpec(
            num_scalar_prefetch=1,
            grid=(slots, steps),
            in_specs=[
                anywhere, anywhere, anywhere, anywhere, anywhere,
                whole(taps * channels, channels), tile, whole(columns, channels),
            ],
            out_specs=tile,
            scratch_shapes=[padded, zscratch, pltpu.SemaphoreType.DMA((slots * 5,))],
        ),
        out_shape=jax.ShapeDtypeStruct(volume, BF),
        compiler_params=params,
        cost_estimate=pl.CostEstimate(
            flops=flops, bytes_accessed=4 * moved, transcendentals=0
        ),
        name="backward",
    )(meta, gpre, *grad_faces, turned, upstream, colg)

    total = all_summed(pay)
    conv_rows = taps * channels
    return (
        result.reshape(features_in.shape),
        head_tile.reshape(grad_head.shape),
        grad_local.reshape(features_in.shape),
        total[:conv_rows].reshape(taps, channels, channels),
        total[conv_rows + channels],
        total[conv_rows : conv_rows + channels],
    )


def solution(mesh):
    tiles = P("region", "mx", "my", None, None, None, None, None)
    rows = P("region", "mx", "my", None, None)
    return jax.shard_map(
        body,
        mesh=mesh,
        in_specs=(tiles, P(), P(), P(), tiles, rows, P("region", "mx", "my"), rows),
        out_specs=(tiles, rows, tiles, P(), P(), P()),
        check_vma=False,
    )
```

time: 365 us -> 88 us (0.24); the launches traced: 360 us -> 87.6 us
  local copies, waits for them, and re-layouts: 150 us -> 8.86 us
  waiting for transfers between devices: 73.2 us -> 16.1 us
  blocking collectives: 40.3 us -> 0 us
  matrix products: 32.1 us -> 0 us
  Pallas kernels: 0 us -> 28.9 us
  other arithmetic: 22.4 us -> 6.59 us
  between operations: 15.8 us -> 1.58 us
    psum x1 -> x0, waiting for transfers between devices: 73.2 us -> none  [body(): lax.psum((conv_part, bias_part, head_part), ('region', 'mx', 'my'))]
    scatter x12 -> x0, local copies, waits for them, and re-layouts: 44.4 us -> none  [the longest x2 15 us: pad_block(): padded.at[:, 1:-1, 1:-1, 0]]
    psum x1 -> x0, blocking collectives: 40.3 us -> none  [body(): lax.psum((conv_part, bias_part, head_part), ('region', 'mx', 'my'))]
    dot_general x10 -> x0, matrix products: 32.1 us -> none  [the longest x2 22.8 us: stencil(): total = jnp.dot(stacked, matrix, preferred_element_type=jnp.float32)]
    unnamed x95 -> x19, local copies, waits for them, and re-layouts: 35.1 us -> 5.87 us
    pallas_call x0 -> x2, Pallas kernels: none -> 28.9 us  [the longest x1 21.8 us: body(): pl.pallas_call(forward_kernel, grid_spec=pltpu.PrefetchScalarGridSpec(num...]
    dot_general x1 -> x0, local copies, waits for them, and re-layouts: 19.7 us -> none  [weight_terms(): lax.dot_general(stacked, rows, (((0,), (0,)), ((), ())), preferred_elemen...]
    slice x5 -> x2, local copies, waits for them, and re-layouts: 19 us -> 1.43 us  [the longest x1 0.8 us: body(): total[:conv_rows].reshape(taps, channels, channels)]
  transfers between devices with their start and end apart: 9 -> 15, of which waited for: 1 -> 6; matrix products, arithmetic and copies ran while one was open for 25% -> 4% of each run, Pallas kernels for 0% -> 8%
where the time goes in v1:
time: 88 us; the launch traced here: 87.6 us
  Pallas kernels  28.9 us (33%)
  starting transfers between devices  25.5 us (29%)
  waiting for transfers between devices  16.1 us (18%)
  local copies, waits for them, and re-layouts  8.86 us (10%)
  other arithmetic  6.59 us (7%)
  between operations  1.58 us (2%)
    pallas_call x1, Pallas kernels, body(): pl.pallas_call(forward_kernel, grid_spec=pltpu.PrefetchScalarGridSpec(num...  21.8 us
    ppermute x8, starting transfers between devices, swap(): return lax.ppermute(x, axis, pairs)  19.6 us
    ppermute x7, waiting for transfers between devices, partner(): lax.ppermute(x, axis, [(i, i ^ 1 << bit) for i in range(lax.axis_size(axi...  12.1 us
    pallas_call x1, Pallas kernels, body(): pl.pallas_call(backward_kernel, grid_spec=pltpu.PrefetchScalarGridSpec(nu...  7.15 us
    ppermute x7, starting transfers between devices, partner(): lax.ppermute(x, axis, [(i, i ^ 1 << bit) for i in range(lax.axis_size(axi...  5.9 us
    unnamed x19, local copies, waits for them, and re-layouts  5.87 us
    ppermute x8, waiting for transfers between devices, swap(): return lax.ppermute(x, axis, pairs)  4.02 us
    convert_element_type x3, other arithmetic, summed(): return x + partner(x.astype(BF), axis, bit).astype(F32)  2.81 us
  transfers between devices with their start and end apart: 15, of which 6 were waited for; matrix products, arithmetic and copies ran while one was open for 4% of the time, Pallas kernels for 8%

profile of v1, /device:TPU:0, one launch (start us, length us, event | category | flops | bytes accessed | tf_op | source)
XLA Modules:
  0.0 87.6 jit_solution(7500961063309755046)
XLA Ops:
  0.7 0.0 copy-start.8
  0.7 0.0 copy-start.3
  0.7 0.0 copy-start.4
  0.7 0.0 copy-start.5
  0.7 0.0 copy-start.6
  0.7 2.2 %copy.21 = bf16[1,1,1,2,16,16,16,128]{7,6,4,3,5,2,1,0:T(8,128)(2,1)S(1)} copy(bf16[1,1,1,2,16,16,16,128]{7,6,5,4,3,2,1,0:T(8,128)(2,1)} %param.8) | data formatting | bytes 4194304 | tf_op args[0]
  3.0 0.7 collective-permute-start.1
  3.7 5.8 %collective-permute-start = (bf16[2,16,16,128]{3,2,0,1:T(8,128)(2,1)S(1)}, bf16[2,16,16,128]{3,2,0,1:T(8,128)(2,1)S(1)}, u32[]{:S(2)}, u32[]{:S(2)}) collective-permute-start(bf16[2,16,16,128]{3,2,0,1:T(8,128)(2,1)S(1)} %get-tuple-element.23), channel_id=1, source_target_pairs={{0,4},{4,0},{8,12},{12,8},{1,5},{5,1},{9,13},{13,9},{2,6},{6,2},{1... | collective-permute-start | bytes 393224 | tf_op jit(solution)/shard_map/ppermute | solution.py:207
  9.4 0.7 collective-permute-start.3
  10.1 4.5 %collective-permute-start.2 = (bf16[2,16,16,128]{3,2,1,0:T(8,128)(2,1)S(1)}, bf16[2,16,16,128]{3,2,1,0:T(8,128)(2,1)S(1)}, u32[]{:S(2)}, u32[]{:S(2)}) collective-permute-start(bf16[2,16,16,128]{3,2,1,0:T(8,128)(2,1)S(1)} %get-tuple-element.21), channel_id=1, source_target_pairs={{0,1},{1,0},{2,3},{3,2},{4,5},{5,4},{6,7},{7,6},{8,9},{9,8},{10,11... | collective-permute-start | bytes 393224 | tf_op jit(solution)/shard_map/ppermute | solution.py:207
  15.2 0.0 copy-done.8
  15.2 0.1 reshape.81
  15.3 0.1 concatenate.15.meta
  15.4 0.0 collective-permute-done.1
  15.4 0.0 collective-permute-done
  15.5 0.0 collective-permute-done.3.y1f
  15.5 2.1 %collective-permute-done.2.y0f = bf16[2,16,16,128]{3,2,1,0:T(8,128)(2,1)S(1)} collective-permute-done((bf16[2,16,16,128]{3,2,1,0:T(8,128)(2,1)S(1)}, bf16[2,16,16,128]{3,2,1,0:T(8,128)(2,1)S(1)}, u32[]{:S(2)}, u32[]{:S(2)}) %collective-permute-start.2) | collective-permute-done | bytes 131104 | tf_op jit(solution)/shard_map/ppermute | solution.py:207
  17.5 0.0 copy-done.3
  17.5 0.0 copy-done.4
  17.5 0.0 copy-done.5
  17.5 0.0 copy-done.6
  17.5 21.8 %forward.1 = (bf16[2,16,16,16,128]{4,3,2,1,0:T(8,128)(2,1)}, bf16[256,128]{1,0:T(8,128)(2,1)}, bf16[2,16,16,16,128]{4,3,2,1,0:T(8,128)(2,1)S(1)}, bf16[2,2,16,16...) custom-call(s32[16]{0:T(128)S(1)} %concatenate.15.meta, ...), custom_call_target="tpu_custom_call" | custom-call | flops 3758096384 | bytes 10485760 | tf_op jit(solution)/shard_map/forward/pallas_call | solution.py:299
  39.3 0.0 copy-start.1
  39.3 1.3 %copy-done.1 = bf16[2,16,16,16,128]{4,3,2,1,0:T(8,128)(2,1)} copy-done((bf16[2,16,16,16,128]{4,3,2,1,0:T(8,128)(2,1)}, bf16[2,16,16,16,128]{4,3,2,1,0:T(8,128)(2,1)S(1)}, u32[]{:S(2)}) %copy-start.1) | copy-done | bytes 2097176
  40.7 0.7 fusion.1
  41.3 0.0 collective-permute-start.8
  41.3 1.7 %collective-permute-done.8 = bf16[544,128]{1,0:T(8,128)(2,1)} collective-permute-done((bf16[544,128]{1,0:T(8,128)(2,1)}, bf16[544,128]{1,0:T(8,128)(2,1)}, u32[]{:S(2)}, u32[]{:S(2)}) %collective-permute-start.8) | collective-permute-done | bytes 139296 | tf_op jit(solution)/shard_map/ppermute | solution.py:220
  43.0 0.9 %bitcast_add_fusion = f32[544,128]{1,0:T(8,128)S(1)} fusion(bf16[544,128]{1,0:T(8,128)(2,1)} %collective-permute-done.8, f32[2,544,128]{2,1,0:T(8,128)S(1)} %bitcast.58, s32[]{:T(128)S(6)} %select_n.151), kind=kLoop, calls=%fused_computation.3 | loop fusion | flops 139264 | bytes 696324 | tf_op jit(solution)/shard_map/add | solution.py:232
  44.0 0.0 copy-start.7
  44.0 0.7 copy-done.7
  44.7 2.1 %collective-permute-start.9 = (bf16[272,128]{1,0:T(8,128)(2,1)S(1)}, bf16[272,128]{1,0:T(8,128)(2,1)S(1)}, u32[]{:S(2)}, u32[]{:S(2)}) collective-permute-start(bf16[272,128]{1,0:T(8,128)(2,1)S(1)} %fusion.3), channel_id=1, source_target_pairs={{0,1},{1,0},{2,3},{3,2},{4,5},{5,4},{6,7},{7,6},{8,9},{9,8},{10,11... | collective-permute-start | bytes 208904 | tf_op jit(solution)/shard_map/ppermute | solution.py:220
  46.8 2.5 %collective-permute-done.9 = bf16[272,128]{1,0:T(8,128)(2,1)S(1)} collective-permute-done((bf16[272,128]{1,0:T(8,128)(2,1)S(1)}, bf16[272,128]{1,0:T(8,128)(2,1)S(1)}, u32[]{:S(2)}, u32[]{:S(2)}) %collective-permute-start.9) | collective-permute-done | bytes 69664 | tf_op jit(solution)/shard_map/ppermute | solution.py:220
  49.3 0.9 %fusion.5 = bf16[272,128]{1,0:T(8,128)(2,1)S(1)} fusion(bf16[272,128]{1,0:T(8,128)(2,1)S(1)} %collective-permute-done.9, f32[2,272,128]{2,1,0:T(8,128)} %bitcast.66, s32[]{:T(128)S(6)} %select_n.153), kind=kLoop, calls=%fused_computation.24 | loop fusion | flops 104448 | bytes 278532 | tf_op jit(solution)/shard_map/convert_element_type | solution.py:236
  50.2 1.8 %collective-permute-start.10 = (bf16[272,128]{1,0:T(8,128)(2,1)S(1)}, bf16[272,128]{1,0:T(8,128)(2,1)S(1)}, u32[]{:S(2)}, u32[]{:S(2)}) collective-permute-start(bf16[272,128]{1,0:T(8,128)(2,1)S(1)} %fusion.5), channel_id=1, source_target_pairs={{0,2},{1,3},{2,0},{3,1},{4,6},{5,7},{6,4},{7,5},{8,10},{9,11},{10,... | collective-permute-start | bytes 208904 | tf_op jit(solution)/shard_map/ppermute | solution.py:220
  52.0 3.6 %collective-permute-done.10 = bf16[272,128]{1,0:T(8,128)(2,1)S(1)} collective-permute-done((bf16[272,128]{1,0:T(8,128)(2,1)S(1)}, bf16[272,128]{1,0:T(8,128)(2,1)S(1)}, u32[]{:S(2)}, u32[]{:S(2)}) %collective-permute-start.10) | collective-permute-done | bytes 69664 | tf_op jit(solution)/shard_map/ppermute | solution.py:220
  55.6 0.9 %fusion.2 = bf16[272,128]{1,0:T(8,128)(2,1)S(1)} fusion(bf16[272,128]{1,0:T(8,128)(2,1)S(1)} %collective-permute-done.10, bf16[272,128]{1,0:T(8,128)(2,1)S(1)} %collective-permute-done.9, f32[2,272,128]{2,1,0:T(8,128)} %bitcast.67, s32[]{:T(128)S(6)} %select_n.153), kind=kLoop, calls=%fused_computation.20 | loop fusion | flops 174080 | bytes 348164 | tf_op jit(solution)/shard_map/convert_element_type | solution.py:236
  56.5 0.1 collective-permute-start.11
  56.6 4.3 %collective-permute-done.11 = bf16[272,128]{1,0:T(8,128)(2,1)S(1)} collective-permute-done((bf16[272,128]{1,0:T(8,128)(2,1)S(1)}, bf16[272,128]{1,0:T(8,128)(2,1)S(1)}, u32[]{:S(2)}, u32[]{:S(2)}) %collective-permute-start.11) | collective-permute-done | bytes 69664 | tf_op jit(solution)/shard_map/ppermute | solution.py:220
  60.9 0.9 %fusion.4 = bf16[272,128]{1,0:T(8,128)(2,1)S(1)} fusion(bf16[272,128]{1,0:T(8,128)(2,1)S(1)} %collective-permute-done.11, bf16[272,128]{1,0:T(8,128)(2,1)S(1)} %collective-permute-done.10, bf16[272,128]{1,0:T(8,128)(2,1)S(1)} %collective-permute-done.9, f32[2,272,128]{2,1,0:T(8,128)} %bitcast.68, s32[]{:T(128)S(6)} %select_n.153), kind=kLoop, calls=%fused_computation.22 | loop fusion | flops 243712 | bytes 417796 | tf_op jit(solution)/shard_map/convert_element_type | solution.py:236
  61.8 0.1 collective-permute-start.12
  61.9 0.7 collective-permute-start.5
  62.6 4.8 %collective-permute-start.4 = (bf16[2,16,16,128]{3,2,1,0:T(8,128)(2,1)S(1)}, bf16[2,16,16,128]{3,2,1,0:T(8,128)(2,1)S(1)}, u32[]{:S(2)}, u32[]{:S(2)}) collective-permute-start(bf16[2,16,16,128]{3,2,1,0:T(8,128)(2,1)S(1)} %get-tuple-element.27), channel_id=1, source_target_pairs={{0,4},{4,0},{8,12},{12,8},{1,5},{5,1},{9,13},{13,9},{2,6},{6,2},{1... | collective-permute-start | bytes 393224 | tf_op jit(solution)/shard_map/ppermute | solution.py:207
  67.4 0.0 collective-permute-done.12
  67.4 1.0 %add_convert_fusion = bf16[272,128]{1,0:T(8,128)(2,1)S(1)} fusion(bf16[272,128]{1,0:T(8,128)(2,1)S(1)} %collective-permute-done.12, bf16[272,128]{1,0:T(8,128)(2,1)S(1)} %collective-permute-done.11, bf16[272,128]{1,0:T(8,128)(2,1)S(1)} %collective-permute-done.10, bf16[272,128]{1,0:T(8,128)(2,1)S(1)} %collective-permute-done.9, f32[2,272,128]{2,1,0:T(8,128)} %bitcast.69, ...), kind=kLoop, calls=%fused_computation.8 | loop fusion | flops 313344 | bytes 487428 | tf_op jit(solution)/shard_map/convert_element_type | solution.py:257
  68.4 1.8 %collective-permute-start.13 = (bf16[272,128]{1,0:T(8,128)(2,1)S(1)}, bf16[272,128]{1,0:T(8,128)(2,1)}, u32[]{:S(2)}, u32[]{:S(2)}) collective-permute-start(bf16[272,128]{1,0:T(8,128)(2,1)S(1)} %add_convert_fusion), channel_id=1, source_target_pairs={{0,1},{1,0},{2,3},{3,2},{4,5},{5,4},{6,7},{7,6},{8,9},{9,8},{10,11... | collective-permute-start | bytes 208904 | tf_op jit(solution)/shard_map/ppermute | solution.py:220
  70.2 0.7 select_bitcast_fusion
  70.9 0.7 collective-permute-start.7
  71.5 2.0 %collective-permute-start.6 = (bf16[2,16,16,128]{3,2,1,0:T(8,128)(2,1)}, bf16[2,16,16,128]{3,2,1,0:T(8,128)(2,1)S(1)}, u32[]{:S(2)}, u32[]{:S(2)}) collective-permute-start(bf16[2,16,16,128]{3,2,1,0:T(8,128)(2,1)} %get-tuple-element.25), channel_id=1, source_target_pairs={{0,1},{1,0},{2,3},{3,2},{4,5},{5,4},{6,7},{7,6},{8,9},{9,8},{10,11... | collective-permute-start | bytes 393224 | tf_op jit(solution)/shard_map/ppermute | solution.py:207
  73.5 0.2 copy.18
  73.7 0.0 collective-permute-done.13
  73.7 1.0 %maximum_select_fusion.1 = bf16[544,128]{1,0:T(8,128)(2,1)S(1)} fusion(bf16[272,128]{1,0:T(8,128)(2,1)} %collective-permute-done.13, bf16[272,128]{1,0:T(8,128)(2,1)S(1)} %add_convert_fusion, pred[]{:T(512)S(6)} %eq.34), kind=kLoop, calls=%fused_computation.6 | loop fusion | flops 626688 | bytes 278529 | tf_op jit(solution)/shard_map/jit(_where)/select_n | solution.py:241
  74.7 0.1 collective-permute-start.14
  74.8 0.0 collective-permute-done.5.x1f
  74.8 0.0 collective-permute-done.4.x0f
  74.8 0.0 collective-permute-done.7.y1f
  74.8 1.9 %collective-permute-done.6.y0f = bf16[2,16,16,128]{3,2,1,0:T(8,128)(2,1)S(1)} collective-permute-done((bf16[2,16,16,128]{3,2,1,0:T(8,128)(2,1)}, bf16[2,16,16,128]{3,2,1,0:T(8,128)(2,1)S(1)}, u32[]{:S(2)}, u32[]{:S(2)}) %collective-permute-start.6) | collective-permute-done | bytes 131104 | tf_op jit(solution)/shard_map/ppermute | solution.py:207
  76.8 0.0 copy-done
  76.8 1.6 %copy-done.2 = bf16[2,16,16,16,128]{4,3,2,1,0:T(8,128)(2,1)S(1)} copy-done((bf16[2,16,16,16,128]{4,3,2,1,0:T(8,128)(2,1)S(1)}, bf16[2,16,16,16,128]{4,3,2,1,0:T(8,128)(2,1)}, u32[]{:S(2)}) %copy-start.2) | copy-done | bytes 2097176
  78.4 7.1 %backward.1 = bf16[2,16,16,16,128]{4,3,2,1,0:T(8,128)(2,1)} custom-call(s32[16]{0:T(128)S(1)} %concatenate.15.meta, bf16[2,16,16,16,128]{4,3,2,1,0:T(8,128)(2,1)S(1)} %copy-done.2, bf16[2,16,16,128]{3,2,1,0:T(8,128)(2,1)S(1)} %collective-permute-done.4.x0f, bf16[2,16,16,128]{3,2,1,0:T(8,128)(2,1)S(1)} %collective-permute-done.5.x1f, ...), custom_call_target="tpu_custom_call" | custom-call | flops 1879048192 | bytes 8388608 | tf_op jit(solution)/shard_map/backward/pallas_call | solution.py:340
  85.5 0.0 collective-permute-done.14
  85.6 0.1 fusion
  85.6 0.5 slice_bitcast_fusion
  86.1 0.6 slice.54
  86.8 0.8 slice.52
  (8 shorter events, 0.1 us)
Async XLA Ops:
  0.7 14.6 %copy-start.8 = (s32[1,1,1,2,6]{4,3,2,1,0:T(2,128)S(1)}, s32[1,1,1,2,6]{4,3,2,1,0:T(2,128)}, u32[]{:S(2)}) copy-start(s32[1,1,1,2,6]{4,3,2,1,0:T(2,128)} %param.15) | copy-start | bytes 148
  0.7 16.9 %copy-start.3 = (bf16[7,128,128]{2,1,0:T(8,128)(2,1)S(1)}, bf16[7,128,128]{2,1,0:T(8,128)(2,1)}, u32[]{:S(2)}) copy-start(bf16[7,128,128]{2,1,0:T(8,128)(2,1)} %param.9) | copy-start | bytes 688132
  0.7 16.9 %copy-start.4 = (bf16[1,1,1,256,128]{4,3,2,1,0:T(8,128)(2,1)S(1)}, bf16[1,1,1,256,128]{4,3,2,1,0:T(8,128)(2,1)}, u32[]{:S(2)}) copy-start(bf16[1,1,1,256,128]{4,3,2,1,0:T(8,128)(2,1)} %param.13) | copy-start | bytes 196612
  0.7 16.9 %copy-start.5 = (bf16[128,128]{1,0:T(8,128)(2,1)S(1)}, bf16[128,128]{1,0:T(8,128)(2,1)}, u32[]{:S(2)}) copy-start(bf16[128,128]{1,0:T(8,128)(2,1)} %hw.1) | copy-start | bytes 98308
  0.7 16.8 %copy-start.6 = (f32[128]{0:T(128)S(1)}, f32[128]{0:T(128)}, u32[]{:S(2)}) copy-start(f32[128]{0:T(128)} %param.10) | copy-start | bytes 1540
  3.0 12.4 %collective-permute-start.1 = (bf16[2,16,16,128]{3,2,0,1:T(8,128)(2,1)S(1)}, bf16[2,16,16,128]{3,2,0,1:T(8,128)(2,1)S(1)}, u32[]{:S(2)}, u32[]{:S(2)}) collective-permute-start(bf16[2,16,16,128]{3,2,0,1:T(8,128)(2,1)S(1)} %get-tuple-element.22), channel_id=1, source_target_pairs={{4,8},{8,4},{5,9},{9,5},{6,10},{10,6},{7,11},{11,7},{20,24},{24,20... | collective-permute-start | bytes 393224 | tf_op jit(solution)/shard_map/ppermute | solution.py:207
  3.7 11.8 %collective-permute-start = (bf16[2,16,16,128]{3,2,0,1:T(8,128)(2,1)S(1)}, bf16[2,16,16,128]{3,2,0,1:T(8,128)(2,1)S(1)}, u32[]{:S(2)}, u32[]{:S(2)}) collective-permute-start(bf16[2,16,16,128]{3,2,0,1:T(8,128)(2,1)S(1)} %get-tuple-element.23), channel_id=1, source_target_pairs={{0,4},{4,0},{8,12},{12,8},{1,5},{5,1},{9,13},{13,9},{2,6},{6,2},{1... | collective-permute-start | bytes 393224 | tf_op jit(solution)/shard_map/ppermute | solution.py:207
  9.4 6.0 %collective-permute-start.3 = (bf16[2,16,16,128]{3,2,1,0:T(8,128)(2,1)S(1)}, bf16[2,16,16,128]{3,2,1,0:T(8,128)(2,1)S(1)}, u32[]{:S(2)}, u32[]{:S(2)}) collective-permute-start(bf16[2,16,16,128]{3,2,1,0:T(8,128)(2,1)S(1)} %get-tuple-element.20), channel_id=1, source_target_pairs={{1,2},{2,1},{5,6},{6,5},{9,10},{10,9},{13,14},{14,13},{17,18},{18,... | collective-permute-start | bytes 393224 | tf_op jit(solution)/shard_map/ppermute | solution.py:207
  10.1 7.4 %collective-permute-start.2 = (bf16[2,16,16,128]{3,2,1,0:T(8,128)(2,1)S(1)}, bf16[2,16,16,128]{3,2,1,0:T(8,128)(2,1)S(1)}, u32[]{:S(2)}, u32[]{:S(2)}) collective-permute-start(bf16[2,16,16,128]{3,2,1,0:T(8,128)(2,1)S(1)} %get-tuple-element.21), channel_id=1, source_target_pairs={{0,1},{1,0},{2,3},{3,2},{4,5},{5,4},{6,7},{7,6},{8,9},{9,8},{10,11... | collective-permute-start | bytes 393224 | tf_op jit(solution)/shard_map/ppermute | solution.py:207
  39.3 1.3 %copy-start.1 = (bf16[2,16,16,16,128]{4,3,2,1,0:T(8,128)(2,1)}, bf16[2,16,16,16,128]{4,3,2,1,0:T(8,128)(2,1)S(1)}, u32[]{:S(2)}) copy-start(bf16[2,16,16,16,128]{4,3,2,1,0:T(8,128)(2,1)S(1)} %get-tuple-element.15.grad) | copy-start | bytes 6291460
  41.3 1.7 %collective-permute-start.8 = (bf16[544,128]{1,0:T(8,128)(2,1)}, bf16[544,128]{1,0:T(8,128)(2,1)}, u32[]{:S(2)}, u32[]{:S(2)}) collective-permute-start(bf16[544,128]{1,0:T(8,128)(2,1)} %fusion.1), channel_id=1, source_target_pairs={{0,16},{16,0},{1,17},{17,1},{2,18},{18,2},{3,19},{19,3},{4,20},{20... | collective-permute-start | bytes 417800 | tf_op jit(solution)/shard_map/ppermute | solution.py:220
  41.3 35.5 %copy-start = (bf16[1,1,1,2,16,16,16,128]{7,6,5,4,3,2,1,0:T(8,128)(2,1)S(1)}, bf16[1,1,1,2,16,16,16,128]{7,6,5,4,3,2,1,0:T(8,128)(2,1)}, u32[]{:S(2)}) copy-start(bf16[1,1,1,2,16,16,16,128]{7,6,5,4,3,2,1,0:T(8,128)(2,1)} %param.12) | copy-start | bytes 6291460
  44.0 0.7 copy-start.7
  44.7 4.6 %collective-permute-start.9 = (bf16[272,128]{1,0:T(8,128)(2,1)S(1)}, bf16[272,128]{1,0:T(8,128)(2,1)S(1)}, u32[]{:S(2)}, u32[]{:S(2)}) collective-permute-start(bf16[272,128]{1,0:T(8,128)(2,1)S(1)} %fusion.3), channel_id=1, source_target_pairs={{0,1},{1,0},{2,3},{3,2},{4,5},{5,4},{6,7},{7,6},{8,9},{9,8},{10,11... | collective-permute-start | bytes 208904 | tf_op jit(solution)/shard_map/ppermute | solution.py:220
  50.2 5.4 %collective-permute-start.10 = (bf16[272,128]{1,0:T(8,128)(2,1)S(1)}, bf16[272,128]{1,0:T(8,128)(2,1)S(1)}, u32[]{:S(2)}, u32[]{:S(2)}) collective-permute-start(bf16[272,128]{1,0:T(8,128)(2,1)S(1)} %fusion.5), channel_id=1, source_target_pairs={{0,2},{1,3},{2,0},{3,1},{4,6},{5,7},{6,4},{7,5},{8,10},{9,11},{10,... | collective-permute-start | bytes 208904 | tf_op jit(solution)/shard_map/ppermute | solution.py:220
  56.5 4.4 %collective-permute-start.11 = (bf16[272,128]{1,0:T(8,128)(2,1)S(1)}, bf16[272,128]{1,0:T(8,128)(2,1)S(1)}, u32[]{:S(2)}, u32[]{:S(2)}) collective-permute-start(bf16[272,128]{1,0:T(8,128)(2,1)S(1)} %fusion.2), channel_id=1, source_target_pairs={{0,4},{4,0},{8,12},{12,8},{1,5},{5,1},{9,13},{13,9},{2,6},{6,2},{1... | collective-permute-start | bytes 208904 | tf_op jit(solution)/shard_map/ppermute | solution.py:220
  61.8 5.6 %collective-permute-start.12 = (bf16[272,128]{1,0:T(8,128)(2,1)S(1)}, bf16[272,128]{1,0:T(8,128)(2,1)S(1)}, u32[]{:S(2)}, u32[]{:S(2)}) collective-permute-start(bf16[272,128]{1,0:T(8,128)(2,1)S(1)} %fusion.4), channel_id=1, source_target_pairs={{0,8},{4,12},{8,0},{12,4},{1,9},{5,13},{9,1},{13,5},{2,10},{6,14},... | collective-permute-start | bytes 208904 | tf_op jit(solution)/shard_map/ppermute | solution.py:220
  61.9 12.9 %collective-permute-start.5 = (bf16[2,16,16,128]{3,2,1,0:T(8,128)(2,1)S(1)}, bf16[2,16,16,128]{3,2,1,0:T(8,128)(2,1)S(1)}, u32[]{:S(2)}, u32[]{:S(2)}) collective-permute-start(bf16[2,16,16,128]{3,2,1,0:T(8,128)(2,1)S(1)} %get-tuple-element.26), channel_id=1, source_target_pairs={{4,8},{8,4},{5,9},{9,5},{6,10},{10,6},{7,11},{11,7},{20,24},{24,20... | collective-permute-start | bytes 393224 | tf_op jit(solution)/shard_map/ppermute | solution.py:207
  62.6 12.2 %collective-permute-start.4 = (bf16[2,16,16,128]{3,2,1,0:T(8,128)(2,1)S(1)}, bf16[2,16,16,128]{3,2,1,0:T(8,128)(2,1)S(1)}, u32[]{:S(2)}, u32[]{:S(2)}) collective-permute-start(bf16[2,16,16,128]{3,2,1,0:T(8,128)(2,1)S(1)} %get-tuple-element.27), channel_id=1, source_target_pairs={{0,4},{4,0},{8,12},{12,8},{1,5},{5,1},{9,13},{13,9},{2,6},{6,2},{1... | collective-permute-start | bytes 393224 | tf_op jit(solution)/shard_map/ppermute | solution.py:207
  68.4 5.4 %collective-permute-start.13 = (bf16[272,128]{1,0:T(8,128)(2,1)S(1)}, bf16[272,128]{1,0:T(8,128)(2,1)}, u32[]{:S(2)}, u32[]{:S(2)}) collective-permute-start(bf16[272,128]{1,0:T(8,128)(2,1)S(1)} %add_convert_fusion), channel_id=1, source_target_pairs={{0,1},{1,0},{2,3},{3,2},{4,5},{5,4},{6,7},{7,6},{8,9},{9,8},{10,11... | collective-permute-start | bytes 208904 | tf_op jit(solution)/shard_map/ppermute | solution.py:220
  70.9 4.0 %collective-permute-start.7 = (bf16[2,16,16,128]{3,2,1,0:T(8,128)(2,1)}, bf16[2,16,16,128]{3,2,1,0:T(8,128)(2,1)S(1)}, u32[]{:S(2)}, u32[]{:S(2)}) collective-permute-start(bf16[2,16,16,128]{3,2,1,0:T(8,128)(2,1)} %get-tuple-element.24), channel_id=1, source_target_pairs={{1,2},{2,1},{5,6},{6,5},{9,10},{10,9},{13,14},{14,13},{17,18},{18,... | collective-permute-start | bytes 393224 | tf_op jit(solution)/shard_map/ppermute | solution.py:207
  71.5 5.2 %collective-permute-start.6 = (bf16[2,16,16,128]{3,2,1,0:T(8,128)(2,1)}, bf16[2,16,16,128]{3,2,1,0:T(8,128)(2,1)S(1)}, u32[]{:S(2)}, u32[]{:S(2)}) collective-permute-start(bf16[2,16,16,128]{3,2,1,0:T(8,128)(2,1)} %get-tuple-element.25), channel_id=1, source_target_pairs={{0,1},{1,0},{2,3},{3,2},{4,5},{5,4},{6,7},{7,6},{8,9},{9,8},{10,11... | collective-permute-start | bytes 393224 | tf_op jit(solution)/shard_map/ppermute | solution.py:207
  74.7 10.8 %collective-permute-start.14 = (bf16[544,128]{1,0:T(8,128)(2,1)S(1)}, bf16[544,128]{1,0:T(8,128)(2,1)S(1)}, u32[]{:S(2)}, u32[]{:S(2)}) collective-permute-start(bf16[544,128]{1,0:T(8,128)(2,1)S(1)} %maximum_select_fusion.1), channel_id=1, source_target_pairs={{0,16},{16,0},{1,17},{17,1},{2,18},{18,2},{3,19},{19,3},{4,20},{20... | collective-permute-start | bytes 417800 | tf_op jit(solution)/shard_map/ppermute | solution.py:220
  76.8 1.6 %copy-start.2 = (bf16[2,16,16,16,128]{4,3,2,1,0:T(8,128)(2,1)S(1)}, bf16[2,16,16,16,128]{4,3,2,1,0:T(8,128)(2,1)}, u32[]{:S(2)}) copy-start(bf16[2,16,16,16,128]{4,3,2,1,0:T(8,128)(2,1)} %copy-done.1) | copy-start | bytes 6291460

commit v2 on v1

v2 whole, which is shorter than its diff:
```python
import functools

import jax
import jax.numpy as jnp
from jax import lax
from jax.experimental import pallas as pl
from jax.experimental.pallas import tpu as pltpu
from jax.sharding import PartitionSpec as P


BF = jnp.bfloat16
F32 = jnp.float32
PLANES = 8
PIECE = 16
GRANT = 60 * 1024 * 1024


def halo_copies(meta, slots, faces, vol, sems, first, planes, edge):
    found = []
    for s in range(slots):
        for f in range(4):
            link = meta[4 + s * 6 + f]
            axis, upper = f // 2, f % 2
            if axis == 0 and first + (planes if upper else 0) != (edge if upper else 0):
                continue
            source = jnp.minimum(link, slots - 1)
            if axis == 0:
                index = (s, planes + 1 if upper else 0, slice(1, edge + 1))
                arrived = [faces[ph].at[source] for ph in range(2)]
            else:
                index = (s, slice(1, planes + 1), edge + 1 if upper else 0)
                arrived = [faces[2 + ph].at[source, first : first + planes] for ph in range(2)]
            copies = [
                pltpu.make_async_copy(arrived[ph], vol.at[index], sems.at[s * 4 + f])
                for ph in range(2)
            ]
            phase = (meta[1 + axis] + upper + 1) % 2
            found.append((link < slots, phase, copies, index))
    return found


def start_halos(found, vol):
    for valid, phase, copies, index in found:
        for ph in range(2):
            @pl.when(valid & (phase == ph))
            def _(copy=copies[ph]):
                copy.start()

        @pl.when(jnp.logical_not(valid))
        def _(index=index):
            vol[index] = jnp.zeros(vol.at[index].shape, vol.dtype)


def wait_halos(found):
    for valid, _, copies, _ in found:
        @pl.when(valid)
        def _(copy=copies[0]):
            copy.wait()


def shifted(vol, s, x0, planes, dx, dy):
    edge = vol.shape[2] - 2
    view = vol[s, pl.ds(x0 + 1 + dx, planes), 1 + dy : 1 + dy + edge]
    return view.reshape(planes * edge * edge, vol.shape[4])


def z_shifted(meta, vol, zbuf, s, x0, planes):
    slots, edge, channels = vol.shape[0], vol.shape[2] - 2, vol.shape[4]
    rows = planes * edge * edge

    def beyond(face, part):
        link = meta[4 + s * 6 + face]
        other = vol[jnp.minimum(link, slots - 1), pl.ds(x0 + 1, planes), 1 : 1 + edge]
        other = other.astype(F32).reshape(planes * edge, edge, channels)[:, part]
        return jnp.where(link < slots, other, 0.0)

    centre = shifted(vol, s, x0, planes, 0, 0)
    zbuf[:, 0:8] = beyond(4, slice(edge - 8, edge))
    zbuf[:, 8 : 8 + edge] = centre.astype(F32).reshape(planes * edge, edge, channels)
    zbuf[:, 8 + edge : 16 + edge] = beyond(5, slice(0, 8))
    below = zbuf[:, 7 : 7 + edge].astype(BF).reshape(rows, channels)
    above = zbuf[:, 9 : 9 + edge].astype(BF).reshape(rows, channels)
    return below, above


def windows(meta, vol, zbuf, s, x0, planes, direction):
    below, above = z_shifted(meta, vol, zbuf, s, x0, planes)
    d = direction
    pieces = [
        shifted(vol, s, x0, planes, dx, dy)
        for dx, dy in ((0, 0), (-d, 0), (d, 0), (0, -d), (0, d))
    ]
    pieces += [below, above] if d > 0 else [above, below]
    return jnp.concatenate(pieces, axis=1)


def add_weight_terms(acc, turned, vol, zlow, zhigh, s, x0, planes):
    channels = vol.shape[4]
    near = [(0, 0), (-1, 0), (1, 0), (0, -1), (0, 1)]
    pieces = [lambda d=d: shifted(vol, s, x0, planes, *d) for d in near]
    pieces += [lambda: zlow[...], lambda: zhigh[...]]
    left = turned[...]
    for t in range(0, len(pieces), 2):
        right = jnp.concatenate([piece() for piece in pieces[t : t + 2]], axis=1)
        at = slice(t * channels, t * channels + right.shape[1])
        acc[:, at] += jnp.dot(left, right, preferred_element_type=F32)


def pick_kernel(feat, x0, x1, y0, y1, sems):
    edge = feat.shape[1]
    copies = []
    for i, out in enumerate((x0, x1, y0, y1)):
        upward = lax.axis_index(("mx", "my")[i // 2]) % 2 == i % 2
        layer = jnp.where(upward, edge - 1, 0)
        face = feat.at[:, layer] if i < 2 else feat.at[:, :, layer]
        copies.append(pltpu.make_async_copy(face, out, sems.at[i]))
    for copy in copies:
        copy.start()
    for copy in copies:
        copy.wait()


def finish_kernel(meta, own, other, conv_o, bias_o, head_o):
    half = own.shape[0]
    edges = (conv_o.shape[0], conv_o.shape[0] + head_o.shape[0])

    def place(h, value):
        lo = h * half
        n = min(max(edges[0] - lo, 0), half)
        if n:
            conv_o[lo : lo + n] = value[:n]
        start, stop = max(edges[0] - lo, 0), min(edges[1] - lo, half)
        if start < stop:
            at = lo + start - edges[0]
            head_o[at : at + stop - start] = value[start:stop]
        if 0 <= edges[1] - lo < half:
            bias_o[...] = value[edges[1] - lo : edges[1] - lo + 1]

    first = meta[3] == 0
    place(0, jnp.where(first, own[...], other[...]).astype(F32))
    place(1, jnp.where(first, other[...], own[...]).astype(F32))


def forward_kernel(
    meta, feat, x0f, x1f, y0f, y1f, w, bias, hw, gout, ghead,
    res_o, head_o, gpre_o, gx0_o, gx1_o, gy0_o, gy1_o, colg_o, pay_o,
    vol, zbuf, colsum, acc, turned, zlow, zhigh, sems,
):
    slots, edge, channels = feat.shape[0], feat.shape[1], feat.shape[4]
    s, xi = pl.program_id(0), pl.program_id(1)
    planes = res_o.shape[1]
    steps = edge // planes
    count = meta[0]
    scale = 1.0 / (edge * count).astype(F32)
    taps = w.shape[0] // channels

    @pl.when((s == 0) & (xi == 0))
    def _():
        body = [
            pltpu.make_async_copy(
                feat.at[i], vol.at[i, 1 : edge + 1, 1 : edge + 1], sems.at[slots * 4 + i]
            )
            for i in range(slots)
        ]
        found = halo_copies(meta, slots, (x0f, x1f, y0f, y1f), vol, sems, 0, edge, edge)
        for copy in body:
            copy.start()
        start_halos(found, vol)
        colg_o[...] = (
            lax.dot_general(
                ghead[...], hw[...], (((1,), (1,)), ((), ())), preferred_element_type=F32
            )
            * scale
        )
        pay_o[...] = jnp.zeros_like(pay_o)
        for ref in (acc, turned, zlow, zhigh):
            ref[...] = jnp.zeros_like(ref)
        colsum[...] = jnp.zeros_like(colsum)
        for copy in body:
            copy.wait()
        wait_halos(found)

    x0 = xi * planes
    rows = planes * edge * edge
    cols = planes * edge
    before_s = jnp.maximum(jnp.where(xi == 0, s - 1, s), 0)
    before_x0 = jnp.where(xi == 0, edge - planes, x0 - planes)
    add_weight_terms(acc, turned, vol, zlow, zhigh, before_s, before_x0, planes)
    stacked = windows(meta, vol, zbuf, s, x0, planes, 1)
    preact = jnp.dot(stacked, w[...], preferred_element_type=F32) + bias[...]
    occupied = s < count
    sigma = 0.5 * jnp.tanh(0.5 * preact) + 0.5
    silu = preact * sigma
    result = jnp.where(occupied, stacked[:, :channels].astype(F32) + silu, 0.0).astype(BF)
    res_o[0] = result.reshape(planes, edge, edge, channels)
    column = pl.ds(pl.multiple_of(x0 * edge, cols), cols)
    spread = colg_o[column].reshape(cols, 1, channels)
    grad_result = gout[0].astype(F32).reshape(cols, edge, channels) + spread
    slope = sigma * (1.0 + (preact - silu))
    gpre = jnp.where(occupied, grad_result.reshape(rows, channels) * slope, 0.0).astype(BF)
    gtile = gpre.reshape(planes, edge, edge, channels)
    gpre_o[0] = gtile
    for upper, step, layer in ((0, 0, 0), (1, steps - 1, planes - 1)):
        for phase, out in ((0, gx0_o), (1, gx1_o)):
            @pl.when((xi == step) & ((meta[1] == phase) == bool(upper)))
            def _(out=out, layer=layer):
                out[s] = gtile[layer]

    even = meta[2] == 0
    low, high = gtile[:, 0], gtile[:, edge - 1]
    gy0_o[s, pl.ds(x0, planes)] = jnp.where(even, high, low)
    gy1_o[s, pl.ds(x0, planes)] = jnp.where(even, low, high)

    of_row = lax.broadcasted_iota(jnp.int32, (cols, rows), 1) // edge
    pool = (of_row == lax.broadcasted_iota(jnp.int32, (cols, rows), 0)).astype(BF)
    colsum[column] += jnp.dot(pool, result, preferred_element_type=F32)
    tail = (taps + 1) * channels
    pay_o[tail : tail + 1] += jnp.sum(gpre.astype(F32), axis=0, keepdims=True)
    turned[...] = gpre.T
    zlow[...] = stacked[:, 5 * channels : 6 * channels]
    zhigh[...] = stacked[:, 6 * channels : 7 * channels]

    @pl.when((s == slots - 1) & (xi == steps - 1))
    def _():
        add_weight_terms(acc, turned, vol, zlow, zhigh, s, x0, planes)
        for t in range(taps):
            at = slice(t * channels, (t + 1) * channels)
            pay_o[at] = acc[:, at].T
        column_bf = (colsum[...] * scale).astype(BF)
        head_o[...] = jnp.dot(column_bf, hw[...], preferred_element_type=F32).astype(BF)
        pay_o[taps * channels : tail] = lax.dot_general(
            column_bf, ghead[...], (((0,), (0,)), ((), ())), preferred_element_type=F32
        )


def backward_kernel(first, meta, grad, x0f, x1f, y0f, y1f, wt, gout, colg, *rest):
    out_o, vol, zbuf, sems = rest[-4:]
    slots, edge, channels = grad.shape[0], grad.shape[1], grad.shape[4]
    planes = gout.shape[1]
    s = pl.program_id(0)

    @pl.when(s == 0)
    def _():
        below, above = min(first, 1), min(edge - first - planes, 1)
        body = [
            pltpu.make_async_copy(
                grad.at[i, first - below : first + planes + above],
                vol.at[i, 1 - below : 1 + planes + above, 1 : edge + 1],
                sems.at[slots * 4 + i],
            )
            for i in range(slots)
        ]
        found = halo_copies(meta, slots, (x0f, x1f, y0f, y1f), vol, sems, first, planes, edge)
        for copy in body:
            copy.start()
        start_halos(found, vol)
        for copy in body:
            copy.wait()
        wait_halos(found)

    rows = planes * edge * edge
    cols = planes * edge
    stacked = windows(meta, vol, zbuf, s, 0, planes, -1)
    conv = jnp.dot(stacked, wt[...], preferred_element_type=F32)
    spread = colg[first * edge : first * edge + cols].reshape(cols, 1, channels)
    grad_result = gout[0].astype(F32).reshape(cols, edge, channels) + spread
    total = jnp.where(s < meta[0], grad_result.reshape(rows, channels) + conv, 0.0).astype(BF)
    out_o[0] = total.reshape(planes, edge, edge, channels)


def swap(x, axis, odd):
    pairs = []
    for i in range(odd, lax.axis_size(axis) - 1, 2):
        pairs += [(i, i + 1), (i + 1, i)]
    return lax.ppermute(x, axis, pairs)


def swap_faces(sent, axis):
    arrived = []
    for odd in range(2):
        arrived.append(swap(sent[odd], axis, odd))
    return arrived


def partner(x, axis, bit):
    return lax.ppermute(x, axis, [(i, i ^ (1 << bit)) for i in range(lax.axis_size(axis))])


def own_bit(axis, bit):
    return (lax.axis_index(axis) >> bit) & 1


def halved(x, axis, bit):
    me = own_bit(axis, bit)
    parts = x.reshape((2, x.shape[0] // 2) + x.shape[1:])
    own = lax.dynamic_index_in_dim(parts, me, 0, False)
    sent = lax.dynamic_index_in_dim(parts, 1 - me, 0, False)
    return own + partner(sent.astype(BF), axis, bit).astype(F32)


def summed(x, axis, bit):
    return x + partner(x.astype(BF), axis, bit).astype(F32)


def doubled(x, axis, bit):
    other = partner(x, axis, bit)
    return jnp.where(
        own_bit(axis, bit) == 0, jnp.concatenate([x, other]), jnp.concatenate([other, x])
    )


def bits(axis):
    return range((lax.axis_size(axis) - 1).bit_length())


def all_summed(x):
    x = halved(x, "region", 0)
    x = halved(x, "my", 0)
    rest = [(axis, b) for axis in ("mx", "my") for b in bits(axis)]
    rest.remove(("my", 0))
    for axis, bit in sorted(rest, key=lambda stage: stage[1]):
        x = summed(x, axis, bit)
    x = doubled(x.astype(BF), "my", 0)
    return x, partner(x, "region", 0)


def body(
    features_in, conv_weight, conv_bias, head_weight, grad_out, grad_head, block_count, neighbours
):
    blocks = features_in.reshape(features_in.shape[3:])
    upstream = grad_out.reshape(grad_out.shape[3:])
    head_grad = grad_head.reshape(grad_head.shape[3:])
    slots, edge, channels = blocks.shape[0], blocks.shape[1], blocks.shape[4]
    taps = conv_weight.shape[0]
    meta = jnp.concatenate(
        [
            block_count.reshape(1),
            (lax.axis_index("mx") % 2).astype(jnp.int32).reshape(1),
            (lax.axis_index("my") % 2).astype(jnp.int32).reshape(1),
            lax.axis_index("region").astype(jnp.int32).reshape(1),
            neighbours.reshape(-1),
        ]
    )
    anywhere = pl.BlockSpec(memory_space=pl.ANY)
    hbm = pl.BlockSpec(memory_space=pltpu.HBM)
    vmem = pl.BlockSpec(memory_space=pltpu.VMEM)
    face = jax.ShapeDtypeStruct((slots, edge, edge, channels), BF)
    sent = pl.pallas_call(
        pick_kernel,
        in_specs=[hbm],
        out_specs=[vmem] * 4,
        scratch_shapes=[pltpu.SemaphoreType.DMA((4,))],
        out_shape=[face] * 4,
        name="pick",
    )(blocks)
    faces = swap_faces(sent[:2], "mx") + swap_faces(sent[2:], "my")

    whole = lambda *shape: pl.BlockSpec(shape, lambda i, j, m: (0,) * len(shape))
    tile = pl.BlockSpec((1, PLANES, edge, edge, channels), lambda i, j, m: (i, j, 0, 0, 0))
    volume = (slots, edge, edge, edge, channels)
    padded = pltpu.VMEM((slots, edge + 2, edge + 2, edge, channels), BF)
    columns = edge * edge
    pay_rows = ((taps + 1) * channels // 64 + 1) * 64
    flops = 2 * slots * edge**3 * taps * channels * channels
    moved = slots * edge**3 * channels * 2
    params = pltpu.CompilerParams(
        dimension_semantics=("arbitrary", "arbitrary"), vmem_limit_bytes=GRANT
    )
    result, head_tile, gpre, gx0, gx1, gy0, gy1, colg, pay = pl.pallas_call(
        forward_kernel,
        grid_spec=pltpu.PrefetchScalarGridSpec(
            num_scalar_prefetch=1,
            grid=(slots, edge // PLANES),
            in_specs=[
                hbm, anywhere, anywhere, anywhere, anywhere,
                whole(taps * channels, channels), whole(1, channels), whole(channels, channels),
                tile, whole(columns, channels),
            ],
            out_specs=[
                tile, whole(columns, channels), tile,
                *[whole(slots, edge, edge, channels)] * 4,
                whole(columns, channels), whole(pay_rows, channels),
            ],
            scratch_shapes=[
                padded, pltpu.VMEM((PLANES * edge, edge + 16, channels), F32),
                pltpu.VMEM((columns, channels), F32),
                pltpu.VMEM((channels, taps * channels), F32),
                pltpu.VMEM((channels, PLANES * columns), BF),
                pltpu.VMEM((PLANES * columns, channels), BF),
                pltpu.VMEM((PLANES * columns, channels), BF),
                pltpu.SemaphoreType.DMA((slots * 5,)),
            ],
        ),
        out_shape=[
            jax.ShapeDtypeStruct(volume, BF),
            jax.ShapeDtypeStruct((columns, channels), BF),
            jax.ShapeDtypeStruct(volume, BF),
            *[face] * 4,
            jax.ShapeDtypeStruct((columns, channels), F32),
            jax.ShapeDtypeStruct((pay_rows, channels), F32),
        ],
        compiler_params=params,
        cost_estimate=pl.CostEstimate(
            flops=2 * flops, bytes_accessed=5 * moved, transcendentals=moved // 2
        ),
        name="forward",
    )(
        meta, blocks, *faces, conv_weight.reshape(taps * channels, channels),
        conv_bias.reshape(1, channels), head_weight, upstream, head_grad,
    )

    grad_faces = swap_faces((gx0, gx1), "mx") + swap_faces((gy0, gy1), "my")
    turned = jnp.transpose(conv_weight, (0, 2, 1)).reshape(taps * channels, channels)
    grad_local = None
    pieces = edge // PIECE
    for k in range(pieces):
        part = pl.BlockSpec((1, PIECE, edge, edge, channels), lambda i, m, k=k: (i, k, 0, 0, 0))
        all_of = lambda *shape: pl.BlockSpec(shape, lambda i, m: (0,) * len(shape))
        operands = [meta, gpre, *grad_faces, turned, upstream, colg]
        specs = [hbm] + [anywhere] * 4
        specs += [all_of(taps * channels, channels), part, all_of(columns, channels)]
        if grad_local is not None:
            operands.append(grad_local)
            specs.append(hbm)
        grad_local = pl.pallas_call(
            functools.partial(backward_kernel, k * PIECE),
            grid_spec=pltpu.PrefetchScalarGridSpec(
                num_scalar_prefetch=1,
                grid=(slots,),
                in_specs=specs,
                out_specs=part,
                scratch_shapes=[
                    pltpu.VMEM((slots, PIECE + 2, edge + 2, edge, channels), BF),
                    pltpu.VMEM((PIECE * edge, edge + 16, channels), F32),
                    pltpu.SemaphoreType.DMA((slots * 5,)),
                ],
            ),
            out_shape=jax.ShapeDtypeStruct(volume, BF),
            input_output_aliases={len(operands) - 1: 0} if k else {},
            compiler_params=pltpu.CompilerParams(
                dimension_semantics=("arbitrary",), vmem_limit_bytes=GRANT
            ),
            cost_estimate=pl.CostEstimate(
                flops=flops // pieces, bytes_accessed=4 * moved // pieces, transcendentals=0
            ),
        )(*operands)

    own, other = all_summed(pay)
    conv_rows = taps * channels
    grad_conv, grad_bias, grad_head_weight = pl.pallas_call(
        finish_kernel,
        grid_spec=pltpu.PrefetchScalarGridSpec(
            num_scalar_prefetch=1, grid=(), in_specs=[vmem] * 2, out_specs=[vmem] * 3
        ),
        out_shape=[
            jax.ShapeDtypeStruct((conv_rows, channels), F32),
            jax.ShapeDtypeStruct((1, channels), F32),
            jax.ShapeDtypeStruct((channels, channels), F32),
        ],
        name="finish",
    )(meta, own, other)
    return (
        result.reshape(features_in.shape),
        head_tile.reshape(grad_head.shape),
        grad_local.reshape(features_in.shape),
        grad_conv.reshape(conv_weight.shape),
        grad_bias.reshape(channels),
        grad_head_weight,
    )


def solution(mesh):
    tiles = P("region", "mx", "my", None, None, None, None, None)
    rows = P("region", "mx", "my", None, None)

    return jax.shard_map(
        body,
        mesh=mesh,
        in_specs=(tiles, P(), P(), P(), tiles, rows, P("region", "mx", "my"), rows),
        out_specs=(tiles, rows, tiles, P(), P(), P()),
        check_vma=False,
    )
```

time: 88 us -> 81.9 us (0.931)
  the two profiles are of different devices: /device:TPU:0 before, /device:TPU:18 now
where the time goes in v2:
time: 81.9 us; the launch traced here: 81.5 us
  Pallas kernels  30.7 us (37%)
  waiting for transfers between devices  27 us (33%)
  starting transfers between devices  16.4 us (20%)
  local copies, waits for them, and re-layouts  4.64 us (6%)
  between operations  1.61 us (2%)
  other arithmetic  1.15 us (1%)
    ppermute x7, waiting for transfers between devices, partner(): lax.ppermute(x, axis, [(i, i ^ 1 << bit) for i in range(lax.axis_size(axi...  19.4 us
    pallas_call x1, Pallas kernels, body(): pl.pallas_call(forward_kernel, grid_spec=pltpu.PrefetchScalarGridSpec(num...  16.9 us
    ppermute x8, starting transfers between devices, swap(): return lax.ppermute(x, axis, pairs)  15.6 us
    pallas_call x1, Pallas kernels, body(): pl.pallas_call(functools.partial(backward_kernel, k * PIECE), grid_spec=p...  9.45 us
    ppermute x8, waiting for transfers between devices, swap(): return lax.ppermute(x, axis, pairs)  7.6 us
    pallas_call x1, Pallas kernels, body(): pl.pallas_call(finish_kernel, grid_spec=pltpu.PrefetchScalarGridSpec(num_...  2.47 us
    unnamed x32, local copies, waits for them, and re-layouts  1.98 us
    pallas_call x1, Pallas kernels, body(): pl.pallas_call(pick_kernel, in_specs=[hbm], out_specs=[vmem] * 4, scratch...  1.92 us
  transfers between devices with their start and end apart: 15, of which 9 were waited for; matrix products, arithmetic and copies ran while one was open for 2% of the time, Pallas kernels for 12%

profile of v2, /device:TPU:18, one launch (start us, length us, event | category | flops | bytes accessed | tf_op | source)
XLA Modules:
  0.0 81.5 jit_solution(561394762164983511)
XLA Ops:
  0.6 0.0 copy-start.15
  0.6 1.9 %pick.1 = (bf16[2,16,16,128]{3,2,1,0:T(8,128)(2,1)}, bf16[2,16,16,128]{3,2,1,0:T(8,128)(2,1)}, bf16[2,16,16,128]{3,2,1,0:T(8,128)(2,1)}, bf16[2,16,16,128]{3,2,1,0:T(8,128)(2,1)}) custom-call(bf16[2,16,16,16,128]{4,3,2,1,0:T(8,128)(2,1)} %bitcast.43), custom_call_target="tpu_custom_call" | custom-call | tf_op jit(solution)/shard_map/pick/pallas_call | solution.py:348
  2.6 0.6 collective-permute-start
  3.2 4.3 %collective-permute-start.1 = (bf16[2,16,16,128]{3,2,1,0:T(8,128)(2,1)}, bf16[2,16,16,128]{3,2,1,0:T(8,128)(2,1)S(1)}, u32[]{:S(2)}, u32[]{:S(2)}) collective-permute-start(bf16[2,16,16,128]{3,2,1,0:T(8,128)(2,1)} %get-tuple-element.23), channel_id=1, source_target_pairs={{4,8},{8,4},{5,9},{9,5},{6,10},{10,6},{7,11},{11,7},{20,24},{24,20... | collective-permute-start | bytes 393224 | tf_op jit(solution)/shard_map/ppermute | solution.py:275
  7.5 1.6 %collective-permute-start.2 = (bf16[2,16,16,128]{3,2,1,0:T(8,128)(2,1)}, bf16[2,16,16,128]{3,2,1,0:T(8,128)(2,1)S(1)}, u32[]{:S(2)}, u32[]{:S(2)}) collective-permute-start(bf16[2,16,16,128]{3,2,1,0:T(8,128)(2,1)} %get-tuple-element.24), channel_id=1, source_target_pairs={{0,1},{1,0},{2,3},{3,2},{4,5},{5,4},{6,7},{7,6},{8,9},{9,8},{10,11... | collective-permute-start | bytes 393224 | tf_op jit(solution)/shard_map/ppermute | solution.py:275
  9.2 1.9 %collective-permute-start.3 = (bf16[2,16,16,128]{3,2,1,0:T(8,128)(2,1)}, bf16[2,16,16,128]{3,2,1,0:T(8,128)(2,1)S(1)}, u32[]{:S(2)}, u32[]{:S(2)}) collective-permute-start(bf16[2,16,16,128]{3,2,1,0:T(8,128)(2,1)} %get-tuple-element.25), channel_id=1, source_target_pairs={{1,2},{2,1},{5,6},{6,5},{9,10},{10,9},{13,14},{14,13},{17,18},{18,... | collective-permute-start | bytes 393224 | tf_op jit(solution)/shard_map/ppermute | solution.py:275
  11.7 0.0 copy-done.15
  11.8 0.1 reshape.72
  11.8 0.7 concatenate.9.meta
  12.5 0.0 collective-permute-done.x0f
  12.5 0.0 collective-permute-done.1.x1f
  12.5 0.0 copy-start.12
  12.5 0.2 collective-permute-done.2.y0f
  12.8 3.5 %collective-permute-done.3.y1f = bf16[2,16,16,128]{3,2,1,0:T(8,128)(2,1)S(1)} collective-permute-done((bf16[2,16,16,128]{3,2,1,0:T(8,128)(2,1)}, bf16[2,16,16,128]{3,2,1,0:T(8,128)(2,1)S(1)}, u32[]{:S(2)}, u32[]{:S(2)}) %collective-permute-start.3) | collective-permute-done | bytes 131104 | tf_op jit(solution)/shard_map/ppermute | solution.py:275
  16.2 0.0 copy-done.11
  16.2 0.0 copy-done.12
  16.2 0.0 copy-done.13
  16.2 0.6 copy-done.14
  16.9 16.9 %forward.1 = (bf16[2,16,16,16,128]{4,3,2,1,0:T(8,128)(2,1)}, bf16[256,128]{1,0:T(8,128)(2,1)}, bf16[2,16,16,16,128]{4,3,2,1,0:T(8,128)(2,1)}, bf16[2,16,16,128]{...) custom-call(s32[16]{0:T(128)} %concatenate.9.meta, ...), custom_call_target="tpu_custom_call" | custom-call | flops 3758096384 | bytes 10485760 | tf_op jit(solution)/shard_map/forward/pallas_call | solution.py:369
  33.8 0.0 copy-start.10
  33.8 0.0 copy-start.9
  33.8 0.0 copy-start.8
  33.8 0.0 copy-start.7
  33.8 0.0 copy-start.1
  33.8 1.1 %fusion = bf16[544,128]{1,0:T(8,128)(2,1)S(1)} fusion(f32[2,544,128]{2,1,0:T(8,128)} %bitcast.46, s32[]{:T(128)S(6)} %select_n.37), kind=kLoop, calls=%fused_computation.2 | loop fusion | bytes 278532 | tf_op jit(solution)/shard_map/convert_element_type | solution.py:298
  34.9 0.1 collective-permute-start.8
  35.0 1.3 %collective-permute-done.8 = bf16[544,128]{1,0:T(8,128)(2,1)S(1)} collective-permute-done((bf16[544,128]{1,0:T(8,128)(2,1)S(1)}, bf16[544,128]{1,0:T(8,128)(2,1)S(1)}, u32[]{:S(2)}, u32[]{:S(2)}) %collective-permute-start.8) | collective-permute-done | bytes 139296 | tf_op jit(solution)/shard_map/ppermute | solution.py:286
  36.3 1.0 %bitcast_add_fusion = f32[544,128]{1,0:T(8,128)S(1)} fusion(bf16[544,128]{1,0:T(8,128)(2,1)S(1)} %collective-permute-done.8, f32[2,544,128]{2,1,0:T(8,128)} %bitcast.47, s32[]{:T(128)S(6)} %select_n.36), kind=kLoop, calls=%fused_computation | loop fusion | flops 139264 | bytes 696324 | tf_op jit(solution)/shard_map/add | solution.py:298
  37.3 0.1 collective-permute-start.9
  37.4 4.3 %collective-permute-done.9 = bf16[272,128]{1,0:T(8,128)(2,1)S(1)} collective-permute-done((bf16[272,128]{1,0:T(8,128)(2,1)S(1)}, bf16[272,128]{1,0:T(8,128)(2,1)S(1)}, u32[]{:S(2)}, u32[]{:S(2)}) %collective-permute-start.9) | collective-permute-done | bytes 69664 | tf_op jit(solution)/shard_map/ppermute | solution.py:286
  41.7 0.1 collective-permute-start.10
  41.8 4.3 %collective-permute-done.10 = bf16[272,128]{1,0:T(8,128)(2,1)S(1)} collective-permute-done((bf16[272,128]{1,0:T(8,128)(2,1)S(1)}, bf16[272,128]{1,0:T(8,128)(2,1)S(1)}, u32[]{:S(2)}, u32[]{:S(2)}) %collective-permute-start.10) | collective-permute-done | bytes 69664 | tf_op jit(solution)/shard_map/ppermute | solution.py:286
  46.1 0.1 collective-permute-start.11
  46.2 4.3 %collective-permute-done.11 = bf16[272,128]{1,0:T(8,128)(2,1)S(1)} collective-permute-done((bf16[272,128]{1,0:T(8,128)(2,1)S(1)}, bf16[272,128]{1,0:T(8,128)(2,1)S(1)}, u32[]{:S(2)}, u32[]{:S(2)}) %collective-permute-start.11) | collective-permute-done | bytes 69664 | tf_op jit(solution)/shard_map/ppermute | solution.py:286
  50.6 0.1 collective-permute-start.12
  50.6 5.2 %collective-permute-done.12 = bf16[272,128]{1,0:T(8,128)(2,1)S(1)} collective-permute-done((bf16[272,128]{1,0:T(8,128)(2,1)S(1)}, bf16[272,128]{1,0:T(8,128)(2,1)S(1)}, u32[]{:S(2)}, u32[]{:S(2)}) %collective-permute-start.12) | collective-permute-done | bytes 69664 | tf_op jit(solution)/shard_map/ppermute | solution.py:286
  55.8 0.1 add_convert_fusion
  55.9 0.4 collective-permute-start.13
  56.3 0.0 copy-done.10
  56.3 0.0 collective-permute-start.4
  56.3 0.0 copy-done.9
  56.3 3.4 %collective-permute-start.5 = (bf16[2,16,16,128]{3,2,1,0:T(8,128)(2,1)S(1)}, bf16[2,16,16,128]{3,2,1,0:T(8,128)(2,1)S(1)}, u32[]{:S(2)}, u32[]{:S(2)}) collective-permute-start(bf16[2,16,16,128]{3,2,1,0:T(8,128)(2,1)S(1)} %copy-done.9), channel_id=1, source_target_pairs={{4,8},{8,4},{5,9},{9,5},{6,10},{10,6},{7,11},{11,7},{20,24},{24,20... | collective-permute-start | bytes 393224 | tf_op jit(solution)/shard_map/ppermute | solution.py:275
  59.6 0.0 copy-done.8
  59.6 1.8 %collective-permute-start.6 = (bf16[2,16,16,128]{3,2,1,0:T(8,128)(2,1)S(1)}, bf16[2,16,16,128]{3,2,1,0:T(8,128)(2,1)S(1)}, u32[]{:S(2)}, u32[]{:S(2)}) collective-permute-start(bf16[2,16,16,128]{3,2,1,0:T(8,128)(2,1)S(1)} %copy-done.8), channel_id=1, source_target_pairs={{0,1},{1,0},{2,3},{3,2},{4,5},{5,4},{6,7},{7,6},{8,9},{9,8},{10,11... | collective-permute-start | bytes 393224 | tf_op jit(solution)/shard_map/ppermute | solution.py:275
  61.4 0.0 copy-done.7
  61.4 1.9 %collective-permute-start.7 = (bf16[2,16,16,128]{3,2,1,0:T(8,128)(2,1)S(1)}, bf16[2,16,16,128]{3,2,1,0:T(8,128)(2,1)S(1)}, u32[]{:S(2)}, u32[]{:S(2)}) collective-permute-start(bf16[2,16,16,128]{3,2,1,0:T(8,128)(2,1)S(1)} %copy-done.7), channel_id=1, source_target_pairs={{1,2},{2,1},{5,6},{6,5},{9,10},{10,9},{13,14},{14,13},{17,18},{18,... | collective-permute-start | bytes 393224 | tf_op jit(solution)/shard_map/ppermute | solution.py:275
  63.4 0.0 copy-done.1
  63.4 0.8 %copy.14 = bf16[7,128,128]{2,1,0:T(8,128)(2,1)} copy(bf16[7,128,128]{1,2,0:T(8,128)(2,1)S(1)} %bitcast.49) | data formatting | bytes 458752 | tf_op jit(solution)/shard_map/transpose | solution.py:413
  64.2 0.0 collective-permute-done.13
  64.3 0.0 copy-start
  64.3 0.1 collective-permute-start.14
  64.3 0.0 collective-permute-done.4.x0f
  64.3 0.0 copy-start.3
  64.4 0.0 collective-permute-done.5.x1f
  64.4 0.0 copy-start.4
  64.4 0.3 collective-permute-done.6.y0f
  64.7 3.6 %collective-permute-done.7.y1f = bf16[2,16,16,128]{3,2,1,0:T(8,128)(2,1)S(1)} collective-permute-done((bf16[2,16,16,128]{3,2,1,0:T(8,128)(2,1)S(1)}, bf16[2,16,16,128]{3,2,1,0:T(8,128)(2,1)S(1)}, u32[]{:S(2)}, u32[]{:S(2)}) %collective-permute-start.7) | collective-permute-done | bytes 131104 | tf_op jit(solution)/shard_map/ppermute | solution.py:275
  68.3 0.0 copy-done.5
  68.3 0.6 copy-done.6
  68.9 9.4 %shard_map.127 = bf16[2,16,16,16,128]{4,3,2,1,0:T(8,128)(2,1)} custom-call(s32[16]{0:T(128)} %concatenate.9.meta, bf16[2,16,16,16,128]{4,3,2,1,0:T(8,128)(2,1)} %get-tuple-element.28.grad, bf16[2,16,16,128]{3,2,1,0:T(8,128)(2,1)} %copy-done.3, bf16[2,16,16,128]{3,2,1,0:T(8,128)(2,1)} %copy-done.4, bf16[2,16,16,128]{3,2,1,0:T(8,128)(2,1)} %copy-done.5, ...), custom_call_target="tpu_custom_call" | custom-call | flops 1879048192 | bytes 8388608 | tf_op jit(solution)/shard_map/pallas_call | solution.py:425
  78.4 0.0 collective-permute-done.14.other
  78.4 0.0 copy-start.2
  78.4 0.6 copy-done.2
  79.0 2.5 %finish.1 = (f32[896,128]{1,0:T(8,128)}, f32[1,128]{1,0:T(1,128)}, f32[128,128]{1,0:T(8,128)}) custom-call(s32[16]{0:T(128)} %concatenate.9.meta, bf16[544,128]{1,0:T(8,128)(2,1)} %copy-done, bf16[544,128]{1,0:T(8,128)(2,1)} %copy-done.2), custom_call_target="tpu_custom_call" | custom-call | tf_op jit(solution)/shard_map/finish/pallas_call | solution.py:450
  (13 shorter events, 0.2 us)
Async XLA Ops:
  0.6 11.1 %copy-start.15 = (s32[1,1,1,2,6]{4,3,2,1,0:T(2,128)S(1)}, s32[1,1,1,2,6]{4,3,2,1,0:T(2,128)}, u32[]{:S(2)}) copy-start(s32[1,1,1,2,6]{4,3,2,1,0:T(2,128)} %param.15) | copy-start | bytes 148
  2.6 9.9 %collective-permute-start = (bf16[2,16,16,128]{3,2,1,0:T(8,128)(2,1)}, bf16[2,16,16,128]{3,2,1,0:T(8,128)(2,1)S(1)}, u32[]{:S(2)}, u32[]{:S(2)}) collective-permute-start(bf16[2,16,16,128]{3,2,1,0:T(8,128)(2,1)} %get-tuple-element.22), channel_id=1, source_target_pairs={{0,4},{4,0},{8,12},{12,8},{1,5},{5,1},{9,13},{13,9},{2,6},{6,2},{1... | collective-permute-start | bytes 393224 | tf_op jit(solution)/shard_map/ppermute | solution.py:275
  3.2 9.3 %collective-permute-start.1 = (bf16[2,16,16,128]{3,2,1,0:T(8,128)(2,1)}, bf16[2,16,16,128]{3,2,1,0:T(8,128)(2,1)S(1)}, u32[]{:S(2)}, u32[]{:S(2)}) collective-permute-start(bf16[2,16,16,128]{3,2,1,0:T(8,128)(2,1)} %get-tuple-element.23), channel_id=1, source_target_pairs={{4,8},{8,4},{5,9},{9,5},{6,10},{10,6},{7,11},{11,7},{20,24},{24,20... | collective-permute-start | bytes 393224 | tf_op jit(solution)/shard_map/ppermute | solution.py:275
  7.5 5.2 %collective-permute-start.2 = (bf16[2,16,16,128]{3,2,1,0:T(8,128)(2,1)}, bf16[2,16,16,128]{3,2,1,0:T(8,128)(2,1)S(1)}, u32[]{:S(2)}, u32[]{:S(2)}) collective-permute-start(bf16[2,16,16,128]{3,2,1,0:T(8,128)(2,1)} %get-tuple-element.24), channel_id=1, source_target_pairs={{0,1},{1,0},{2,3},{3,2},{4,5},{5,4},{6,7},{7,6},{8,9},{9,8},{10,11... | collective-permute-start | bytes 393224 | tf_op jit(solution)/shard_map/ppermute | solution.py:275
  9.2 7.1 %collective-permute-start.3 = (bf16[2,16,16,128]{3,2,1,0:T(8,128)(2,1)}, bf16[2,16,16,128]{3,2,1,0:T(8,128)(2,1)S(1)}, u32[]{:S(2)}, u32[]{:S(2)}) collective-permute-start(bf16[2,16,16,128]{3,2,1,0:T(8,128)(2,1)} %get-tuple-element.25), channel_id=1, source_target_pairs={{1,2},{2,1},{5,6},{6,5},{9,10},{10,9},{13,14},{14,13},{17,18},{18,... | collective-permute-start | bytes 393224 | tf_op jit(solution)/shard_map/ppermute | solution.py:275
  12.5 3.7 %copy-start.11 = (bf16[2,16,16,128]{3,2,1,0:T(8,128)(2,1)}, bf16[2,16,16,128]{3,2,1,0:T(8,128)(2,1)S(1)}, u32[]{:S(2)}) copy-start(bf16[2,16,16,128]{3,2,1,0:T(8,128)(2,1)S(1)} %collective-permute-done.x0f) | copy-start | bytes 393220
  12.5 3.7 %copy-start.12 = (bf16[2,16,16,128]{3,2,1,0:T(8,128)(2,1)}, bf16[2,16,16,128]{3,2,1,0:T(8,128)(2,1)S(1)}, u32[]{:S(2)}) copy-start(bf16[2,16,16,128]{3,2,1,0:T(8,128)(2,1)S(1)} %collective-permute-done.1.x1f) | copy-start | bytes 393220
  12.8 3.5 %copy-start.13 = (bf16[2,16,16,128]{3,2,1,0:T(8,128)(2,1)}, bf16[2,16,16,128]{3,2,1,0:T(8,128)(2,1)S(1)}, u32[]{:S(2)}) copy-start(bf16[2,16,16,128]{3,2,1,0:T(8,128)(2,1)S(1)} %collective-permute-done.2.y0f) | copy-start | bytes 393220
  16.2 0.7 copy-start.14
  33.8 22.5 %copy-start.10 = (bf16[2,16,16,128]{3,2,1,0:T(8,128)(2,1)S(1)}, bf16[2,16,16,128]{3,2,1,0:T(8,128)(2,1)}, u32[]{:S(2)}) copy-start(bf16[2,16,16,128]{3,2,1,0:T(8,128)(2,1)} %get-tuple-element.29) | copy-start | bytes 393220
  33.8 22.5 %copy-start.9 = (bf16[2,16,16,128]{3,2,1,0:T(8,128)(2,1)S(1)}, bf16[2,16,16,128]{3,2,1,0:T(8,128)(2,1)}, u32[]{:S(2)}) copy-start(bf16[2,16,16,128]{3,2,1,0:T(8,128)(2,1)} %get-tuple-element.30) | copy-start | bytes 393220
  33.8 25.8 %copy-start.8 = (bf16[2,16,16,128]{3,2,1,0:T(8,128)(2,1)S(1)}, bf16[2,16,16,128]{3,2,1,0:T(8,128)(2,1)}, u32[]{:S(2)}) copy-start(bf16[2,16,16,128]{3,2,1,0:T(8,128)(2,1)} %get-tuple-element.31) | copy-start | bytes 393220
  33.8 27.6 %copy-start.7 = (bf16[2,16,16,128]{3,2,1,0:T(8,128)(2,1)S(1)}, bf16[2,16,16,128]{3,2,1,0:T(8,128)(2,1)}, u32[]{:S(2)}) copy-start(bf16[2,16,16,128]{3,2,1,0:T(8,128)(2,1)} %get-tuple-element.32) | copy-start | bytes 393220
  33.8 29.5 %copy-start.1 = (bf16[7,128,128]{2,1,0:T(8,128)(2,1)S(1)}, bf16[7,128,128]{2,1,0:T(8,128)(2,1)}, u32[]{:S(2)}) copy-start(bf16[7,128,128]{2,1,0:T(8,128)(2,1)} %param.9) | copy-start | bytes 688132
  34.9 1.4 %collective-permute-start.8 = (bf16[544,128]{1,0:T(8,128)(2,1)S(1)}, bf16[544,128]{1,0:T(8,128)(2,1)S(1)}, u32[]{:S(2)}, u32[]{:S(2)}) collective-permute-start(bf16[544,128]{1,0:T(8,128)(2,1)S(1)} %fusion), channel_id=1, source_target_pairs={{0,16},{16,0},{1,17},{17,1},{2,18},{18,2},{3,19},{19,3},{4,20},{20... | collective-permute-start | bytes 417800 | tf_op jit(solution)/shard_map/ppermute | solution.py:286
  37.3 4.4 %collective-permute-start.9 = (bf16[272,128]{1,0:T(8,128)(2,1)S(1)}, bf16[272,128]{1,0:T(8,128)(2,1)S(1)}, u32[]{:S(2)}, u32[]{:S(2)}) collective-permute-start(bf16[272,128]{1,0:T(8,128)(2,1)S(1)} %fusion.2), channel_id=1, source_target_pairs={{0,1},{1,0},{2,3},{3,2},{4,5},{5,4},{6,7},{7,6},{8,9},{9,8},{10,11... | collective-permute-start | bytes 208904 | tf_op jit(solution)/shard_map/ppermute | solution.py:286
  41.7 4.4 %collective-permute-start.10 = (bf16[272,128]{1,0:T(8,128)(2,1)S(1)}, bf16[272,128]{1,0:T(8,128)(2,1)S(1)}, u32[]{:S(2)}, u32[]{:S(2)}) collective-permute-start(bf16[272,128]{1,0:T(8,128)(2,1)S(1)} %fusion.4), channel_id=1, source_target_pairs={{0,4},{4,0},{8,12},{12,8},{1,5},{5,1},{9,13},{13,9},{2,6},{6,2},{1... | collective-permute-start | bytes 208904 | tf_op jit(solution)/shard_map/ppermute | solution.py:286
  46.1 4.4 %collective-permute-start.11 = (bf16[272,128]{1,0:T(8,128)(2,1)S(1)}, bf16[272,128]{1,0:T(8,128)(2,1)S(1)}, u32[]{:S(2)}, u32[]{:S(2)}) collective-permute-start(bf16[272,128]{1,0:T(8,128)(2,1)S(1)} %fusion.1), channel_id=1, source_target_pairs={{0,8},{4,12},{8,0},{12,4},{1,9},{5,13},{9,1},{13,5},{2,10},{6,14},... | collective-permute-start | bytes 208904 | tf_op jit(solution)/shard_map/ppermute | solution.py:286
  50.6 5.3 %collective-permute-start.12 = (bf16[272,128]{1,0:T(8,128)(2,1)S(1)}, bf16[272,128]{1,0:T(8,128)(2,1)S(1)}, u32[]{:S(2)}, u32[]{:S(2)}) collective-permute-start(bf16[272,128]{1,0:T(8,128)(2,1)S(1)} %fusion.3), channel_id=1, source_target_pairs={{0,2},{1,3},{2,0},{3,1},{4,6},{5,7},{6,4},{7,5},{8,10},{9,11},{10,... | collective-permute-start | bytes 208904 | tf_op jit(solution)/shard_map/ppermute | solution.py:286
  55.9 8.3 %collective-permute-start.13 = (bf16[272,128]{1,0:T(8,128)(2,1)S(1)}, bf16[272,128]{1,0:T(8,128)(2,1)S(1)}, u32[]{:S(2)}, u32[]{:S(2)}) collective-permute-start(bf16[272,128]{1,0:T(8,128)(2,1)S(1)} %add_convert_fusion), channel_id=1, source_target_pairs={{0,1},{1,0},{2,3},{3,2},{4,5},{5,4},{6,7},{7,6},{8,9},{9,8},{10,11... | collective-permute-start | bytes 208904 | tf_op jit(solution)/shard_map/ppermute | solution.py:286
  56.3 8.1 %collective-permute-start.4 = (bf16[2,16,16,128]{3,2,1,0:T(8,128)(2,1)S(1)}, bf16[2,16,16,128]{3,2,1,0:T(8,128)(2,1)S(1)}, u32[]{:S(2)}, u32[]{:S(2)}) collective-permute-start(bf16[2,16,16,128]{3,2,1,0:T(8,128)(2,1)S(1)} %copy-done.10), channel_id=1, source_target_pairs={{0,4},{4,0},{8,12},{12,8},{1,5},{5,1},{9,13},{13,9},{2,6},{6,2},{1... | collective-permute-start | bytes 393224 | tf_op jit(solution)/shard_map/ppermute | solution.py:275
  56.3 8.1 %collective-permute-start.5 = (bf16[2,16,16,128]{3,2,1,0:T(8,128)(2,1)S(1)}, bf16[2,16,16,128]{3,2,1,0:T(8,128)(2,1)S(1)}, u32[]{:S(2)}, u32[]{:S(2)}) collective-permute-start(bf16[2,16,16,128]{3,2,1,0:T(8,128)(2,1)S(1)} %copy-done.9), channel_id=1, source_target_pairs={{4,8},{8,4},{5,9},{9,5},{6,10},{10,6},{7,11},{11,7},{20,24},{24,20... | collective-permute-start | bytes 393224 | tf_op jit(solution)/shard_map/ppermute | solution.py:275
  59.6 5.0 %collective-permute-start.6 = (bf16[2,16,16,128]{3,2,1,0:T(8,128)(2,1)S(1)}, bf16[2,16,16,128]{3,2,1,0:T(8,128)(2,1)S(1)}, u32[]{:S(2)}, u32[]{:S(2)}) collective-permute-start(bf16[2,16,16,128]{3,2,1,0:T(8,128)(2,1)S(1)} %copy-done.8), channel_id=1, source_target_pairs={{0,1},{1,0},{2,3},{3,2},{4,5},{5,4},{6,7},{7,6},{8,9},{9,8},{10,11... | collective-permute-start | bytes 393224 | tf_op jit(solution)/shard_map/ppermute | solution.py:275
  61.4 6.8 %collective-permute-start.7 = (bf16[2,16,16,128]{3,2,1,0:T(8,128)(2,1)S(1)}, bf16[2,16,16,128]{3,2,1,0:T(8,128)(2,1)S(1)}, u32[]{:S(2)}, u32[]{:S(2)}) collective-permute-start(bf16[2,16,16,128]{3,2,1,0:T(8,128)(2,1)S(1)} %copy-done.7), channel_id=1, source_target_pairs={{1,2},{2,1},{5,6},{6,5},{9,10},{10,9},{13,14},{14,13},{17,18},{18,... | collective-permute-start | bytes 393224 | tf_op jit(solution)/shard_map/ppermute | solution.py:275
  64.3 14.1 %copy-start = (bf16[544,128]{1,0:T(8,128)(2,1)}, bf16[544,128]{1,0:T(8,128)(2,1)S(1)}, u32[]{:S(2)}) copy-start(bf16[544,128]{1,0:T(8,128)(2,1)S(1)} %maximum_select_fusion.own) | copy-start | bytes 417796
  64.3 14.1 %collective-permute-start.14 = (bf16[544,128]{1,0:T(8,128)(2,1)S(1)}, bf16[544,128]{1,0:T(8,128)(2,1)S(1)}, u32[]{:S(2)}, u32[]{:S(2)}) collective-permute-start(bf16[544,128]{1,0:T(8,128)(2,1)S(1)} %maximum_select_fusion.own), channel_id=1, source_target_pairs={{0,16},{16,0},{1,17},{17,1},{2,18},{18,2},{3,19},{19,3},{4,20},{20... | collective-permute-start | bytes 417800 | tf_op jit(solution)/shard_map/ppermute | solution.py:286
  64.3 3.9 %copy-start.3 = (bf16[2,16,16,128]{3,2,1,0:T(8,128)(2,1)}, bf16[2,16,16,128]{3,2,1,0:T(8,128)(2,1)S(1)}, u32[]{:S(2)}) copy-start(bf16[2,16,16,128]{3,2,1,0:T(8,128)(2,1)S(1)} %collective-permute-done.4.x0f) | copy-start | bytes 393220
  64.4 3.9 %copy-start.4 = (bf16[2,16,16,128]{3,2,1,0:T(8,128)(2,1)}, bf16[2,16,16,128]{3,2,1,0:T(8,128)(2,1)S(1)}, u32[]{:S(2)}) copy-start(bf16[2,16,16,128]{3,2,1,0:T(8,128)(2,1)S(1)} %collective-permute-done.5.x1f) | copy-start | bytes 393220
  64.7 3.6 %copy-start.5 = (bf16[2,16,16,128]{3,2,1,0:T(8,128)(2,1)}, bf16[2,16,16,128]{3,2,1,0:T(8,128)(2,1)S(1)}, u32[]{:S(2)}) copy-start(bf16[2,16,16,128]{3,2,1,0:T(8,128)(2,1)S(1)} %collective-permute-done.6.y0f) | copy-start | bytes 393220
  68.3 0.6 copy-start.6
  78.4 0.7 copy-start.2

commit v3 on v2

--- a/solution.py
+++ b/solution.py
@@ -12,14 +12,15 @@
 F32 = jnp.float32
 PLANES = 8
 PIECE = 16
-GRANT = 60 * 1024 * 1024
+STEP = 8
+GRANT = 44 << 20
 
 
 def halo_copies(meta, slots, faces, vol, sems, first, planes, edge):
     found = []
     for s in range(slots):
         for f in range(4):
-            link = meta[4 + s * 6 + f]
+            link = meta[s * 6 + f]
             axis, upper = f // 2, f % 2
             if axis == 0 and first + (planes if upper else 0) != (edge if upper else 0):
                 continue
@@ -34,7 +35,7 @@
                 pltpu.make_async_copy(arrived[ph], vol.at[index], sems.at[s * 4 + f])
                 for ph in range(2)
             ]
-            phase = (meta[1 + axis] + upper + 1) % 2
+            phase = (lax.axis_index(("mx", "my")[axis]) + upper + 1) % 2
             found.append((link < slots, phase, copies, index))
     return found
 
@@ -69,7 +70,7 @@
     rows = planes * edge * edge
 
     def beyond(face, part):
-        link = meta[4 + s * 6 + face]
+        link = meta[s * 6 + face]
         other = vol[jnp.minimum(link, slots - 1), pl.ds(x0 + 1, planes), 1 : 1 + edge]
         other = other.astype(F32).reshape(planes * edge, edge, channels)[:, part]
         return jnp.where(link < slots, other, 0.0)
@@ -120,7 +121,7 @@
         copy.wait()
 
 
-def finish_kernel(meta, own, other, conv_o, bias_o, head_o):
+def finish_kernel(own, other, conv_o, bias_o, head_o):
     half = own.shape[0]
     edges = (conv_o.shape[0], conv_o.shape[0] + head_o.shape[0])
 
@@ -136,13 +137,13 @@
         if 0 <= edges[1] - lo < half:
             bias_o[...] = value[edges[1] - lo : edges[1] - lo + 1]
 
-    first = meta[3] == 0
+    first = lax.axis_index("region") == 0
     place(0, jnp.where(first, own[...], other[...]).astype(F32))
     place(1, jnp.where(first, other[...], own[...]).astype(F32))
 
 
 def forward_kernel(
-    meta, feat, x0f, x1f, y0f, y1f, w, bias, hw, gout, ghead,
+    total, meta, feat, x0f, x1f, y0f, y1f, w, bias, hw, gout, ghead,
     res_o, head_o, gpre_o, gx0_o, gx1_o, gy0_o, gy1_o, colg_o, pay_o,
     vol, zbuf, colsum, acc, turned, zlow, zhigh, sems,
 ):
@@ -150,7 +151,7 @@
     s, xi = pl.program_id(0), pl.program_id(1)
     planes = res_o.shape[1]
     steps = edge // planes
-    count = meta[0]
+    count = total[0]
     scale = 1.0 / (edge * count).astype(F32)
     taps = w.shape[0] // channels
 
@@ -202,11 +203,11 @@
     gpre_o[0] = gtile
     for upper, step, layer in ((0, 0, 0), (1, steps - 1, planes - 1)):
         for phase, out in ((0, gx0_o), (1, gx1_o)):
-            @pl.when((xi == step) & ((meta[1] == phase) == bool(upper)))
+            @pl.when((xi == step) & ((lax.axis_index("mx") % 2 == phase) == bool(upper)))
             def _(out=out, layer=layer):
                 out[s] = gtile[layer]
 
-    even = meta[2] == 0
+    even = lax.axis_index("my") % 2 == 0
     low, high = gtile[:, 0], gtile[:, edge - 1]
     gy0_o[s, pl.ds(x0, planes)] = jnp.where(even, high, low)
     gy1_o[s, pl.ds(x0, planes)] = jnp.where(even, low, high)
@@ -233,24 +234,24 @@
         )
 
 
-def backward_kernel(first, meta, grad, x0f, x1f, y0f, y1f, wt, gout, colg, *rest):
+def backward_kernel(first, total, meta, grad, x0f, x1f, y0f, y1f, wt, gout, colg, *rest):
     out_o, vol, zbuf, sems = rest[-4:]
     slots, edge, channels = grad.shape[0], grad.shape[1], grad.shape[4]
-    planes = gout.shape[1]
-    s = pl.program_id(0)
-
-    @pl.when(s == 0)
+    planes, held = gout.shape[1], vol.shape[1] - 2
+    s, xi = pl.program_id(0), pl.program_id(1)
+
+    @pl.when((s == 0) & (xi == 0))
     def _():
-        below, above = min(first, 1), min(edge - first - planes, 1)
+        below, above = min(first, 1), min(edge - first - held, 1)
         body = [
             pltpu.make_async_copy(
-                grad.at[i, first - below : first + planes + above],
-                vol.at[i, 1 - below : 1 + planes + above, 1 : edge + 1],
+                grad.at[i, first - below : first + held + above],
+                vol.at[i, 1 - below : 1 + held + above, 1 : edge + 1],
                 sems.at[slots * 4 + i],
             )
             for i in range(slots)
         ]
-        found = halo_copies(meta, slots, (x0f, x1f, y0f, y1f), vol, sems, first, planes, edge)
+        found = halo_copies(meta, slots, (x0f, x1f, y0f, y1f), vol, sems, first, held, edge)
         for copy in body:
             copy.start()
         start_halos(found, vol)
@@ -260,12 +261,17 @@
 
     rows = planes * edge * edge
     cols = planes * edge
-    stacked = windows(meta, vol, zbuf, s, 0, planes, -1)
+    stacked = windows(meta, vol, zbuf, s, xi * planes, planes, -1)
     conv = jnp.dot(stacked, wt[...], preferred_element_type=F32)
-    spread = colg[first * edge : first * edge + cols].reshape(cols, 1, channels)
+    column = pl.ds(pl.multiple_of(first * edge + xi * cols, cols), cols)
+    spread = colg[column].reshape(cols, 1, channels)
     grad_result = gout[0].astype(F32).reshape(cols, edge, channels) + spread
-    total = jnp.where(s < meta[0], grad_result.reshape(rows, channels) + conv, 0.0).astype(BF)
+    total = jnp.where(s < total[0], grad_result.reshape(rows, channels) + conv, 0.0).astype(BF)
     out_o[0] = total.reshape(planes, edge, edge, channels)
+
+
+def in_hbm(x):
+    return pltpu.with_memory_space_constraint(x, pltpu.HBM)
 
 
 def swap(x, axis, odd):
@@ -302,25 +308,16 @@
     return x + partner(x.astype(BF), axis, bit).astype(F32)
 
 
-def doubled(x, axis, bit):
-    other = partner(x, axis, bit)
-    return jnp.where(
-        own_bit(axis, bit) == 0, jnp.concatenate([x, other]), jnp.concatenate([other, x])
-    )
-
-
 def bits(axis):
     return range((lax.axis_size(axis) - 1).bit_length())
 
 
 def all_summed(x):
     x = halved(x, "region", 0)
-    x = halved(x, "my", 0)
-    rest = [(axis, b) for axis in ("mx", "my") for b in bits(axis)]
-    rest.remove(("my", 0))
-    for axis, bit in sorted(rest, key=lambda stage: stage[1]):
+    later = [(axis, b) for axis in ("mx", "my") for b in bits(axis) if b]
+    for axis, bit in [("my", 0), ("mx", 0)] + sorted(later, key=lambda stage: stage[1]):
         x = summed(x, axis, bit)
-    x = doubled(x.astype(BF), "my", 0)
+    x = x.astype(BF)
     return x, partner(x, "region", 0)
 
 
@@ -332,15 +329,7 @@
     head_grad = grad_head.reshape(grad_head.shape[3:])
     slots, edge, channels = blocks.shape[0], blocks.shape[1], blocks.shape[4]
     taps = conv_weight.shape[0]
-    meta = jnp.concatenate(
-        [
-            block_count.reshape(1),
-            (lax.axis_index("mx") % 2).astype(jnp.int32).reshape(1),
-            (lax.axis_index("my") % 2).astype(jnp.int32).reshape(1),
-            lax.axis_index("region").astype(jnp.int32).reshape(1),
-            neighbours.reshape(-1),
-        ]
-    )
+    meta = (block_count.reshape(1), neighbours.reshape(-1))
     anywhere = pl.BlockSpec(memory_space=pl.ANY)
     hbm = pl.BlockSpec(memory_space=pltpu.HBM)
     vmem = pl.BlockSpec(memory_space=pltpu.VMEM)
@@ -351,16 +340,17 @@
         out_specs=[vmem] * 4,
         scratch_shapes=[pltpu.SemaphoreType.DMA((4,))],
         out_shape=[face] * 4,
+        compiler_params=pltpu.CompilerParams(vmem_limit_bytes=8 << 20),
         name="pick",
-    )(blocks)
+    )(in_hbm(blocks))
     faces = swap_faces(sent[:2], "mx") + swap_faces(sent[2:], "my")
 
-    whole = lambda *shape: pl.BlockSpec(shape, lambda i, j, m: (0,) * len(shape))
-    tile = pl.BlockSpec((1, PLANES, edge, edge, channels), lambda i, j, m: (i, j, 0, 0, 0))
+    whole = lambda *shape: pl.BlockSpec(shape, lambda i, j, m, n: (0,) * len(shape))
+    tile = pl.BlockSpec((1, PLANES, edge, edge, channels), lambda i, j, m, n: (i, j, 0, 0, 0))
     volume = (slots, edge, edge, edge, channels)
     padded = pltpu.VMEM((slots, edge + 2, edge + 2, edge, channels), BF)
     columns = edge * edge
-    pay_rows = ((taps + 1) * channels // 64 + 1) * 64
+    pay_rows = ((taps + 1) * channels // 32 + 1) * 32
     flops = 2 * slots * edge**3 * taps * channels * channels
     moved = slots * edge**3 * channels * 2
     params = pltpu.CompilerParams(
@@ -369,7 +359,7 @@
     result, head_tile, gpre, gx0, gx1, gy0, gy1, colg, pay = pl.pallas_call(
         forward_kernel,
         grid_spec=pltpu.PrefetchScalarGridSpec(
-            num_scalar_prefetch=1,
+            num_scalar_prefetch=2,
             grid=(slots, edge // PLANES),
             in_specs=[
                 hbm, anywhere, anywhere, anywhere, anywhere,
@@ -392,9 +382,9 @@
             ],
         ),
         out_shape=[
-            jax.ShapeDtypeStruct(volume, BF),
+            pltpu.HBM(volume, BF),
             jax.ShapeDtypeStruct((columns, channels), BF),
-            jax.ShapeDtypeStruct(volume, BF),
+            pltpu.HBM(volume, BF),
             *[face] * 4,
             jax.ShapeDtypeStruct((columns, channels), F32),
             jax.ShapeDtypeStruct((pay_rows, channels), F32),
@@ -405,8 +395,8 @@
         ),
         name="forward",
     )(
-        meta, blocks, *faces, conv_weight.reshape(taps * channels, channels),
-        conv_bias.reshape(1, channels), head_weight, upstream, head_grad,
+        *meta, in_hbm(blocks), *faces, in_hbm(conv_weight.reshape(taps * channels, channels)),
+        conv_bias.reshape(1, channels), in_hbm(head_weight), in_hbm(upstream), in_hbm(head_grad),
     )
 
     grad_faces = swap_faces((gx0, gx1), "mx") + swap_faces((gy0, gy1), "my")
@@ -414,9 +404,12 @@
     grad_local = None
     pieces = edge // PIECE
     for k in range(pieces):
-        part = pl.BlockSpec((1, PIECE, edge, edge, channels), lambda i, m, k=k: (i, k, 0, 0, 0))
-        all_of = lambda *shape: pl.BlockSpec(shape, lambda i, m: (0,) * len(shape))
-        operands = [meta, gpre, *grad_faces, turned, upstream, colg]
+        part = pl.BlockSpec(
+            (1, STEP, edge, edge, channels),
+            lambda i, j, m, n, k=k: (i, k * (PIECE // STEP) + j, 0, 0, 0),
+        )
+        all_of = lambda *shape: pl.BlockSpec(shape, lambda i, j, m, n: (0,) * len(shape))
+        operands = [*meta, in_hbm(gpre), *grad_faces, turned, in_hbm(upstream), colg]
         specs = [hbm] + [anywhere] * 4
         specs += [all_of(taps * channels, channels), part, all_of(columns, channels)]
         if grad_local is not None:
@@ -425,20 +418,20 @@
         grad_local = pl.pallas_call(
             functools.partial(backward_kernel, k * PIECE),
             grid_spec=pltpu.PrefetchScalarGridSpec(
-                num_scalar_prefetch=1,
-                grid=(slots,),
+                num_scalar_prefetch=2,
+                grid=(slots, PIECE // STEP),
                 in_specs=specs,
                 out_specs=part,
                 scratch_shapes=[
                     pltpu.VMEM((slots, PIECE + 2, edge + 2, edge, channels), BF),
-                    pltpu.VMEM((PIECE * edge, edge + 16, channels), F32),
+                    pltpu.VMEM((STEP * edge, edge + 16, channels), F32),
                     pltpu.SemaphoreType.DMA((slots * 5,)),
                 ],
             ),
             out_shape=jax.ShapeDtypeStruct(volume, BF),
             input_output_aliases={len(operands) - 1: 0} if k else {},
             compiler_params=pltpu.CompilerParams(
-                dimension_semantics=("arbitrary",), vmem_limit_bytes=GRANT
+                dimension_semantics=("arbitrary", "arbitrary"), vmem_limit_bytes=GRANT
             ),
             cost_estimate=pl.CostEstimate(
                 flops=flops // pieces, bytes_accessed=4 * moved // pieces, transcendentals=0
@@ -449,16 +442,16 @@
     conv_rows = taps * channels
     grad_conv, grad_bias, grad_head_weight = pl.pallas_call(
         finish_kernel,
-        grid_spec=pltpu.PrefetchScalarGridSpec(
-            num_scalar_prefetch=1, grid=(), in_specs=[vmem] * 2, out_specs=[vmem] * 3
-        ),
+        in_specs=[vmem] * 2,
+        out_specs=[vmem] * 3,
         out_shape=[
             jax.ShapeDtypeStruct((conv_rows, channels), F32),
             jax.ShapeDtypeStruct((1, channels), F32),
             jax.ShapeDtypeStruct((channels, channels), F32),
         ],
+        compiler_params=pltpu.CompilerParams(vmem_limit_bytes=8 << 20),
         name="finish",
-    )(meta, own, other)
+    )(own, other)
     return (
         result.reshape(features_in.shape),
         head_tile.reshape(grad_head.shape),

time: 81.9 us -> 72.8 us (0.89)
  the two profiles are of different devices: /device:TPU:18 before, /device:TPU:12 now
where the time goes in v3:
time: 72.8 us; the launch traced here: 72.5 us
  Pallas kernels  27.1 us (37%)
  waiting for transfers between devices  22.9 us (31%)
  starting transfers between devices  20.3 us (28%)
  between operations  1.47 us (2%)
    ppermute x8, starting transfers between devices, swap(): return lax.ppermute(x, axis, pairs)  17.1 us
    pallas_call x1, Pallas kernels, body(): pl.pallas_call(forward_kernel, grid_spec=pltpu.PrefetchScalarGridSpec(num...  16.3 us
    ppermute x6, waiting for transfers between devices, partner(): lax.ppermute(x, axis, [(i, i ^ 1 << bit) for i in range(lax.axis_size(axi...  16 us
    pallas_call x1, Pallas kernels, body(): pl.pallas_call(functools.partial(backward_kernel, k * PIECE), grid_spec=p...  8.83 us
    ppermute x8, waiting for transfers between devices, swap(): return lax.ppermute(x, axis, pairs)  6.96 us
    ppermute x6, starting transfers between devices, partner(): lax.ppermute(x, axis, [(i, i ^ 1 << bit) for i in range(lax.axis_size(axi...  3.2 us
  transfers between devices with their start and end apart: 14, of which 8 were waited for; matrix products, arithmetic and copies ran while one was open for 0% of the time, Pallas kernels for 12%

profile of v3, /device:TPU:12, one launch (start us, length us, event | category | flops | bytes accessed | tf_op | source)
XLA Modules:
  0.0 72.5 jit_solution(2368733856372205656)
XLA Ops:
  0.6 0.0 copy-start.2
  0.6 0.0 copy-start
  0.7 1.1 %pick.1 = (bf16[2,16,16,128]{3,2,1,0:T(8,128)(2,1)S(1)}, bf16[2,16,16,128]{3,2,1,0:T(8,128)(2,1)S(1)}, bf16[2,16,16,128]{3,2,1,0:T(8,128)(2,1)S(1)}, bf16[2,16,16,128]{3,2,1,0:T(8,128)(2,1)S(1)}) custom-call(bf16[2,16,16,16,128]{4,3,2,1,0:T(8,128)(2,1)} %bitcast.33), custom_call_target="tpu_custom_call" | custom-call | tf_op jit(solution)/shard_map/pick/pallas_call | solution.py:337
  1.8 1.6 %collective-permute-start = (bf16[2,16,16,128]{3,2,1,0:T(8,128)(2,1)S(1)}, bf16[2,16,16,128]{3,2,1,0:T(8,128)(2,1)S(1)}, u32[]{:S(2)}, u32[]{:S(2)}) collective-permute-start(bf16[2,16,16,128]{3,2,1,0:T(8,128)(2,1)S(1)} %get-tuple-element.22), channel_id=1, source_target_pairs={{0,4},{4,0},{8,12},{12,8},{1,5},{5,1},{9,13},{13,9},{2,6},{6,2},{1... | collective-permute-start | bytes 393224 | tf_op jit(solution)/shard_map/ppermute | solution.py:281
  3.4 2.4 %collective-permute-start.1 = (bf16[2,16,16,128]{3,2,1,0:T(8,128)(2,1)S(1)}, bf16[2,16,16,128]{3,2,1,0:T(8,128)(2,1)S(1)}, u32[]{:S(2)}, u32[]{:S(2)}) collective-permute-start(bf16[2,16,16,128]{3,2,1,0:T(8,128)(2,1)S(1)} %get-tuple-element.23), channel_id=1, source_target_pairs={{4,8},{8,4},{5,9},{9,5},{6,10},{10,6},{7,11},{11,7},{20,24},{24,20... | collective-permute-start | bytes 393224 | tf_op jit(solution)/shard_map/ppermute | solution.py:281
  5.7 0.1 collective-permute-start.2
  5.8 5.0 %collective-permute-start.3 = (bf16[2,16,16,128]{3,2,1,0:T(8,128)(2,1)S(1)}, bf16[2,16,16,128]{3,2,1,0:T(8,128)(2,1)S(1)}, u32[]{:S(2)}, u32[]{:S(2)}) collective-permute-start(bf16[2,16,16,128]{3,2,1,0:T(8,128)(2,1)S(1)} %get-tuple-element.25), channel_id=1, source_target_pairs={{1,2},{2,1},{5,6},{6,5},{9,10},{10,9},{13,14},{14,13},{17,18},{18,... | collective-permute-start | bytes 393224 | tf_op jit(solution)/shard_map/ppermute | solution.py:281
  11.5 0.0 copy-done.2
  11.5 0.1 reshape.56.meta
  11.6 0.0 collective-permute-done.x0f
  11.6 0.0 collective-permute-done.1.x1f
  11.6 0.0 collective-permute-done.2.y0f
  11.6 2.2 %collective-permute-done.3.y1f = bf16[2,16,16,128]{3,2,1,0:T(8,128)(2,1)S(1)} collective-permute-done((bf16[2,16,16,128]{3,2,1,0:T(8,128)(2,1)S(1)}, bf16[2,16,16,128]{3,2,1,0:T(8,128)(2,1)S(1)}, u32[]{:S(2)}, u32[]{:S(2)}) %collective-permute-start.3) | collective-permute-done | bytes 131104 | tf_op jit(solution)/shard_map/ppermute | solution.py:281
  13.8 0.0 copy-done
  13.8 16.3 %forward.1 = (bf16[2,16,16,16,128]{4,3,2,1,0:T(8,128)(2,1)}, bf16[256,128]{1,0:T(8,128)(2,1)}, bf16[2,16,16,16,128]{4,3,2,1,0:T(8,128)(2,1)}, bf16[2,16,16,128]{...) custom-call(s32[1]{0:T(128)} %bitcast.25.total, ...), custom_call_target="tpu_custom_call" | custom-call | flops 3758096384 | bytes 10485760 | tf_op jit(solution)/shard_map/forward/pallas_call | solution.py:359
  30.1 0.0 copy-start.1
  30.2 0.1 collective-permute-start.8
  30.2 1.3 %collective-permute-done.8 = bf16[528,128]{1,0:T(8,128)(2,1)S(1)} collective-permute-done((bf16[528,128]{1,0:T(8,128)(2,1)S(1)}, bf16[528,128]{1,0:T(8,128)(2,1)S(1)}, u32[]{:S(2)}, u32[]{:S(2)}) %collective-permute-start.8) | collective-permute-done | bytes 135200 | tf_op jit(solution)/shard_map/ppermute | solution.py:292
  31.6 0.1 collective-permute-start.9
  31.7 5.6 %collective-permute-done.9 = bf16[528,128]{1,0:T(8,128)(2,1)S(1)} collective-permute-done((bf16[528,128]{1,0:T(8,128)(2,1)S(1)}, bf16[528,128]{1,0:T(8,128)(2,1)S(1)}, u32[]{:S(2)}, u32[]{:S(2)}) %collective-permute-start.9) | collective-permute-done | bytes 135200 | tf_op jit(solution)/shard_map/ppermute | solution.py:292
  37.3 0.1 fusion
  37.4 0.1 collective-permute-start.10
  37.5 5.0 %collective-permute-done.10 = bf16[528,128]{1,0:T(8,128)(2,1)S(1)} collective-permute-done((bf16[528,128]{1,0:T(8,128)(2,1)S(1)}, bf16[528,128]{1,0:T(8,128)(2,1)S(1)}, u32[]{:S(2)}, u32[]{:S(2)}) %collective-permute-start.10) | collective-permute-done | bytes 135200 | tf_op jit(solution)/shard_map/ppermute | solution.py:292
  42.5 0.1 fusion.4
  42.5 1.1 %collective-permute-start.11 = (bf16[528,128]{1,0:T(8,128)(2,1)S(1)}, bf16[528,128]{1,0:T(8,128)(2,1)S(1)}, u32[]{:S(2)}, u32[]{:S(2)}) collective-permute-start(bf16[528,128]{1,0:T(8,128)(2,1)S(1)} %get-tuple-element.38), channel_id=1, source_target_pairs={{0,8},{4,12},{8,0},{12,4},{1,9},{5,13},{9,1},{13,5},{2,10},{6,14},... | collective-permute-start | bytes 405512 | tf_op jit(solution)/shard_map/ppermute | solution.py:292
  43.6 4.0 %collective-permute-done.11 = bf16[528,128]{1,0:T(8,128)(2,1)S(1)} collective-permute-done((bf16[528,128]{1,0:T(8,128)(2,1)S(1)}, bf16[528,128]{1,0:T(8,128)(2,1)S(1)}, u32[]{:S(2)}, u32[]{:S(2)}) %collective-permute-start.11) | collective-permute-done | bytes 135200 | tf_op jit(solution)/shard_map/ppermute | solution.py:292
  47.7 1.9 %collective-permute-start.12 = (bf16[528,128]{1,0:T(8,128)(2,1)S(1)}, bf16[528,128]{1,0:T(8,128)(2,1)S(1)}, u32[]{:S(2)}, u32[]{:S(2)}) collective-permute-start(bf16[528,128]{1,0:T(8,128)(2,1)S(1)} %fusion.1), channel_id=1, source_target_pairs={{0,2},{1,3},{2,0},{3,1},{4,6},{5,7},{6,4},{7,5},{8,10},{9,11},{10,... | collective-permute-start | bytes 405512 | tf_op jit(solution)/shard_map/ppermute | solution.py:292
  49.5 0.0 copy-done.1
  49.5 0.2 copy.14
  49.7 1.0 %collective-permute-start.4 = (bf16[2,16,16,128]{3,2,1,0:T(8,128)(2,1)S(1)}, bf16[2,16,16,128]{3,2,1,0:T(8,128)(2,1)S(1)}, u32[]{:S(2)}, u32[]{:S(2)}) collective-permute-start(bf16[2,16,16,128]{3,2,1,0:T(8,128)(2,1)S(1)} %get-tuple-element.29), channel_id=1, source_target_pairs={{0,4},{4,0},{8,12},{12,8},{1,5},{5,1},{9,13},{13,9},{2,6},{6,2},{1... | collective-permute-start | bytes 393224 | tf_op jit(solution)/shard_map/ppermute | solution.py:281
  50.7 3.6 %collective-permute-start.5 = (bf16[2,16,16,128]{3,2,1,0:T(8,128)(2,1)S(1)}, bf16[2,16,16,128]{3,2,1,0:T(8,128)(2,1)S(1)}, u32[]{:S(2)}, u32[]{:S(2)}) collective-permute-start(bf16[2,16,16,128]{3,2,1,0:T(8,128)(2,1)S(1)} %get-tuple-element.30), channel_id=1, source_target_pairs={{4,8},{8,4},{5,9},{9,5},{6,10},{10,6},{7,11},{11,7},{20,24},{24,20... | collective-permute-start | bytes 393224 | tf_op jit(solution)/shard_map/ppermute | solution.py:281
  54.4 1.5 %collective-permute-start.6 = (bf16[2,16,16,128]{3,2,1,0:T(8,128)(2,1)S(1)}, bf16[2,16,16,128]{3,2,1,0:T(8,128)(2,1)S(1)}, u32[]{:S(2)}, u32[]{:S(2)}) collective-permute-start(bf16[2,16,16,128]{3,2,1,0:T(8,128)(2,1)S(1)} %get-tuple-element.31), channel_id=1, source_target_pairs={{0,1},{1,0},{2,3},{3,2},{4,5},{5,4},{6,7},{7,6},{8,9},{9,8},{10,11... | collective-permute-start | bytes 393224 | tf_op jit(solution)/shard_map/ppermute | solution.py:281
  55.9 1.9 %collective-permute-start.7 = (bf16[2,16,16,128]{3,2,1,0:T(8,128)(2,1)S(1)}, bf16[2,16,16,128]{3,2,1,0:T(8,128)(2,1)S(1)}, u32[]{:S(2)}, u32[]{:S(2)}) collective-permute-start(bf16[2,16,16,128]{3,2,1,0:T(8,128)(2,1)S(1)} %get-tuple-element.32), channel_id=1, source_target_pairs={{1,2},{2,1},{5,6},{6,5},{9,10},{10,9},{13,14},{14,13},{17,18},{18,... | collective-permute-start | bytes 393224 | tf_op jit(solution)/shard_map/ppermute | solution.py:281
  57.8 0.0 collective-permute-done.12
  57.8 0.1 add_convert_fusion.own
  57.9 0.1 collective-permute-start.13
  58.0 0.0 collective-permute-done.4.x0f
  58.0 0.5 collective-permute-done.5.x1f
  58.5 0.9 %collective-permute-done.6.y0f = bf16[2,16,16,128]{3,2,1,0:T(8,128)(2,1)S(1)} collective-permute-done((bf16[2,16,16,128]{3,2,1,0:T(8,128)(2,1)S(1)}, bf16[2,16,16,128]{3,2,1,0:T(8,128)(2,1)S(1)}, u32[]{:S(2)}, u32[]{:S(2)}) %collective-permute-start.6) | collective-permute-done | bytes 131104 | tf_op jit(solution)/shard_map/ppermute | solution.py:281
  59.4 3.3 %collective-permute-done.7.y1f = bf16[2,16,16,128]{3,2,1,0:T(8,128)(2,1)S(1)} collective-permute-done((bf16[2,16,16,128]{3,2,1,0:T(8,128)(2,1)S(1)}, bf16[2,16,16,128]{3,2,1,0:T(8,128)(2,1)S(1)}, u32[]{:S(2)}, u32[]{:S(2)}) %collective-permute-start.7) | collective-permute-done | bytes 131104 | tf_op jit(solution)/shard_map/ppermute | solution.py:281
  62.7 8.8 %shard_map.127 = bf16[2,16,16,16,128]{4,3,2,1,0:T(8,128)(2,1)} custom-call(s32[1]{0:T(128)} %bitcast.26.total, s32[12]{0:T(128)S(1)} %reshape.56.meta, bf16[2,16,16,16,128]{4,3,2,1,0:T(8,128)(2,1)} %get-tuple-element.28.grad, bf16[2,16,16,128]{3,2,1,0:T(8,128)(2,1)S(1)} %collective-permute-done.4.x0f, ...), custom_call_target="tpu_custom_call" | custom-call | flops 1879048192 | bytes 8388608 | tf_op jit(solution)/shard_map/pallas_call | solution.py:418
  71.6 0.0 collective-permute-done.13.other
  71.6 0.8 %finish.1 = (f32[896,128]{1,0:T(8,128)}, f32[1,128]{1,0:T(1,128)}, f32[128,128]{1,0:T(8,128)}) custom-call(bf16[528,128]{1,0:T(8,128)(2,1)S(1)} %add_convert_fusion.own, bf16[528,128]{1,0:T(8,128)(2,1)S(1)} %collective-permute-done.13.other), custom_call_target="tpu_custom_call" | custom-call | tf_op jit(solution)/shard_map/finish/pallas_call | solution.py:443
  (3 shorter events, 0.1 us)
Async XLA Ops:
  0.6 10.9 %copy-start.2 = (s32[1,1,1,2,6]{4,3,2,1,0:T(2,128)S(1)}, s32[1,1,1,2,6]{4,3,2,1,0:T(2,128)}, u32[]{:S(2)}) copy-start(s32[1,1,1,2,6]{4,3,2,1,0:T(2,128)} %param.15) | copy-start | bytes 148
  0.6 13.2 %copy-start = (f32[128]{0:T(128)S(1)}, f32[128]{0:T(128)}, u32[]{:S(2)}) copy-start(f32[128]{0:T(128)} %param.10) | copy-start | bytes 1540
  1.8 9.8 %collective-permute-start = (bf16[2,16,16,128]{3,2,1,0:T(8,128)(2,1)S(1)}, bf16[2,16,16,128]{3,2,1,0:T(8,128)(2,1)S(1)}, u32[]{:S(2)}, u32[]{:S(2)}) collective-permute-start(bf16[2,16,16,128]{3,2,1,0:T(8,128)(2,1)S(1)} %get-tuple-element.22), channel_id=1, source_target_pairs={{0,4},{4,0},{8,12},{12,8},{1,5},{5,1},{9,13},{13,9},{2,6},{6,2},{1... | collective-permute-start | bytes 393224 | tf_op jit(solution)/shard_map/ppermute | solution.py:281
  3.4 8.3 %collective-permute-start.1 = (bf16[2,16,16,128]{3,2,1,0:T(8,128)(2,1)S(1)}, bf16[2,16,16,128]{3,2,1,0:T(8,128)(2,1)S(1)}, u32[]{:S(2)}, u32[]{:S(2)}) collective-permute-start(bf16[2,16,16,128]{3,2,1,0:T(8,128)(2,1)S(1)} %get-tuple-element.23), channel_id=1, source_target_pairs={{4,8},{8,4},{5,9},{9,5},{6,10},{10,6},{7,11},{11,7},{20,24},{24,20... | collective-permute-start | bytes 393224 | tf_op jit(solution)/shard_map/ppermute | solution.py:281
  5.7 5.9 %collective-permute-start.2 = (bf16[2,16,16,128]{3,2,1,0:T(8,128)(2,1)S(1)}, bf16[2,16,16,128]{3,2,1,0:T(8,128)(2,1)S(1)}, u32[]{:S(2)}, u32[]{:S(2)}) collective-permute-start(bf16[2,16,16,128]{3,2,1,0:T(8,128)(2,1)S(1)} %get-tuple-element.24), channel_id=1, source_target_pairs={{0,1},{1,0},{2,3},{3,2},{4,5},{5,4},{6,7},{7,6},{8,9},{9,8},{10,11... | collective-permute-start | bytes 393224 | tf_op jit(solution)/shard_map/ppermute | solution.py:281
  5.8 8.0 %collective-permute-start.3 = (bf16[2,16,16,128]{3,2,1,0:T(8,128)(2,1)S(1)}, bf16[2,16,16,128]{3,2,1,0:T(8,128)(2,1)S(1)}, u32[]{:S(2)}, u32[]{:S(2)}) collective-permute-start(bf16[2,16,16,128]{3,2,1,0:T(8,128)(2,1)S(1)} %get-tuple-element.25), channel_id=1, source_target_pairs={{1,2},{2,1},{5,6},{6,5},{9,10},{10,9},{13,14},{14,13},{17,18},{18,... | collective-permute-start | bytes 393224 | tf_op jit(solution)/shard_map/ppermute | solution.py:281
  30.1 19.4 %copy-start.1 = (bf16[7,128,128]{2,1,0:T(8,128)(2,1)S(1)}, bf16[7,128,128]{2,1,0:T(8,128)(2,1)}, u32[]{:S(2)}) copy-start(bf16[7,128,128]{2,1,0:T(8,128)(2,1)} %param.9) | copy-start | bytes 688132
  30.2 1.4 %collective-permute-start.8 = (bf16[528,128]{1,0:T(8,128)(2,1)S(1)}, bf16[528,128]{1,0:T(8,128)(2,1)S(1)}, u32[]{:S(2)}, u32[]{:S(2)}) collective-permute-start(bf16[528,128]{1,0:T(8,128)(2,1)S(1)} %fusion.2), channel_id=1, source_target_pairs={{0,16},{16,0},{1,17},{17,1},{2,18},{18,2},{3,19},{19,3},{4,20},{20... | collective-permute-start | bytes 405512 | tf_op jit(solution)/shard_map/ppermute | solution.py:292
  31.6 5.7 %collective-permute-start.9 = (bf16[528,128]{1,0:T(8,128)(2,1)S(1)}, bf16[528,128]{1,0:T(8,128)(2,1)S(1)}, u32[]{:S(2)}, u32[]{:S(2)}) collective-permute-start(bf16[528,128]{1,0:T(8,128)(2,1)S(1)} %fusion.3), channel_id=1, source_target_pairs={{0,1},{1,0},{2,3},{3,2},{4,5},{5,4},{6,7},{7,6},{8,9},{9,8},{10,11... | collective-permute-start | bytes 405512 | tf_op jit(solution)/shard_map/ppermute | solution.py:292
  37.4 5.1 %collective-permute-start.10 = (bf16[528,128]{1,0:T(8,128)(2,1)S(1)}, bf16[528,128]{1,0:T(8,128)(2,1)S(1)}, u32[]{:S(2)}, u32[]{:S(2)}) collective-permute-start(bf16[528,128]{1,0:T(8,128)(2,1)S(1)} %fusion), channel_id=1, source_target_pairs={{0,4},{4,0},{8,12},{12,8},{1,5},{5,1},{9,13},{13,9},{2,6},{6,2},{1... | collective-permute-start | bytes 405512 | tf_op jit(solution)/shard_map/ppermute | solution.py:292
  42.5 5.1 %collective-permute-start.11 = (bf16[528,128]{1,0:T(8,128)(2,1)S(1)}, bf16[528,128]{1,0:T(8,128)(2,1)S(1)}, u32[]{:S(2)}, u32[]{:S(2)}) collective-permute-start(bf16[528,128]{1,0:T(8,128)(2,1)S(1)} %get-tuple-element.38), channel_id=1, source_target_pairs={{0,8},{4,12},{8,0},{12,4},{1,9},{5,13},{9,1},{13,5},{2,10},{6,14},... | collective-permute-start | bytes 405512 | tf_op jit(solution)/shard_map/ppermute | solution.py:292
  47.7 10.2 %collective-permute-start.12 = (bf16[528,128]{1,0:T(8,128)(2,1)S(1)}, bf16[528,128]{1,0:T(8,128)(2,1)S(1)}, u32[]{:S(2)}, u32[]{:S(2)}) collective-permute-start(bf16[528,128]{1,0:T(8,128)(2,1)S(1)} %fusion.1), channel_id=1, source_target_pairs={{0,2},{1,3},{2,0},{3,1},{4,6},{5,7},{6,4},{7,5},{8,10},{9,11},{10,... | collective-permute-start | bytes 405512 | tf_op jit(solution)/shard_map/ppermute | solution.py:292
  49.7 8.3 %collective-permute-start.4 = (bf16[2,16,16,128]{3,2,1,0:T(8,128)(2,1)S(1)}, bf16[2,16,16,128]{3,2,1,0:T(8,128)(2,1)S(1)}, u32[]{:S(2)}, u32[]{:S(2)}) collective-permute-start(bf16[2,16,16,128]{3,2,1,0:T(8,128)(2,1)S(1)} %get-tuple-element.29), channel_id=1, source_target_pairs={{0,4},{4,0},{8,12},{12,8},{1,5},{5,1},{9,13},{13,9},{2,6},{6,2},{1... | collective-permute-start | bytes 393224 | tf_op jit(solution)/shard_map/ppermute | solution.py:281
  50.7 7.7 %collective-permute-start.5 = (bf16[2,16,16,128]{3,2,1,0:T(8,128)(2,1)S(1)}, bf16[2,16,16,128]{3,2,1,0:T(8,128)(2,1)S(1)}, u32[]{:S(2)}, u32[]{:S(2)}) collective-permute-start(bf16[2,16,16,128]{3,2,1,0:T(8,128)(2,1)S(1)} %get-tuple-element.30), channel_id=1, source_target_pairs={{4,8},{8,4},{5,9},{9,5},{6,10},{10,6},{7,11},{11,7},{20,24},{24,20... | collective-permute-start | bytes 393224 | tf_op jit(solution)/shard_map/ppermute | solution.py:281
  54.4 5.0 %collective-permute-start.6 = (bf16[2,16,16,128]{3,2,1,0:T(8,128)(2,1)S(1)}, bf16[2,16,16,128]{3,2,1,0:T(8,128)(2,1)S(1)}, u32[]{:S(2)}, u32[]{:S(2)}) collective-permute-start(bf16[2,16,16,128]{3,2,1,0:T(8,128)(2,1)S(1)} %get-tuple-element.31), channel_id=1, source_target_pairs={{0,1},{1,0},{2,3},{3,2},{4,5},{5,4},{6,7},{7,6},{8,9},{9,8},{10,11... | collective-permute-start | bytes 393224 | tf_op jit(solution)/shard_map/ppermute | solution.py:281
  55.9 6.8 %collective-permute-start.7 = (bf16[2,16,16,128]{3,2,1,0:T(8,128)(2,1)S(1)}, bf16[2,16,16,128]{3,2,1,0:T(8,128)(2,1)S(1)}, u32[]{:S(2)}, u32[]{:S(2)}) collective-permute-start(bf16[2,16,16,128]{3,2,1,0:T(8,128)(2,1)S(1)} %get-tuple-element.32), channel_id=1, source_target_pairs={{1,2},{2,1},{5,6},{6,5},{9,10},{10,9},{13,14},{14,13},{17,18},{18,... | collective-permute-start | bytes 393224 | tf_op jit(solution)/shard_map/ppermute | solution.py:281
  57.9 13.7 %collective-permute-start.13 = (bf16[528,128]{1,0:T(8,128)(2,1)S(1)}, bf16[528,128]{1,0:T(8,128)(2,1)S(1)}, u32[]{:S(2)}, u32[]{:S(2)}) collective-permute-start(bf16[528,128]{1,0:T(8,128)(2,1)S(1)} %add_convert_fusion.own), channel_id=1, source_target_pairs={{0,16},{16,0},{1,17},{17,1},{2,18},{18,2},{3,19},{19,3},{4,20},{20... | collective-permute-start | bytes 405512 | tf_op jit(solution)/shard_map/ppermute | solution.py:292

commit v4 on v3

--- a/solution.py
+++ b/solution.py
@@ -16,7 +16,7 @@
 GRANT = 44 << 20
 
 
-def halo_copies(meta, slots, faces, vol, sems, first, planes, edge):
+def halo_copies(meta, slots, faces, vol, sems, first, planes, edge, paired):
     found = []
     for s in range(slots):
         for f in range(4):
@@ -27,24 +27,32 @@
             source = jnp.minimum(link, slots - 1)
             if axis == 0:
                 index = (s, planes + 1 if upper else 0, slice(1, edge + 1))
-                arrived = [faces[ph].at[source] for ph in range(2)]
+                part = ()
             else:
                 index = (s, slice(1, planes + 1), edge + 1 if upper else 0)
-                arrived = [faces[2 + ph].at[source, first : first + planes] for ph in range(2)]
+                part = (slice(first, first + planes),)
+            valid = link < slots
+            if paired:
+                phase = (lax.axis_index(("mx", "my")[axis]) + upper + 1) % 2
+                wanted = [(valid & (phase == ph), faces[2 * axis + ph]) for ph in range(2)]
+            else:
+                wanted = [(valid, faces[f])]
             copies = [
-                pltpu.make_async_copy(arrived[ph], vol.at[index], sems.at[s * 4 + f])
-                for ph in range(2)
+                (
+                    condition,
+                    pltpu.make_async_copy(face.at[(source,) + part], vol.at[index], sems.at[s * 4 + f]),
+                )
+                for condition, face in wanted
             ]
-            phase = (lax.axis_index(("mx", "my")[axis]) + upper + 1) % 2
-            found.append((link < slots, phase, copies, index))
+            found.append((valid, copies, index))
     return found
 
 
 def start_halos(found, vol):
-    for valid, phase, copies, index in found:
-        for ph in range(2):
-            @pl.when(valid & (phase == ph))
-            def _(copy=copies[ph]):
+    for valid, copies, index in found:
+        for wanted, copy in copies:
+            @pl.when(wanted)
+            def _(copy=copy):
                 copy.start()
 
         @pl.when(jnp.logical_not(valid))
@@ -53,9 +61,9 @@
 
 
 def wait_halos(found):
-    for valid, _, copies, _ in found:
+    for valid, copies, _ in found:
         @pl.when(valid)
-        def _(copy=copies[0]):
+        def _(copy=copies[0][1]):
             copy.wait()
 
 
@@ -111,8 +119,7 @@
     edge = feat.shape[1]
     copies = []
     for i, out in enumerate((x0, x1, y0, y1)):
-        upward = lax.axis_index(("mx", "my")[i // 2]) % 2 == i % 2
-        layer = jnp.where(upward, edge - 1, 0)
+        layer = 0 if i % 2 else edge - 1
         face = feat.at[:, layer] if i < 2 else feat.at[:, :, layer]
         copies.append(pltpu.make_async_copy(face, out, sems.at[i]))
     for copy in copies:
@@ -155,15 +162,23 @@
     scale = 1.0 / (edge * count).astype(F32)
     taps = w.shape[0] // channels
 
-    @pl.when((s == 0) & (xi == 0))
-    def _():
-        body = [
+    cut = min(planes + 1, edge)
+    parts = [
+        [
             pltpu.make_async_copy(
-                feat.at[i], vol.at[i, 1 : edge + 1, 1 : edge + 1], sems.at[slots * 4 + i]
+                feat.at[i, lo:hi],
+                vol.at[i, 1 + lo : 1 + hi, 1 : edge + 1],
+                sems.at[slots * (4 + h) + i],
             )
             for i in range(slots)
         ]
-        found = halo_copies(meta, slots, (x0f, x1f, y0f, y1f), vol, sems, 0, edge, edge)
+        for h, (lo, hi) in enumerate(((0, cut), (cut, edge)))
+    ]
+
+    @pl.when((s == 0) & (xi == 0))
+    def _():
+        body = parts[0] + parts[1]
+        found = halo_copies(meta, slots, (x0f, x1f, y0f, y1f), vol, sems, 0, edge, edge, False)
         for copy in body:
             copy.start()
         start_halos(found, vol)
@@ -177,15 +192,20 @@
         for ref in (acc, turned, zlow, zhigh):
             ref[...] = jnp.zeros_like(ref)
         colsum[...] = jnp.zeros_like(colsum)
-        for copy in body:
+        for copy in parts[0]:
             copy.wait()
         wait_halos(found)
+
+    @pl.when((s == 0) & (xi == 1))
+    def _():
+        for copy in parts[1]:
+            copy.wait()
 
     x0 = xi * planes
     rows = planes * edge * edge
     cols = planes * edge
     before_s = jnp.maximum(jnp.where(xi == 0, s - 1, s), 0)
-    before_x0 = jnp.where(xi == 0, edge - planes, x0 - planes)
+    before_x0 = jnp.where(xi == 0, jnp.where(s == 0, 0, edge - planes), x0 - planes)
     add_weight_terms(acc, turned, vol, zlow, zhigh, before_s, before_x0, planes)
     stacked = windows(meta, vol, zbuf, s, x0, planes, 1)
     preact = jnp.dot(stacked, w[...], preferred_element_type=F32) + bias[...]
@@ -240,24 +260,35 @@
     planes, held = gout.shape[1], vol.shape[1] - 2
     s, xi = pl.program_id(0), pl.program_id(1)
 
-    @pl.when((s == 0) & (xi == 0))
-    def _():
-        below, above = min(first, 1), min(edge - first - held, 1)
-        body = [
+    below, above = min(first, 1), min(edge - first - held, 1)
+    cut = min(planes + 1, held)
+    parts = [
+        [
             pltpu.make_async_copy(
-                grad.at[i, first - below : first + held + above],
-                vol.at[i, 1 - below : 1 + held + above, 1 : edge + 1],
-                sems.at[slots * 4 + i],
+                grad.at[i, first + lo : first + hi],
+                vol.at[i, 1 + lo : 1 + hi, 1 : edge + 1],
+                sems.at[slots * (4 + h) + i],
             )
             for i in range(slots)
         ]
-        found = halo_copies(meta, slots, (x0f, x1f, y0f, y1f), vol, sems, first, held, edge)
+        for h, (lo, hi) in enumerate(((-below, cut), (cut, held + above)))
+    ]
+
+    @pl.when((s == 0) & (xi == 0))
+    def _():
+        body = parts[0] + parts[1]
+        found = halo_copies(meta, slots, (x0f, x1f, y0f, y1f), vol, sems, first, held, edge, True)
         for copy in body:
             copy.start()
         start_halos(found, vol)
-        for copy in body:
+        for copy in parts[0]:
             copy.wait()
         wait_halos(found)
+
+    @pl.when((s == 0) & (xi == 1))
+    def _():
+        for copy in parts[1]:
+            copy.wait()
 
     rows = planes * edge * edge
     cols = planes * edge
@@ -285,6 +316,18 @@
     arrived = []
     for odd in range(2):
         arrived.append(swap(sent[odd], axis, odd))
+    return arrived
+
+
+def turn(x, axis, by):
+    count = lax.axis_size(axis)
+    return lax.ppermute(x, axis, [(i, (i + by) % count) for i in range(count)])
+
+
+def turn_faces(sent, axis):
+    arrived = []
+    for i, by in enumerate((1, -1)):
+        arrived.append(turn(sent[i], axis, by))
     return arrived
 
 
@@ -343,7 +386,7 @@
         compiler_params=pltpu.CompilerParams(vmem_limit_bytes=8 << 20),
         name="pick",
     )(in_hbm(blocks))
-    faces = swap_faces(sent[:2], "mx") + swap_faces(sent[2:], "my")
+    faces = turn_faces(sent[:2], "mx") + turn_faces(sent[2:], "my")
 
     whole = lambda *shape: pl.BlockSpec(shape, lambda i, j, m, n: (0,) * len(shape))
     tile = pl.BlockSpec((1, PLANES, edge, edge, channels), lambda i, j, m, n: (i, j, 0, 0, 0))
@@ -378,7 +421,7 @@
                 pltpu.VMEM((channels, PLANES * columns), BF),
                 pltpu.VMEM((PLANES * columns, channels), BF),
                 pltpu.VMEM((PLANES * columns, channels), BF),
-                pltpu.SemaphoreType.DMA((slots * 5,)),
+                pltpu.SemaphoreType.DMA((slots * 6,)),
             ],
         ),
         out_shape=[
@@ -425,7 +468,7 @@
                 scratch_shapes=[
                     pltpu.VMEM((slots, PIECE + 2, edge + 2, edge, channels), BF),
                     pltpu.VMEM((STEP * edge, edge + 16, channels), F32),
-                    pltpu.SemaphoreType.DMA((slots * 5,)),
+                    pltpu.SemaphoreType.DMA((slots * 6,)),
                 ],
             ),
             out_shape=jax.ShapeDtypeStruct(volume, BF),

time: 72.8 us -> 70.1 us (0.963)
  the two profiles are of different devices: /device:TPU:12 before, /device:TPU:10 now
where the time goes in v4:
time: 70.1 us; the launch traced here: 69.8 us
  Pallas kernels  26.5 us (38%)
  waiting for transfers between devices  22.4 us (32%)
  starting transfers between devices  18.8 us (27%)
  between operations  1.43 us (2%)
    pallas_call x1, Pallas kernels, body(): pl.pallas_call(forward_kernel, grid_spec=pltpu.PrefetchScalarGridSpec(num...  16 us
    ppermute x6, waiting for transfers between devices, partner(): lax.ppermute(x, axis, [(i, i ^ 1 << bit) for i in range(lax.axis_size(axi...  13.1 us
    pallas_call x1, Pallas kernels, body(): pl.pallas_call(functools.partial(backward_kernel, k * PIECE), grid_spec=p...  8.55 us
    ppermute x4, starting transfers between devices, swap(): return lax.ppermute(x, axis, pairs)  8.37 us
    ppermute x6, starting transfers between devices, partner(): lax.ppermute(x, axis, [(i, i ^ 1 << bit) for i in range(lax.axis_size(axi...  6.35 us
    ppermute x4, waiting for transfers between devices, turn(): return lax.ppermute(x, axis, [(i, (i + by) % count) for i in range(count)])  5.56 us
    ppermute x4, starting transfers between devices, turn(): return lax.ppermute(x, axis, [(i, (i + by) % count) for i in range(count)])  4.1 us
    ppermute x4, waiting for transfers between devices, swap(): return lax.ppermute(x, axis, pairs)  3.77 us
  transfers between devices with their start and end apart: 14, of which 10 were waited for; matrix products, arithmetic and copies ran while one was open for 0% of the time, Pallas kernels for 12%

profile of v4, /device:TPU:10, one launch (start us, length us, event | category | flops | bytes accessed | tf_op | source)
XLA Modules:
  0.0 69.8 jit_solution(18170083937787275098)
XLA Ops:
  0.6 0.0 copy-start.2
  0.6 0.0 copy-start
  0.7 1.1 %pick.1 = (bf16[2,16,16,128]{3,2,1,0:T(8,128)(2,1)S(1)}, bf16[2,16,16,128]{3,2,1,0:T(8,128)(2,1)S(1)}, bf16[2,16,16,128]{3,2,1,0:T(8,128)(2,1)S(1)}, bf16[2,16,16,128]{3,2,1,0:T(8,128)(2,1)S(1)}) custom-call(bf16[2,16,16,16,128]{4,3,2,1,0:T(8,128)(2,1)} %bitcast.33), custom_call_target="tpu_custom_call" | custom-call | tf_op jit(solution)/shard_map/pick/pallas_call | solution.py:380
  1.8 1.5 %collective-permute-start = (bf16[2,16,16,128]{3,2,1,0:T(8,128)(2,1)S(1)}, bf16[2,16,16,128]{3,2,1,0:T(8,128)(2,1)S(1)}, u32[]{:S(2)}, u32[]{:S(2)}) collective-permute-start(bf16[2,16,16,128]{3,2,1,0:T(8,128)(2,1)S(1)} %get-tuple-element.22), channel_id=1, source_target_pairs={{0,4},{4,8},{8,12},{12,0},{1,5},{5,9},{9,13},{13,1},{2,6},{6,10},{... | collective-permute-start | bytes 393224 | tf_op jit(solution)/shard_map/ppermute | solution.py:324
  3.3 0.5 collective-permute-start.1
  3.9 1.6 %collective-permute-start.2 = (bf16[2,16,16,128]{3,2,1,0:T(8,128)(2,1)S(1)}, bf16[2,16,16,128]{3,2,1,0:T(8,128)(2,1)S(1)}, u32[]{:S(2)}, u32[]{:S(2)}) collective-permute-start(bf16[2,16,16,128]{3,2,1,0:T(8,128)(2,1)S(1)} %get-tuple-element.24), channel_id=1, source_target_pairs={{0,1},{1,2},{2,3},{3,0},{4,5},{5,6},{6,7},{7,4},{8,9},{9,10},{10,1... | collective-permute-start | bytes 393224 | tf_op jit(solution)/shard_map/ppermute | solution.py:324
  5.5 0.4 collective-permute-start.3
  6.6 0.0 copy-done.2
  6.6 0.1 reshape.56.meta
  6.7 1.6 %collective-permute-done.x0f = bf16[2,16,16,128]{3,2,1,0:T(8,128)(2,1)S(1)} collective-permute-done((bf16[2,16,16,128]{3,2,1,0:T(8,128)(2,1)S(1)}, bf16[2,16,16,128]{3,2,1,0:T(8,128)(2,1)S(1)}, u32[]{:S(2)}, u32[]{:S(2)}) %collective-permute-start) | collective-permute-done | bytes 131104 | tf_op jit(solution)/shard_map/ppermute | solution.py:324
  8.2 2.6 %collective-permute-done.1.x1f = bf16[2,16,16,128]{3,2,1,0:T(8,128)(2,1)S(1)} collective-permute-done((bf16[2,16,16,128]{3,2,1,0:T(8,128)(2,1)S(1)}, bf16[2,16,16,128]{3,2,1,0:T(8,128)(2,1)S(1)}, u32[]{:S(2)}, u32[]{:S(2)}) %collective-permute-start.1) | collective-permute-done | bytes 131104 | tf_op jit(solution)/shard_map/ppermute | solution.py:324
  10.9 0.0 collective-permute-done.2.y0f
  10.9 1.4 %collective-permute-done.3.y1f = bf16[2,16,16,128]{3,2,1,0:T(8,128)(2,1)S(1)} collective-permute-done((bf16[2,16,16,128]{3,2,1,0:T(8,128)(2,1)S(1)}, bf16[2,16,16,128]{3,2,1,0:T(8,128)(2,1)S(1)}, u32[]{:S(2)}, u32[]{:S(2)}) %collective-permute-start.3) | collective-permute-done | bytes 131104 | tf_op jit(solution)/shard_map/ppermute | solution.py:324
  12.2 0.0 copy-done
  12.2 16.0 %forward.1 = (bf16[2,16,16,16,128]{4,3,2,1,0:T(8,128)(2,1)}, bf16[256,128]{1,0:T(8,128)(2,1)}, bf16[2,16,16,16,128]{4,3,2,1,0:T(8,128)(2,1)}, bf16[2,16,16,128]{...) custom-call(s32[1]{0:T(128)} %bitcast.25.total, ...), custom_call_target="tpu_custom_call" | custom-call | flops 3758096384 | bytes 10485760 | tf_op jit(solution)/shard_map/forward/pallas_call | solution.py:402
  28.2 0.0 copy-start.1
  28.2 0.1 collective-permute-start.8
  28.3 1.3 %collective-permute-done.8 = bf16[528,128]{1,0:T(8,128)(2,1)S(1)} collective-permute-done((bf16[528,128]{1,0:T(8,128)(2,1)S(1)}, bf16[528,128]{1,0:T(8,128)(2,1)S(1)}, u32[]{:S(2)}, u32[]{:S(2)}) %collective-permute-start.8) | collective-permute-done | bytes 135200 | tf_op jit(solution)/shard_map/ppermute | solution.py:335
  29.7 1.0 %collective-permute-start.9 = (bf16[528,128]{1,0:T(8,128)(2,1)S(1)}, bf16[528,128]{1,0:T(8,128)(2,1)S(1)}, u32[]{:S(2)}, u32[]{:S(2)}) collective-permute-start(bf16[528,128]{1,0:T(8,128)(2,1)S(1)} %fusion.3), channel_id=1, source_target_pairs={{0,1},{1,0},{2,3},{3,2},{4,5},{5,4},{6,7},{7,6},{8,9},{9,8},{10,11... | collective-permute-start | bytes 405512 | tf_op jit(solution)/shard_map/ppermute | solution.py:335
  30.7 4.7 %collective-permute-done.9 = bf16[528,128]{1,0:T(8,128)(2,1)S(1)} collective-permute-done((bf16[528,128]{1,0:T(8,128)(2,1)S(1)}, bf16[528,128]{1,0:T(8,128)(2,1)S(1)}, u32[]{:S(2)}, u32[]{:S(2)}) %collective-permute-start.9) | collective-permute-done | bytes 135200 | tf_op jit(solution)/shard_map/ppermute | solution.py:335
  35.4 0.1 fusion
  35.5 1.5 %collective-permute-start.10 = (bf16[528,128]{1,0:T(8,128)(2,1)S(1)}, bf16[528,128]{1,0:T(8,128)(2,1)S(1)}, u32[]{:S(2)}, u32[]{:S(2)}) collective-permute-start(bf16[528,128]{1,0:T(8,128)(2,1)S(1)} %fusion), channel_id=1, source_target_pairs={{0,4},{4,0},{8,12},{12,8},{1,5},{5,1},{9,13},{13,9},{2,6},{6,2},{1... | collective-permute-start | bytes 405512 | tf_op jit(solution)/shard_map/ppermute | solution.py:335
  37.0 3.6 %collective-permute-done.10 = bf16[528,128]{1,0:T(8,128)(2,1)S(1)} collective-permute-done((bf16[528,128]{1,0:T(8,128)(2,1)S(1)}, bf16[528,128]{1,0:T(8,128)(2,1)S(1)}, u32[]{:S(2)}, u32[]{:S(2)}) %collective-permute-start.10) | collective-permute-done | bytes 135200 | tf_op jit(solution)/shard_map/ppermute | solution.py:335
  40.5 0.1 fusion.4
  40.6 1.6 %collective-permute-start.11 = (bf16[528,128]{1,0:T(8,128)(2,1)S(1)}, bf16[528,128]{1,0:T(8,128)(2,1)S(1)}, u32[]{:S(2)}, u32[]{:S(2)}) collective-permute-start(bf16[528,128]{1,0:T(8,128)(2,1)S(1)} %get-tuple-element.38), channel_id=1, source_target_pairs={{0,8},{4,12},{8,0},{12,4},{1,9},{5,13},{9,1},{13,5},{2,10},{6,14},... | collective-permute-start | bytes 405512 | tf_op jit(solution)/shard_map/ppermute | solution.py:335
  42.2 3.5 %collective-permute-done.11 = bf16[528,128]{1,0:T(8,128)(2,1)S(1)} collective-permute-done((bf16[528,128]{1,0:T(8,128)(2,1)S(1)}, bf16[528,128]{1,0:T(8,128)(2,1)S(1)}, u32[]{:S(2)}, u32[]{:S(2)}) %collective-permute-start.11) | collective-permute-done | bytes 135200 | tf_op jit(solution)/shard_map/ppermute | solution.py:335
  45.7 2.1 %collective-permute-start.12 = (bf16[528,128]{1,0:T(8,128)(2,1)S(1)}, bf16[528,128]{1,0:T(8,128)(2,1)S(1)}, u32[]{:S(2)}, u32[]{:S(2)}) collective-permute-start(bf16[528,128]{1,0:T(8,128)(2,1)S(1)} %fusion.1), channel_id=1, source_target_pairs={{0,2},{1,3},{2,0},{3,1},{4,6},{5,7},{6,4},{7,5},{8,10},{9,11},{10,... | collective-permute-start | bytes 405512 | tf_op jit(solution)/shard_map/ppermute | solution.py:335
  47.8 0.0 copy-done.1
  47.8 0.2 copy.14
  48.0 1.5 %collective-permute-start.4 = (bf16[2,16,16,128]{3,2,1,0:T(8,128)(2,1)S(1)}, bf16[2,16,16,128]{3,2,1,0:T(8,128)(2,1)S(1)}, u32[]{:S(2)}, u32[]{:S(2)}) collective-permute-start(bf16[2,16,16,128]{3,2,1,0:T(8,128)(2,1)S(1)} %get-tuple-element.29), channel_id=1, source_target_pairs={{0,4},{4,0},{8,12},{12,8},{1,5},{5,1},{9,13},{13,9},{2,6},{6,2},{1... | collective-permute-start | bytes 393224 | tf_op jit(solution)/shard_map/ppermute | solution.py:312
  49.5 3.4 %collective-permute-start.5 = (bf16[2,16,16,128]{3,2,1,0:T(8,128)(2,1)S(1)}, bf16[2,16,16,128]{3,2,1,0:T(8,128)(2,1)S(1)}, u32[]{:S(2)}, u32[]{:S(2)}) collective-permute-start(bf16[2,16,16,128]{3,2,1,0:T(8,128)(2,1)S(1)} %get-tuple-element.30), channel_id=1, source_target_pairs={{4,8},{8,4},{5,9},{9,5},{6,10},{10,6},{7,11},{11,7},{20,24},{24,20... | collective-permute-start | bytes 393224 | tf_op jit(solution)/shard_map/ppermute | solution.py:312
  53.0 0.5 collective-permute-start.6
  53.5 2.9 %collective-permute-start.7 = (bf16[2,16,16,128]{3,2,1,0:T(8,128)(2,1)S(1)}, bf16[2,16,16,128]{3,2,1,0:T(8,128)(2,1)S(1)}, u32[]{:S(2)}, u32[]{:S(2)}) collective-permute-start(bf16[2,16,16,128]{3,2,1,0:T(8,128)(2,1)S(1)} %get-tuple-element.32), channel_id=1, source_target_pairs={{1,2},{2,1},{5,6},{6,5},{9,10},{10,9},{13,14},{14,13},{17,18},{18,... | collective-permute-start | bytes 393224 | tf_op jit(solution)/shard_map/ppermute | solution.py:312
  56.4 0.0 collective-permute-done.12
  56.4 0.1 add_convert_fusion.own
  56.5 0.1 collective-permute-start.13
  56.6 0.0 collective-permute-done.4.x0f
  56.6 0.7 %collective-permute-done.5.x1f = bf16[2,16,16,128]{3,2,1,0:T(8,128)(2,1)S(1)} collective-permute-done((bf16[2,16,16,128]{3,2,1,0:T(8,128)(2,1)S(1)}, bf16[2,16,16,128]{3,2,1,0:T(8,128)(2,1)S(1)}, u32[]{:S(2)}, u32[]{:S(2)}) %collective-permute-start.5) | collective-permute-done | bytes 131104 | tf_op jit(solution)/shard_map/ppermute | solution.py:312
  57.3 0.7 %collective-permute-done.6.y0f = bf16[2,16,16,128]{3,2,1,0:T(8,128)(2,1)S(1)} collective-permute-done((bf16[2,16,16,128]{3,2,1,0:T(8,128)(2,1)S(1)}, bf16[2,16,16,128]{3,2,1,0:T(8,128)(2,1)S(1)}, u32[]{:S(2)}, u32[]{:S(2)}) %collective-permute-start.6) | collective-permute-done | bytes 131104 | tf_op jit(solution)/shard_map/ppermute | solution.py:312
  58.0 2.3 %collective-permute-done.7.y1f = bf16[2,16,16,128]{3,2,1,0:T(8,128)(2,1)S(1)} collective-permute-done((bf16[2,16,16,128]{3,2,1,0:T(8,128)(2,1)S(1)}, bf16[2,16,16,128]{3,2,1,0:T(8,128)(2,1)S(1)}, u32[]{:S(2)}, u32[]{:S(2)}) %collective-permute-start.7) | collective-permute-done | bytes 131104 | tf_op jit(solution)/shard_map/ppermute | solution.py:312
  60.3 8.5 %shard_map.127 = bf16[2,16,16,16,128]{4,3,2,1,0:T(8,128)(2,1)} custom-call(s32[1]{0:T(128)} %bitcast.26.total, s32[12]{0:T(128)S(1)} %reshape.56.meta, bf16[2,16,16,16,128]{4,3,2,1,0:T(8,128)(2,1)} %get-tuple-element.28.grad, bf16[2,16,16,128]{3,2,1,0:T(8,128)(2,1)S(1)} %collective-permute-done.4.x0f, ...), custom_call_target="tpu_custom_call" | custom-call | flops 1879048192 | bytes 8388608 | tf_op jit(solution)/shard_map/pallas_call | solution.py:461
  68.9 0.0 collective-permute-done.13.other
  68.9 0.8 %finish.1 = (f32[896,128]{1,0:T(8,128)}, f32[1,128]{1,0:T(1,128)}, f32[128,128]{1,0:T(8,128)}) custom-call(bf16[528,128]{1,0:T(8,128)(2,1)S(1)} %add_convert_fusion.own, bf16[528,128]{1,0:T(8,128)(2,1)S(1)} %collective-permute-done.13.other), custom_call_target="tpu_custom_call" | custom-call | tf_op jit(solution)/shard_map/finish/pallas_call | solution.py:486
  (3 shorter events, 0.1 us)
Async XLA Ops:
  0.6 5.9 %copy-start.2 = (s32[1,1,1,2,6]{4,3,2,1,0:T(2,128)S(1)}, s32[1,1,1,2,6]{4,3,2,1,0:T(2,128)}, u32[]{:S(2)}) copy-start(s32[1,1,1,2,6]{4,3,2,1,0:T(2,128)} %param.15) | copy-start | bytes 148
  0.6 11.6 %copy-start = (f32[128]{0:T(128)S(1)}, f32[128]{0:T(128)}, u32[]{:S(2)}) copy-start(f32[128]{0:T(128)} %param.10) | copy-start | bytes 1540
  1.8 6.4 %collective-permute-start = (bf16[2,16,16,128]{3,2,1,0:T(8,128)(2,1)S(1)}, bf16[2,16,16,128]{3,2,1,0:T(8,128)(2,1)S(1)}, u32[]{:S(2)}, u32[]{:S(2)}) collective-permute-start(bf16[2,16,16,128]{3,2,1,0:T(8,128)(2,1)S(1)} %get-tuple-element.22), channel_id=1, source_target_pairs={{0,4},{4,8},{8,12},{12,0},{1,5},{5,9},{9,13},{13,1},{2,6},{6,10},{... | collective-permute-start | bytes 393224 | tf_op jit(solution)/shard_map/ppermute | solution.py:324
  3.3 7.5 %collective-permute-start.1 = (bf16[2,16,16,128]{3,2,1,0:T(8,128)(2,1)S(1)}, bf16[2,16,16,128]{3,2,1,0:T(8,128)(2,1)S(1)}, u32[]{:S(2)}, u32[]{:S(2)}) collective-permute-start(bf16[2,16,16,128]{3,2,1,0:T(8,128)(2,1)S(1)} %get-tuple-element.23), channel_id=1, source_target_pairs={{0,12},{4,0},{8,4},{12,8},{1,13},{5,1},{9,5},{13,9},{2,14},{6,2},{... | collective-permute-start | bytes 393224 | tf_op jit(solution)/shard_map/ppermute | solution.py:324
  3.9 7.0 %collective-permute-start.2 = (bf16[2,16,16,128]{3,2,1,0:T(8,128)(2,1)S(1)}, bf16[2,16,16,128]{3,2,1,0:T(8,128)(2,1)S(1)}, u32[]{:S(2)}, u32[]{:S(2)}) collective-permute-start(bf16[2,16,16,128]{3,2,1,0:T(8,128)(2,1)S(1)} %get-tuple-element.24), channel_id=1, source_target_pairs={{0,1},{1,2},{2,3},{3,0},{4,5},{5,6},{6,7},{7,4},{8,9},{9,10},{10,1... | collective-permute-start | bytes 393224 | tf_op jit(solution)/shard_map/ppermute | solution.py:324
  5.5 6.8 %collective-permute-start.3 = (bf16[2,16,16,128]{3,2,1,0:T(8,128)(2,1)S(1)}, bf16[2,16,16,128]{3,2,1,0:T(8,128)(2,1)S(1)}, u32[]{:S(2)}, u32[]{:S(2)}) collective-permute-start(bf16[2,16,16,128]{3,2,1,0:T(8,128)(2,1)S(1)} %get-tuple-element.25), channel_id=1, source_target_pairs={{0,3},{1,0},{2,1},{3,2},{4,7},{5,4},{6,5},{7,6},{8,11},{9,8},{10,9... | collective-permute-start | bytes 393224 | tf_op jit(solution)/shard_map/ppermute | solution.py:324
  28.2 19.6 %copy-start.1 = (bf16[7,128,128]{2,1,0:T(8,128)(2,1)S(1)}, bf16[7,128,128]{2,1,0:T(8,128)(2,1)}, u32[]{:S(2)}) copy-start(bf16[7,128,128]{2,1,0:T(8,128)(2,1)} %param.9) | copy-start | bytes 688132
  28.2 1.4 %collective-permute-start.8 = (bf16[528,128]{1,0:T(8,128)(2,1)S(1)}, bf16[528,128]{1,0:T(8,128)(2,1)S(1)}, u32[]{:S(2)}, u32[]{:S(2)}) collective-permute-start(bf16[528,128]{1,0:T(8,128)(2,1)S(1)} %fusion.2), channel_id=1, source_target_pairs={{0,16},{16,0},{1,17},{17,1},{2,18},{18,2},{3,19},{19,3},{4,20},{20... | collective-permute-start | bytes 405512 | tf_op jit(solution)/shard_map/ppermute | solution.py:335
  29.7 5.7 %collective-permute-start.9 = (bf16[528,128]{1,0:T(8,128)(2,1)S(1)}, bf16[528,128]{1,0:T(8,128)(2,1)S(1)}, u32[]{:S(2)}, u32[]{:S(2)}) collective-permute-start(bf16[528,128]{1,0:T(8,128)(2,1)S(1)} %fusion.3), channel_id=1, source_target_pairs={{0,1},{1,0},{2,3},{3,2},{4,5},{5,4},{6,7},{7,6},{8,9},{9,8},{10,11... | collective-permute-start | bytes 405512 | tf_op jit(solution)/shard_map/ppermute | solution.py:335
  35.5 5.1 %collective-permute-start.10 = (bf16[528,128]{1,0:T(8,128)(2,1)S(1)}, bf16[528,128]{1,0:T(8,128)(2,1)S(1)}, u32[]{:S(2)}, u32[]{:S(2)}) collective-permute-start(bf16[528,128]{1,0:T(8,128)(2,1)S(1)} %fusion), channel_id=1, source_target_pairs={{0,4},{4,0},{8,12},{12,8},{1,5},{5,1},{9,13},{13,9},{2,6},{6,2},{1... | collective-permute-start | bytes 405512 | tf_op jit(solution)/shard_map/ppermute | solution.py:335
  40.6 5.1 %collective-permute-start.11 = (bf16[528,128]{1,0:T(8,128)(2,1)S(1)}, bf16[528,128]{1,0:T(8,128)(2,1)S(1)}, u32[]{:S(2)}, u32[]{:S(2)}) collective-permute-start(bf16[528,128]{1,0:T(8,128)(2,1)S(1)} %get-tuple-element.38), channel_id=1, source_target_pairs={{0,8},{4,12},{8,0},{12,4},{1,9},{5,13},{9,1},{13,5},{2,10},{6,14},... | collective-permute-start | bytes 405512 | tf_op jit(solution)/shard_map/ppermute | solution.py:335
  45.7 10.7 %collective-permute-start.12 = (bf16[528,128]{1,0:T(8,128)(2,1)S(1)}, bf16[528,128]{1,0:T(8,128)(2,1)S(1)}, u32[]{:S(2)}, u32[]{:S(2)}) collective-permute-start(bf16[528,128]{1,0:T(8,128)(2,1)S(1)} %fusion.1), channel_id=1, source_target_pairs={{0,2},{1,3},{2,0},{3,1},{4,6},{5,7},{6,4},{7,5},{8,10},{9,11},{10,... | collective-permute-start | bytes 405512 | tf_op jit(solution)/shard_map/ppermute | solution.py:335
  48.0 8.5 %collective-permute-start.4 = (bf16[2,16,16,128]{3,2,1,0:T(8,128)(2,1)S(1)}, bf16[2,16,16,128]{3,2,1,0:T(8,128)(2,1)S(1)}, u32[]{:S(2)}, u32[]{:S(2)}) collective-permute-start(bf16[2,16,16,128]{3,2,1,0:T(8,128)(2,1)S(1)} %get-tuple-element.29), channel_id=1, source_target_pairs={{0,4},{4,0},{8,12},{12,8},{1,5},{5,1},{9,13},{13,9},{2,6},{6,2},{1... | collective-permute-start | bytes 393224 | tf_op jit(solution)/shard_map/ppermute | solution.py:312
  49.5 7.7 %collective-permute-start.5 = (bf16[2,16,16,128]{3,2,1,0:T(8,128)(2,1)S(1)}, bf16[2,16,16,128]{3,2,1,0:T(8,128)(2,1)S(1)}, u32[]{:S(2)}, u32[]{:S(2)}) collective-permute-start(bf16[2,16,16,128]{3,2,1,0:T(8,128)(2,1)S(1)} %get-tuple-element.30), channel_id=1, source_target_pairs={{4,8},{8,4},{5,9},{9,5},{6,10},{10,6},{7,11},{11,7},{20,24},{24,20... | collective-permute-start | bytes 393224 | tf_op jit(solution)/shard_map/ppermute | solution.py:312
  53.0 5.0 %collective-permute-start.6 = (bf16[2,16,16,128]{3,2,1,0:T(8,128)(2,1)S(1)}, bf16[2,16,16,128]{3,2,1,0:T(8,128)(2,1)S(1)}, u32[]{:S(2)}, u32[]{:S(2)}) collective-permute-start(bf16[2,16,16,128]{3,2,1,0:T(8,128)(2,1)S(1)} %get-tuple-element.31), channel_id=1, source_target_pairs={{0,1},{1,0},{2,3},{3,2},{4,5},{5,4},{6,7},{7,6},{8,9},{9,8},{10,11... | collective-permute-start | bytes 393224 | tf_op jit(solution)/shard_map/ppermute | solution.py:312
  53.5 6.8 %collective-permute-start.7 = (bf16[2,16,16,128]{3,2,1,0:T(8,128)(2,1)S(1)}, bf16[2,16,16,128]{3,2,1,0:T(8,128)(2,1)S(1)}, u32[]{:S(2)}, u32[]{:S(2)}) collective-permute-start(bf16[2,16,16,128]{3,2,1,0:T(8,128)(2,1)S(1)} %get-tuple-element.32), channel_id=1, source_target_pairs={{1,2},{2,1},{5,6},{6,5},{9,10},{10,9},{13,14},{14,13},{17,18},{18,... | collective-permute-start | bytes 393224 | tf_op jit(solution)/shard_map/ppermute | solution.py:312
  56.5 12.4 %collective-permute-start.13 = (bf16[528,128]{1,0:T(8,128)(2,1)S(1)}, bf16[528,128]{1,0:T(8,128)(2,1)S(1)}, u32[]{:S(2)}, u32[]{:S(2)}) collective-permute-start(bf16[528,128]{1,0:T(8,128)(2,1)S(1)} %add_convert_fusion.own), channel_id=1, source_target_pairs={{0,16},{16,0},{1,17},{17,1},{2,18},{18,2},{3,19},{19,3},{4,20},{20... | collective-permute-start | bytes 405512 | tf_op jit(solution)/shard_map/ppermute | solution.py:335
